TPU v7x, 256 devices: a whole 4x4x8 slice. The times are simulated.
256 devices in a mesh: space: 32 (over z_hi, y, core), probe: 8 (over x, z_lo).
Axes of the slice: x: 4, y: 4, z: 8 (z_hi: 4, z_lo: 2; z = z_hi * 2 + z_lo), core: 2. Of those that a mesh axis runs over, the one named last changes fastest.
Arguments:
- positions: bfloat16 [256, 3, 32], P('space'), may hold values from -4.3125 to 4.3125
- probes: bfloat16 [256, 512, 128], P('space', 'probe'), may hold values from -4 to 4
- neighbours: int32 [256, 15], P('space'), may hold values from -1 to 255, as said below
Outputs:
- density: bfloat16 [128, 256, 15, 128], P('probe', 'space')
- forces: float32 [256, 3, 32], P('space')
Inputs may be any that keep to these rules, and one draw needn't show every extreme that they name: `neighbours`: slot 0 of each cluster names the cluster itself. Clusters are held 8 to an index of space in order; every other entry is -1 or a cluster held by the same index of space or by the index one before or one after it, cyclically. The clusters named in one row are distinct.
All inputs are finite; a program needn't handle non-finite values.
Results may differ from a plain program's by a relative error of at most 0.0018.
The roundings to bfloat16 on the way count: a program that leaves them out, or rounds other values in their place, can miss the bound.
Values may be sent and summed in bfloat16 or wider, within the bound.
No kernel may reach another device: no remote copies, remote signals or barrier semaphores. Data moves between devices by JAX's collectives and lax.ppermute only.
A program may use at most 64 MiB of HBM per device.

v0:
```python
import jax
import jax.numpy as jnp
from jax import lax
from jax.sharding import PartitionSpec as P

SS_SIGMA = -1.938
SP_SIGMA = 1.745
PP_SIGMA = 3.05
PP_PI = -1.075
BOND_LENGTH = 2.35
SOFT_SQUARE = 0.25
CELL_EDGE = 10.86
COEFF_ZERO = 0.6
COEFF_ONE = -0.7
COEFF_TWO = 0.45


def padded(shard, sides, width):
    for axis, dim in sides:
        size, length = (lax.axis_size(axis), shard.shape[dim])
        up = [(i, (i + 1) % size) for i in range(size)]
        down = [(j, i) for i, j in up]
        last = lax.slice_in_dim(shard, length - width, length, axis=dim)
        initial = lax.slice_in_dim(shard, 0, width, axis=dim)
        before = lax.ppermute(last, axis, up)
        after = lax.ppermute(initial, axis, down)
        shard = jnp.concatenate([before, shard, after], axis=dim)
    return shard


def shifted(block, axis, distance):
    devices = range(lax.axis_size(axis))
    route = [((i - distance) % len(devices), i) for i in devices]
    return lax.ppermute(block, axis, route)


def offsets():
    half = CELL_EDGE / 2.0
    table = [[0.0, 0.0, 0.0]]
    for sign_x in (-1.0, 1.0):
        for sign_y in (-1.0, 1.0):
            for sign_z in (-1.0, 1.0):
                table.append([sign_x * half, sign_y * half, sign_z * half])
    for axis_pick in range(3):
        for sign_a in (1.0, -1.0):
            entry = [0.0, 0.0, 0.0]
            entry[axis_pick] = sign_a * CELL_EDGE
            table.append(entry)
    return jnp.array(table, dtype=jnp.float32)


def build_rows(own_pos, col_pos, start_row, row_count):
    atom_count = own_pos.shape[-1]
    row_index = start_row + jnp.arange(row_count, dtype=jnp.int32)
    orbital = row_index // atom_count
    atom_index = row_index % atom_count
    atom_pick = (jnp.arange(atom_count, dtype=jnp.int32)[:, None] == atom_index[None, :]).astype(
        jnp.float32
    )
    weights = (jnp.arange(4, dtype=jnp.int32)[:, None] == orbital[None, :]).astype(jnp.float32)
    row_pos = jnp.dot(own_pos, atom_pick, precision=lax.Precision.HIGHEST)
    offset_vec = col_pos[:, None, :] - row_pos[:, :, None]
    dist_square = jnp.sum(offset_vec * offset_vec, axis=0) + SOFT_SQUARE
    cosine = offset_vec / jnp.sqrt(dist_square)
    radial = jnp.exp(1.0 - dist_square / (BOND_LENGTH * BOND_LENGTH))
    projected = jnp.sum(weights[1:, :, None] * cosine, axis=0)
    s_orbital = weights[0][:, None]
    columns = [(s_orbital * SS_SIGMA - projected * SP_SIGMA) * radial]
    for direction in range(3):
        columns.append(
            (
                s_orbital * cosine[direction] * SP_SIGMA
                + projected * cosine[direction] * (PP_SIGMA - PP_PI)
                + weights[1 + direction][:, None] * PP_PI
            )
            * radial
        )
    return jnp.stack(columns, axis=1).reshape(row_count, 4 * atom_count)


def cluster_blocks(own_pos, near_pos, present, start_row, row_count):
    made = jax.vmap(build_rows, in_axes=(None, 0, None, None))(
        own_pos, near_pos, start_row, row_count
    )
    return made * present.astype(jnp.float32)[:, None, None]


def per_device(positions, probes, neighbours):
    cluster_count = positions.shape[0]
    orbitals = 4 * positions.shape[2]
    probe_span = probes.shape[1]
    space_count = lax.axis_size("space")
    space_rank = lax.axis_index("space")
    probe_count = lax.axis_size("probe")
    probe_rank = lax.axis_index("probe")
    total_probes = probe_span * probe_count
    present = neighbours >= 0
    target = jnp.where(present, neighbours, space_rank * cluster_count)
    halo_slot = (
        target // cluster_count - space_rank + 1
    ) % space_count * cluster_count + target % cluster_count
    shifts = offsets()
    build = jax.vmap(cluster_blocks, in_axes=(0, 0, 0, None, None))
    all_probes = lax.all_gather(probes, "probe", axis=1, tiled=True)
    near_pos, near_all = (
        padded(positions, (("space", 0),), cluster_count),
        padded(all_probes, (("space", 0),), cluster_count),
    )
    own_near = lax.dynamic_slice_in_dim(near_all, probe_rank * probe_span, probe_span, 1)
    own_coords = positions.astype(jnp.float32)
    near_coords = near_pos.astype(jnp.float32)
    beside_all = near_coords[halo_slot] + shifts[None, :, :, None]
    blocks = build(own_coords, beside_all, present, 0, orbitals)
    row_sums = jnp.sum(jnp.abs(blocks), axis=(1, 3))
    spectral = lax.pmax(jnp.max(row_sums), "space")
    scaled = (blocks / spectral).astype(jnp.bfloat16)
    term_one = jnp.einsum(
        "ckpj,ckij->cpi", own_near[halo_slot], scaled, preferred_element_type=jnp.float32
    )
    one_half = term_one.astype(jnp.bfloat16)
    near_one = padded(one_half, (("space", 0),), cluster_count)
    probe_wide = probes.astype(jnp.float32)
    term_two = (
        2.0
        * jnp.einsum(
            "ckpj,ckij->cpi", near_one[halo_slot], scaled, preferred_element_type=jnp.float32
        )
        - probe_wide
    )
    mixture = (COEFF_ZERO * probe_wide + COEFF_ONE * term_one + COEFF_TWO * term_two).astype(
        jnp.bfloat16
    )
    row_share = orbitals // probe_count
    start_row = probe_rank * row_share
    whole_mixture = lax.all_gather(mixture, "probe", axis=1, tiled=True)
    row_mixture = lax.dynamic_slice_in_dim(whole_mixture, start_row, row_share, 2)

    def per_slot(pair):
        column, alive = pair
        gathered = near_all[column]
        product = jnp.einsum(
            "cpr,cpj->rcj", row_mixture, gathered, preferred_element_type=jnp.float32
        )
        return product * alive[None, :, None]

    stacked = lax.map(per_slot, (halo_slot.T, present.T.astype(jnp.float32)))
    sample = jnp.transpose(stacked, (1, 2, 0, 3))

    def energy(own_pos, halo_pos):
        nearby = halo_pos[halo_slot] + shifts[None, :, :, None]
        made = build(own_pos, nearby, present, start_row, row_share)
        return jnp.einsum("ckrj,rckj->", made, sample) / total_probes

    own_grad, near_grad = jax.grad(energy, argnums=(0, 1))(own_coords, near_coords)
    pull_terms = jnp.concatenate(
        [
            near_grad[:cluster_count],
            near_grad[cluster_count : 2 * cluster_count] + own_grad,
            near_grad[2 * cluster_count :],
        ],
        axis=0,
    )
    pull_terms = lax.psum(pull_terms, "probe")
    from_after = shifted(pull_terms[:cluster_count], "space", -1)
    from_before = shifted(pull_terms[2 * cluster_count :], "space", 1)
    forces = -(pull_terms[cluster_count : 2 * cluster_count] + from_after + from_before)
    density = (sample / jnp.sqrt(jnp.float32(total_probes))).astype(jnp.bfloat16)
    return (density, forces)


def solution(mesh):
    in_specs = (P("space", None, None), P("space", "probe", None), P("space", None))
    out_specs = (P("probe", "space", None, None), P("space", None, None))
    return jax.shard_map(
        per_device, mesh=mesh, in_specs=in_specs, out_specs=out_specs, check_vma=False
    )
```

profile of v0, /device:TPU:2, one launch (start us, length us, event | category | flops | bytes accessed | tf_op | source)
XLA Modules:
  0.0 363.5 jit_solution(9074232415770121323)
XLA Ops:
  7.9 8.2 %collective-permute-start.3 = (bf16[8,3,32]{2,1,0:T(4,128)(2,1)S(1)}, bf16[8,3,32]{2,1,0:T(4,128)(2,1)S(1)}, u32[]{:S(2)}, u32[]{:S(2)}) collective-permute-start(bf16[8,3,32]{2,1,0:T(4,128)(2,1)S(1)} %copy.64), channel_id=1, source_target_pairs={{8,0},{16,8},{24,16},{32,24},{40,32},{48,40},{56,48},{64,56},{72,6... | collective-permute-start | bytes 4616 | tf_op jit(solution)/shard_map/ppermute | solution.py:26
  18.1 5.3 %collective-permute-done.2 = bf16[8,3,32]{2,1,0:T(4,128)(2,1)S(1)} collective-permute-done((bf16[8,3,32]{2,1,0:T(4,128)(2,1)S(1)}, bf16[8,3,32]{2,1,0:T(4,128)(2,1)S(1)}, u32[]{:S(2)}, u32[]{:S(2)}) %collective-permute-start.2) | collective-permute-done | bytes 1568 | tf_op jit(solution)/shard_map/ppermute | solution.py:25
  24.9 2.0 fusion.7
  27.4 1.9 subtract_divide_fusion
  29.3 3.3 bitcast_multiply_fusion.3
  32.6 24.5 %all-gather.3.cloned.1.call-done = bf16[8,512,128]{2,1,0:T(8,128)(2,1)} async-done(((bf16[8,64,128]{2,1,0:T(8,128)(2,1)}), bf16[8,512,128]{2,1,0:T(8,128)(2,1)}) %all-gather.3.cloned.1.call-update) | async-done | bytes 1048592 | tf_op jit(solution)/shard_map/all_gather | solution.py:104
  57.2 5.5 %abs_reduce_fusion = (f32[8,128]{1,0:T(8,128)S(1)}, f32[8,15,128,4,32]{2,4,3,1,0:T(8,128)}) fusion(f32[8,15]{1,0:T(8,128)S(1)} %copy.68, f32[8,15,128,1,32]{2,4,3,1,0:T(8,128)} %get-tuple-element.79, f32[8,15,128,1,32]{2,4,3,1,0:T(8,128)} %get-tuple-element.78, f32[8,15,128,1,32]{2,4,3,1,0:T(8,128)S(1)} %get-tuple-element.77, ...), kind=kLoop, calls=%fused_computation.21 | loop fusion | flops 11795456 | bytes 15733216 | tf_op jit(solution)/shard_map/reduce_sum | solution.py:114
  63.3 84.3 %pmax.7 = f32[]{:T(128)} all-reduce(f32[]{:T(128)} %reduce_max.9), channel_id=1, replica_groups=mesh['space'=32,'probe'=8] {'space'}, use_global_device_ids=true, to_apply=%region_4.5 | all-reduce | flops 1 | bytes 8 | tf_op jit(solution)/shard_map/pmax | solution.py:115
  147.5 6.9 %fusion.6 = bf16[8,15,128,128]{2,3,1,0:T(8,128)(2,1)} fusion(f32[8,15,128,4,32]{2,4,3,1,0:T(8,128)} %get-tuple-element.81, f32[]{:T(128)} %pmax.7, f32[8,15]{1,0:T(8,128)S(1)} %copy.68), kind=kLoop, calls=%fused_computation.20 | loop fusion | flops 5898240 | bytes 11796964 | tf_op jit(solution)/shard_map/convert_element_type | solution.py:116
  154.4 1.3 constant_dynamic-update-slice_fusion.2
  155.9 11.2 %collective-permute-done.1 = bf16[8,512,128]{2,1,0:T(8,128)(2,1)S(1)} collective-permute-done((bf16[8,512,128]{2,1,0:T(8,128)(2,1)}, bf16[8,512,128]{2,1,0:T(8,128)(2,1)S(1)}, u32[]{:S(2)}, u32[]{:S(2)}) %collective-permute-start.1) | collective-permute-done | bytes 1048608 | tf_op jit(solution)/shard_map/ppermute | solution.py:26
  167.3 1.6 copy-done.1
  169.9 3.0 fusion.55
  172.9 6.1 %collective-permute-start.5 = (bf16[8,64,128]{2,1,0:T(8,128)(2,1)S(1)}, bf16[8,64,128]{2,1,0:T(8,128)(2,1)S(1)}, u32[]{:S(2)}, u32[]{:S(2)}) collective-permute-start(bf16[8,64,128]{2,1,0:T(8,128)(2,1)S(1)} %get-tuple-element.116), channel_id=1, source_target_pairs={{8,0},{16,8},{24,16},{32,24},{40,32},{48,40},{56,48},{64,56},{72,6... | collective-permute-start | bytes 393224 | tf_op jit(solution)/shard_map/ppermute | solution.py:26
  179.0 2.5 collective-permute-done.5
  181.5 6.1 %collective-permute-done.4 = bf16[8,64,128]{2,1,0:T(8,128)(2,1)S(1)} collective-permute-done((bf16[8,64,128]{2,1,0:T(8,128)(2,1)S(1)}, bf16[8,64,128]{2,1,0:T(8,128)(2,1)S(1)}, u32[]{:S(2)}, u32[]{:S(2)}) %collective-permute-start.4) | collective-permute-done | bytes 131104 | tf_op jit(solution)/shard_map/ppermute | solution.py:25
  188.6 3.7 %fusion.24 = bf16[8,64,128]{2,1,0:T(8,128)(2,1)} fusion(bf16[8,15,64,128]{3,2,1,0:T(8,128)(2,1)S(1)} %bitcast.225, bf16[8,15,128,128]{2,3,1,0:T(8,128)(2,1)} %fusion.6, bf16[8,64,128]{2,1,0:T(8,128)(2,1)S(1)} %copy-done.5, f32[8,64,128]{2,1,0:T(8,128)S(1)} %get-tuple-element.117), kind=kOutput, calls=%fused_computation.62 | convolution fusion | flops 252248064 | bytes 6422528 | tf_op jit(solution)/shard_map/ckpj,ckij->cpi/dot_general | solution.py:125
  193.4 3.5 multiply_reduce_fusion.1
  196.9 39.5 %all-gather.5.cloned.1.call-done = bf16[8,512,128]{2,1,0:T(8,128)(2,1)} async-done(((bf16[8,64,128]{2,1,0:T(8,128)(2,1)}), bf16[8,512,128]{2,1,0:T(8,128)(2,1)}) %all-gather.5.cloned.1.call-update) | async-done | bytes 1048592 | tf_op jit(solution)/shard_map/all_gather | solution.py:135
  236.4 1.6 constant_dynamic-slice_fusion.2
  238.3 53.6 %while.10 = (s32[]{:T(128)}, f32[15,16,8,128]{3,1,2,0:T(8,128)}, s32[15,8]{1,0:T(8,128)S(1)}, bf16[24,512,128]{2,1,0:T(8,128)(2,1)}, bf16[8,512,16]{1,2,0:T(8,128)(2,1)S(1)}, /*index=5*/f32[15,8]{1,0:T(8,128)S(1)}, s32[]{:T(128)}) while((s32[]{:T(128)}, f32[15,16,8,128]{3,1,2,0:T(8,128)}, s32[15,8]{1,0:T(8,128)S(1)}, ...), condition=%wide.region_6.7_spmd, body=%wide.region_5.6_spmd.sunk | while | flops 16794648 | bytes 3346753 | solution.py:146
  238.4 2.6 gather_fusion
  241.9 2.6 gather_fusion
  245.5 2.6 gather_fusion
  249.1 2.6 gather_fusion
  252.7 2.6 gather_fusion
  256.2 2.6 gather_fusion
  259.8 2.6 gather_fusion
  263.4 2.6 gather_fusion
  267.0 2.6 gather_fusion
  270.5 2.6 gather_fusion
  274.1 2.6 gather_fusion
  277.7 2.6 gather_fusion
  281.3 2.6 gather_fusion
  284.8 2.6 gather_fusion
  288.4 2.6 gather_fusion
  292.0 1.4 fusion.25
  293.4 3.0 reshape.494
  296.4 8.4 %fusion.52 = (f32[8,15,16,1,32]{4,3,2,0,1:T(1,128)S(1)}, f32[8,15,16,1,32]{4,3,2,0,1:T(1,128)S(1)}, f32[8,15,16,1,32]{4,3,2,0,1:T(1,128)S(1)}, f32[8,15,16,1,32]{4,3,2,0,1:T(1,128)S(1)}) fusion(f32[8,15,16,4,32]{4,3,2,0,1:T(4,128)} %reshape.494), kind=kLoop, calls=%fused_computation.158 | loop fusion | bytes 1966080 | tf_op jit(solution)/shard_map/transpose(jvp(vmap(vmap())))/unstack | solution.py:78
  304.8 1.0 multiply_add_fusion.2
  306.0 1.0 bitcast_multiply_fusion.15
  307.0 1.6 fusion.9
  308.6 1.3 multiply_add_fusion.1
  309.9 1.5 fusion.49
  311.5 5.1 %scatter_fusion = f32[24,3,32]{2,1,0:T(4,128)S(1)} fusion(f32[24,3,32]{2,1,0:T(4,128)S(1)} %broadcast_in_dim.20, s32[120]{0:T(128)S(1)} %reshape.505, f32[120,3,32]{2,1,0:T(4,128)S(1)} %bitcast.230), kind=kCustom, calls=%fused_computation.4 | custom fusion | flops 11520 | bytes 138720 | tf_op jit(solution)/shard_map/transpose(jvp())/scatter-add | solution.py:150
  316.9 31.8 %psum.7 = f32[24,3,32]{2,0,1:T(8,128)S(1)} all-reduce(f32[24,3,32]{2,0,1:T(8,128)S(1)} %pad_maximum_fusion.2), channel_id=1, replica_groups=mesh['space'=32,'probe'=8] {'probe'}, use_global_device_ids=true, to_apply=%region_13.14 | all-reduce | flops 2304 | bytes 18432 | tf_op jit(solution)/shard_map/psum | solution.py:163
  348.7 6.0 %collective-permute-start.6 = (f32[8,3,32]{2,0,1:T(8,128)S(1)}, f32[8,3,32]{2,0,1:T(8,128)S(1)}, u32[]{:S(2)}, u32[]{:S(2)}) collective-permute-start(f32[8,3,32]{2,0,1:T(8,128)S(1)} %get-tuple-element.102), channel_id=1, source_target_pairs={{8,0},{16,8},{24,16},{32,24},{40,32},{48,40},{56,48},{64,56},{72,6... | collective-permute-start | bytes 9224 | tf_op jit(solution)/shard_map/ppermute | solution.py:34
  354.7 1.2 fusion.27
  (131 shorter events, 24.1 us)
Async XLA Ops:
  7.2 50.0 %all-gather.3.cloned.1.call-start = ((), (), s32[]{:S(2)}) async-start(), calls=%async_computation | async-start | bytes 1179648 | tf_op jit(solution)/shard_map/all_gather | solution.py:104
  7.9 10.2 %collective-permute-start.3 = (bf16[8,3,32]{2,1,0:T(4,128)(2,1)S(1)}, bf16[8,3,32]{2,1,0:T(4,128)(2,1)S(1)}, u32[]{:S(2)}, u32[]{:S(2)}) collective-permute-start(bf16[8,3,32]{2,1,0:T(4,128)(2,1)S(1)} %copy.64), channel_id=1, source_target_pairs={{8,0},{16,8},{24,16},{32,24},{40,32},{48,40},{56,48},{64,56},{72,6... | collective-permute-start | bytes 4616 | tf_op jit(solution)/shard_map/ppermute | solution.py:26
  16.1 7.3 %collective-permute-start.2 = (bf16[8,3,32]{2,1,0:T(4,128)(2,1)S(1)}, bf16[8,3,32]{2,1,0:T(4,128)(2,1)S(1)}, u32[]{:S(2)}, u32[]{:S(2)}) collective-permute-start(bf16[8,3,32]{2,1,0:T(4,128)(2,1)S(1)} %copy.64), channel_id=1, source_target_pairs={{0,8},{8,16},{16,24},{24,32},{32,40},{40,48},{48,56},{56,64},{64,7... | collective-permute-start | bytes 4616 | tf_op jit(solution)/shard_map/ppermute | solution.py:25
  16.1 220.3 %all-gather.5.cloned.1.call-start = ((), (), s32[]{:S(2)}) async-start(), calls=%async_computation.1 | async-start | bytes 1179648 | tf_op jit(solution)/shard_map/all_gather | solution.py:135
  57.2 97.3 %collective-permute-start = (bf16[8,512,128]{2,1,0:T(8,128)(2,1)}, bf16[8,512,128]{2,1,0:T(8,128)(2,1)}, u32[]{:S(2)}, u32[]{:S(2)}) collective-permute-start(bf16[8,512,128]{2,1,0:T(8,128)(2,1)} %all-gather.3.cloned.1.call-done), channel_id=1, source_target_pairs={{0,8},{8,16},{16,24},{24,32},{32,40},{40,48},{48,56},{56,64},{64,7... | collective-permute-start | bytes 3145736 | tf_op jit(solution)/shard_map/ppermute | solution.py:25
  147.5 19.6 %collective-permute-start.1 = (bf16[8,512,128]{2,1,0:T(8,128)(2,1)}, bf16[8,512,128]{2,1,0:T(8,128)(2,1)S(1)}, u32[]{:S(2)}, u32[]{:S(2)}) collective-permute-start(bf16[8,512,128]{2,1,0:T(8,128)(2,1)} %all-gather.3.cloned.1.call-done), channel_id=1, source_target_pairs={{8,0},{16,8},{24,16},{32,24},{40,32},{48,40},{56,48},{64,56},{72,6... | collective-permute-start | bytes 3145736 | tf_op jit(solution)/shard_map/ppermute | solution.py:26
  147.5 8.2 %copy-start.4 = (bf16[8,512,128]{2,1,0:T(8,128)(2,1)S(1)}, bf16[8,512,128]{2,1,0:T(8,128)(2,1)}, u32[]{:S(2)}) copy-start(bf16[8,512,128]{2,1,0:T(8,128)(2,1)} %all-gather.3.cloned.1.call-done) | copy-start | bytes 3145732
  167.3 1.7 copy-start.1
  172.9 15.7 %copy-start.5 = (bf16[8,64,128]{2,1,0:T(8,128)(2,1)S(1)}, bf16[8,64,128]{2,1,0:T(8,128)(2,1)}, u32[]{:S(2)}) copy-start(bf16[8,64,128]{2,1,0:T(8,128)(2,1)} %param.7) | copy-start | bytes 393220
  172.9 8.6 %collective-permute-start.5 = (bf16[8,64,128]{2,1,0:T(8,128)(2,1)S(1)}, bf16[8,64,128]{2,1,0:T(8,128)(2,1)S(1)}, u32[]{:S(2)}, u32[]{:S(2)}) collective-permute-start(bf16[8,64,128]{2,1,0:T(8,128)(2,1)S(1)} %get-tuple-element.116), channel_id=1, source_target_pairs={{8,0},{16,8},{24,16},{32,24},{40,32},{48,40},{56,48},{64,56},{72,6... | collective-permute-start | bytes 393224 | tf_op jit(solution)/shard_map/ppermute | solution.py:26
  179.0 8.6 %collective-permute-start.4 = (bf16[8,64,128]{2,1,0:T(8,128)(2,1)S(1)}, bf16[8,64,128]{2,1,0:T(8,128)(2,1)S(1)}, u32[]{:S(2)}, u32[]{:S(2)}) collective-permute-start(bf16[8,64,128]{2,1,0:T(8,128)(2,1)S(1)} %get-tuple-element.116), channel_id=1, source_target_pairs={{0,8},{8,16},{16,24},{24,32},{32,40},{40,48},{48,56},{56,64},{64,7... | collective-permute-start | bytes 393224 | tf_op jit(solution)/shard_map/ppermute | solution.py:25
  188.6 3.8 %copy-start.6 = (bf16[8,3,32]{2,0,1:T(8,128)(2,1)S(1)}, bf16[8,3,32]{2,0,1:T(8,128)(2,1)}, u32[]{:S(2)}) copy-start(bf16[8,3,32]{2,0,1:T(8,128)(2,1)} %param.6) | copy-start | bytes 4612
  296.4 8.4 %copy-start = (f32[8,15,3,16,32]{4,3,0,1,2:T(8,128)S(1)}, f32[8,15,3,16,32]{4,3,0,1,2:T(8,128)}, u32[]{:S(2)}) copy-start(f32[8,15,3,16,32]{4,3,0,1,2:T(8,128)} %get-tuple-element.96) | copy-start | bytes 2211844
  304.8 1.2 copy-start.2
  309.9 44.8 %copy-start.3 = (f32[15,16,8,128]{3,1,2,0:T(8,128)S(1)}, f32[15,16,8,128]{3,1,2,0:T(8,128)}, u32[]{:S(2)}) copy-start(f32[15,16,8,128]{3,1,2,0:T(8,128)} %get-tuple-element.34) | copy-start | bytes 2949124
  348.7 7.3 %collective-permute-start.7 = (f32[8,3,32]{2,0,1:T(8,128)S(1)}, f32[8,3,32]{2,0,1:T(8,128)S(1)}, u32[]{:S(2)}, u32[]{:S(2)}) collective-permute-start(f32[8,3,32]{2,0,1:T(8,128)S(1)} %get-tuple-element.103), channel_id=1, source_target_pairs={{248,0},{0,8},{8,16},{16,24},{24,32},{32,40},{40,48},{48,56},{56,6... | collective-permute-start | bytes 9224 | tf_op jit(solution)/shard_map/ppermute | solution.py:34
  348.7 7.4 %collective-permute-start.6 = (f32[8,3,32]{2,0,1:T(8,128)S(1)}, f32[8,3,32]{2,0,1:T(8,128)S(1)}, u32[]{:S(2)}, u32[]{:S(2)}) collective-permute-start(f32[8,3,32]{2,0,1:T(8,128)S(1)} %get-tuple-element.102), channel_id=1, source_target_pairs={{8,0},{16,8},{24,16},{32,24},{40,32},{48,40},{56,48},{64,56},{72,6... | collective-permute-start | bytes 9224 | tf_op jit(solution)/shard_map/ppermute | solution.py:34
Sparse Core Ops, SparseCore 0:
  16.2 40.8 all-gather.2
  192.5 43.9 all-gather.4
where the time goes:
time: 369 us; the launch traced here: 364 us
  blocking collectives  116 us (31%)
  waiting for transfers between devices  89.4 us (24%)
  local copies, waits for them, and re-layouts  60.9 us (17%)
  other arithmetic  40.7 us (11%)
  matrix products  21.3 us (6%)
  starting transfers between devices  20.3 us (6%)
  between operations  14.4 us (4%)
    pmax x1, blocking collectives, per_device(): spectral = lax.pmax(jnp.max(row_sums), 'space')  84.3 us
    gather x15, local copies, waits for them, and re-layouts, per_slot(): gathered = near_all[column]  39.5 us
    all_gather x1, waiting for transfers between devices, per_device(): whole_mixture = lax.all_gather(mixture, 'probe', axis=1, tiled=True)  39.5 us
    psum x1, blocking collectives, per_device(): pull_terms = lax.psum(pull_terms, 'probe')  31.8 us
    all_gather x1, waiting for transfers between devices, per_device(): all_probes = lax.all_gather(probes, 'probe', axis=1, tiled=True)  24.5 us
    ppermute x3, starting transfers between devices, padded(): after = lax.ppermute(initial, axis, down)  14.3 us
    ppermute x3, waiting for transfers between devices, padded(): after = lax.ppermute(initial, axis, down)  13.8 us
    dot_general x15, matrix products, per_slot(): jnp.einsum('cpr,cpj->rcj', row_mixture, gathered, preferred_element_type=...  13.4 us
  transfers between devices with their start and end apart: 10, of which 7 were waited for; matrix products, arithmetic and copies ran while one was open for 9% of the time, Pallas kernels for 0%

commit v1 on v0

v1 whole, which is shorter than its diff:
```python
import functools
import math

import jax
import jax.numpy as jnp
import numpy as np
from jax import lax
from jax.experimental import pallas as pl
from jax.experimental.pallas import tpu as pltpu
from jax.sharding import PartitionSpec as P

SS_SIGMA = -1.938
SP_SIGMA = 1.745
PP_SIGMA = 3.05
PP_PI = -1.075
BOND_LENGTH = 2.35
SOFT_SQUARE = 0.25
CELL_EDGE = 10.86
COEFF_ZERO = 0.6
COEFF_ONE = -0.7
COEFF_TWO = 0.45

PP_SUM = PP_SIGMA - PP_PI
BOND_SQUARE = BOND_LENGTH * BOND_LENGTH
NEAR = 24
DEAD = 24
FAR = 1000.0
SLOTS = 16
F32 = jnp.float32
BF16 = jnp.bfloat16
VMEM = pl.BlockSpec(memory_space=pltpu.VMEM)
SMEM = pl.BlockSpec(memory_space=pltpu.SMEM)
PARAMS = pltpu.CompilerParams(vmem_limit_bytes=48 * 1024 * 1024)


def slot_offsets():
    half = CELL_EDGE / 2.0
    table = [[0.0, 0.0, 0.0]]
    for sign_x in (-1.0, 1.0):
        for sign_y in (-1.0, 1.0):
            for sign_z in (-1.0, 1.0):
                table.append([sign_x * half, sign_y * half, sign_z * half])
    for axis_pick in range(3):
        for sign_a in (1.0, -1.0):
            entry = [0.0, 0.0, 0.0]
            entry[axis_pick] = sign_a * CELL_EDGE
            table.append(entry)
    table.append([0.0, 0.0, 0.0])
    return np.array(table, dtype=np.float32)


def packed_shifts():
    table = slot_offsets().reshape(4, 4, 3).transpose(0, 2, 1)
    table = np.repeat(table, 32, axis=2)
    return np.pad(table, ((0, 0), (0, 5), (0, 0)))


def slot_shifts():
    table = np.broadcast_to(slot_offsets()[:, :, None], (SLOTS, 3, 128))
    return np.pad(table, ((0, 0), (0, 5), (0, 0)))


def lanes():
    return lax.broadcasted_iota(jnp.int32, (1, 128), 1)


def bond(columns, rows):
    d = [columns[x : x + 1, :] - rows[x] for x in range(3)]
    rho_square = d[0] * d[0] + d[1] * d[1] + d[2] * d[2] + SOFT_SQUARE
    inverse = lax.rsqrt(rho_square)
    radial = jnp.exp(1.0 - rho_square / BOND_SQUARE)
    return d, [v * inverse for v in d], radial, inverse


def four_slots(near_ref, slot_ref, shift_ref, c, g, lane):
    v = [near_ref[slot_ref[c, 4 * g + t]] for t in range(4)]
    joined = jnp.where(
        lane < 32, v[0], jnp.where(lane < 64, v[1], jnp.where(lane < 96, v[2], v[3]))
    )
    return joined + shift_ref[g]


def spectral_kernel(slot_ref, before_ref, own_ref, after_ref, shift_ref, row_ref, near_ref, peak_ref):
    near_ref[0:8] = before_ref[...]
    near_ref[8:16] = own_ref[...]
    near_ref[16:24] = after_ref[...]
    near_ref[DEAD] = jnp.full((8, 128), FAR, F32)
    lane = lanes()

    def one_cluster(c, peak):
        rows = [row_ref[c, x] for x in range(3)]
        sums = [jnp.zeros((32, 128), F32) for _ in range(4)]
        for g in range(4):
            columns = four_slots(near_ref, slot_ref, shift_ref, c, g, lane)
            _, cosine, radial, _ = bond(columns, rows)
            size = [jnp.abs(v) for v in cosine]
            sums[0] += (-SS_SIGMA + SP_SIGMA * (size[0] + size[1] + size[2])) * radial
            cross = {}
            for a in range(3):
                for b in range(a, 3):
                    product = cosine[a] * cosine[b] * PP_SUM
                    cross[a, b] = cross[b, a] = jnp.abs(product + PP_PI if a == b else product)
            for a in range(3):
                sums[1 + a] += (
                    SP_SIGMA * size[a] + cross[a, 0] + cross[a, 1] + cross[a, 2]
                ) * radial
        for v in sums:
            peak = jnp.maximum(peak, jnp.sum(v, axis=1, keepdims=True))
        return peak

    peak = lax.fori_loop(0, 8, one_cluster, jnp.zeros((32, 1), F32))
    peak_ref[...] = jnp.broadcast_to(jnp.max(peak), peak_ref.shape)


def build_kernel(
    slot_ref, near_ref, shift_ref, row_ref, before_ref, own_ref, after_ref,
    blocks_ref, operand_ref, turned_ref, probe_ref,
):
    lane = lanes()
    for part, ref in enumerate((before_ref, own_ref, after_ref)):
        for c in range(8):
            turned = ref[c].astype(F32).T
            if part == 1:
                turned_ref[c] = turned
            probe_ref[8 * part + c] = turned.astype(BF16)
    probe_ref[DEAD] = jnp.zeros((128, 64), BF16)

    def one_cluster(c, carry):
        rows = [row_ref[c, x] for x in range(3)]
        for g in range(4):
            columns = four_slots(near_ref, slot_ref, shift_ref, c, g, lane)
            _, cosine, radial, _ = bond(columns, rows)
            base = 512 * g
            blocks_ref[c, 0:32, base : base + 128] = SS_SIGMA * radial
            for a in range(3):
                wave = cosine[a] * SP_SIGMA * radial
                low, high = 32 * (a + 1), 128 * (a + 1)
                blocks_ref[c, 0:32, base + high : base + high + 128] = wave
                blocks_ref[c, low : low + 32, base : base + 128] = -wave
                for b in range(a, 3):
                    product = cosine[a] * cosine[b] * PP_SUM
                    value = (product + PP_PI if a == b else product) * radial
                    other = 128 * (b + 1)
                    blocks_ref[c, low : low + 32, base + other : base + other + 128] = value
                    if a != b:
                        blocks_ref[
                            c, 32 * (b + 1) : 32 * (b + 2), base + high : base + high + 128
                        ] = value
        gather_operand(slot_ref, probe_ref, operand_ref.at[c], c)
        return carry

    lax.fori_loop(0, 8, one_cluster, 0)


def gather_operand(slot_ref, source_ref, target_ref, c):
    for k in range(SLOTS):
        n = slot_ref[c, k]
        for b in range(4):
            low = 512 * (k // 4) + 128 * b + 32 * (k % 4)
            target_ref[low : low + 32, :] = source_ref[n, 32 * b : 32 * b + 32, :]


def first_kernel(peak_ref, blocks_ref, operand_ref, scaled_ref, one_ref, half_ref):
    inverse = 1.0 / jnp.max(peak_ref[...])

    def one_pair(pair, carry):
        for side in range(2):
            c = pair + 4 * side
            scaled = (blocks_ref[c] * inverse).astype(BF16)
            scaled_ref[c] = scaled
            one = jnp.dot(scaled, operand_ref[c], preferred_element_type=F32)
            one_ref[c] = one
            half_ref[pair, :, 64 * side : 64 * side + 64] = one.astype(BF16)
        return carry

    lax.fori_loop(0, 4, one_pair, 0)


def second_kernel(
    slot_ref, scaled_ref, before_ref, own_ref, after_ref, one_ref, turned_ref,
    mixture_ref, half_ref, operand_ref, joined_ref,
):
    for part, ref in enumerate((before_ref, own_ref, after_ref)):
        for pair in range(4):
            half_ref[8 * part + pair] = ref[pair, :, 0:64]
            half_ref[8 * part + pair + 4] = ref[pair, :, 64:128]
    half_ref[DEAD] = jnp.zeros((128, 64), BF16)

    def one_pair(pair, carry):
        for side in range(2):
            c = pair + 4 * side
            gather_operand(slot_ref, half_ref, operand_ref.at[side], c)
            two = jnp.dot(scaled_ref[c], operand_ref[side], preferred_element_type=F32)
            probe = turned_ref[c]
            term_two = 2.0 * two - probe
            mixture = COEFF_ZERO * probe + COEFF_ONE * one_ref[c] + COEFF_TWO * term_two
            joined_ref[:, 64 * side : 64 * side + 64] = mixture.astype(BF16)
        for q in range(8):
            mixture_ref[q, pl.ds(pl.multiple_of(16 * pair, 16), 16), :] = joined_ref[
                16 * q : 16 * q + 16, :
            ]
        return carry

    lax.fori_loop(0, 4, one_pair, 0)


def sample_kernel(
    slot_ref, rank_ref, mixture_ref, before_ref, own_ref, after_ref, near_ref, shift_ref, row_ref,
    density_ref, force_ref, left_ref, sample_ref, turn_ref, pull_ref,
):
    lane = lanes()
    rank = rank_ref[0]
    for q in range(8):
        block = mixture_ref[q]
        left_ref[0:64, 64 * q : 64 * q + 64] = block[:, 0:64]
        left_ref[64:128, 64 * q : 64 * q + 64] = block[:, 64:128]
    left = left_ref[...]
    for part, ref in enumerate((before_ref, own_ref, after_ref)):
        for pair in range(4):
            c = 2 * pair
            right = jnp.concatenate(
                [ref[:, c].reshape(512, 128), ref[:, c + 1].reshape(512, 128)], axis=1
            )
            product = jnp.dot(left, right, preferred_element_type=F32)
            sample_ref[8 * part + c] = product[:, 0:128]
            sample_ref[8 * part + c + 1] = product[:, 128:256]
    sample_ref[DEAD] = jnp.zeros((128, 128), F32)
    pull_ref[...] = jnp.zeros_like(pull_ref)

    orbital = rank // 2
    first_atom = 16 * (rank % 2)
    row_is = [(orbital == a).astype(F32) for a in range(4)]
    column_is = [(lane // 32 == b).astype(F32) for b in range(4)]
    constant = row_is[0] * SS_SIGMA * column_is[0] + PP_PI * (
        row_is[1] * column_is[1] + row_is[2] * column_is[2] + row_is[3] * column_is[3]
    )
    linear = [
        SP_SIGMA * (row_is[0] * column_is[1 + x] - column_is[0] * row_is[1 + x]) for x in range(3)
    ]
    row_sum = [PP_SUM * row_is[1 + x] for x in range(3)]
    column_sum = [PP_SUM * column_is[1 + x] for x in range(3)]
    row_lane = lax.broadcasted_iota(jnp.int32, (16, 128), 0) + first_atom
    on_row = lax.broadcasted_iota(jnp.int32, (16, 128), 1) == row_lane
    scale = 1.0 / math.sqrt(512.0)

    def one_cluster(c, carry):
        rows = [row_ref[c, x, pl.ds(pl.multiple_of(first_atom, 16), 16), :] for x in range(3)]
        own = [jnp.zeros((16, 128), F32) for _ in range(3)]
        for k in range(15):
            n = slot_ref[c, k]
            sample = sample_ref[n, pl.ds(pl.multiple_of(16 * c, 16), 16), :]
            turn_ref[pl.ds(k, 16, stride=SLOTS), :] = sample * scale
            columns = near_ref[n] + shift_ref[k]
            d, cosine, radial, inverse = bond(columns, rows)
            on_rows = row_is[1] * cosine[0] + row_is[2] * cosine[1] + row_is[3] * cosine[2]
            on_columns = (
                column_is[1] * cosine[0] + column_is[2] * cosine[1] + column_is[3] * cosine[2]
            )
            bent = PP_SUM * on_rows * on_columns
            slope = [
                linear[x] + row_sum[x] * on_columns + column_sum[x] * on_rows for x in range(3)
            ]
            straight = linear[0] * cosine[0] + linear[1] * cosine[1] + linear[2] * cosine[2]
            value = constant + straight + bent
            along = straight + 2.0 * bent
            weight = sample * radial
            across = weight * inverse
            inward = weight * (value * (-2.0 / BOND_SQUARE)) - across * (along * inverse)
            for x in range(3):
                pull = across * slope[x] + inward * d[x]
                own[x] = own[x] + pull
                pull_ref[n, x] = pull_ref[n, x] - (pull[0:8] + pull[8:16])
        for x in range(3):
            whole = jnp.broadcast_to(jnp.sum(own[x], axis=1, keepdims=True), (16, 128))
            placed = jnp.where(on_row, whole, 0.0)
            pull_ref[8 + c, x] = pull_ref[8 + c, x] + (placed[0:8] + placed[8:16])
        for r in range(16):
            density_ref[r, c] = turn_ref[SLOTS * r : SLOTS * r + 15, :].astype(BF16)
        return carry

    lax.fori_loop(0, 8, one_cluster, 0)

    total = jnp.sum(pull_ref[0:24], axis=2).reshape(72, 128)
    total = total + pltpu.roll(total, 64, 1)
    total = total + pltpu.roll(total, 32, 1)
    total = (total * (1.0 / 512.0)).reshape(24, 3, 128)
    joined = jnp.where(lane < 32, total[:, 0], jnp.where(lane < 64, total[:, 1], total[:, 2]))
    for q in range(8):
        force_ref[q] = joined


def around(block, size, distance):
    return lax.ppermute(block, "space", [((i - distance) % size, i) for i in range(size)])


def per_device(positions, probes, neighbours):
    space_count = lax.axis_size("space")
    space_rank = lax.axis_index("space")
    probe_rank = lax.axis_index("probe")
    both = lambda block: (around(block, space_count, 1), around(block, space_count, -1))

    coords = positions.astype(F32)
    packed = jnp.pad(jnp.tile(coords, (1, 1, 4)), ((0, 0), (0, 5), (0, 0)))
    pos_before, pos_after = both(packed)
    rows = jnp.broadcast_to(coords[..., None], (8, 3, 32, 128))
    present = neighbours >= 0
    slot = (neighbours // 8 - space_rank + 1) % space_count * 8 + neighbours % 8
    slot = jnp.pad(jnp.where(present, slot, DEAD), ((0, 0), (0, 1)), constant_values=DEAD)
    packed_shift = jnp.asarray(packed_shifts(), F32)
    slot_shift = jnp.asarray(slot_shifts(), F32)

    near, peak = pl.pallas_call(
        spectral_kernel,
        out_shape=(
            jax.ShapeDtypeStruct((NEAR + 1, 8, 128), F32),
            jax.ShapeDtypeStruct((space_count, 128), F32),
        ),
        in_specs=[SMEM] + [VMEM] * 5,
        out_specs=(VMEM, VMEM),
        compiler_params=PARAMS,
        name="spectral",
    )(slot, pos_before, packed, pos_after, packed_shift, rows)
    peaks = lax.all_to_all(peak, "space", 0, 0, tiled=True)

    probe_before, probe_after = both(probes)
    spread = jnp.broadcast_to(probes[None], (8,) + probes.shape)
    all_own = lax.all_to_all(spread, "probe", 0, 0, tiled=True).reshape(8, 8, 64, 128)
    all_before, all_after = both(all_own)

    blocks, operand, turned = pl.pallas_call(
        build_kernel,
        out_shape=(
            jax.ShapeDtypeStruct((8, 128, 2048), F32),
            jax.ShapeDtypeStruct((8, 2048, 64), BF16),
            jax.ShapeDtypeStruct((8, 128, 64), F32),
        ),
        in_specs=[SMEM] + [VMEM] * 6,
        out_specs=(VMEM, VMEM, VMEM),
        scratch_shapes=[pltpu.VMEM((NEAR + 1, 128, 64), BF16)],
        compiler_params=PARAMS,
        name="build",
    )(slot, near, packed_shift, rows, probe_before, probes, probe_after)

    scaled, one, half = pl.pallas_call(
        first_kernel,
        out_shape=(
            jax.ShapeDtypeStruct((8, 128, 2048), BF16),
            jax.ShapeDtypeStruct((8, 128, 64), F32),
            jax.ShapeDtypeStruct((4, 128, 128), BF16),
        ),
        in_specs=[VMEM] * 3,
        out_specs=(VMEM, VMEM, VMEM),
        compiler_params=PARAMS,
        name="first",
    )(peaks, blocks, operand)
    half_before, half_after = both(half)

    mixture = pl.pallas_call(
        second_kernel,
        out_shape=jax.ShapeDtypeStruct((8, 64, 128), BF16),
        in_specs=[SMEM] + [VMEM] * 6,
        out_specs=VMEM,
        scratch_shapes=[
            pltpu.VMEM((NEAR + 1, 128, 64), BF16),
            pltpu.VMEM((2, 2048, 64), BF16),
            pltpu.VMEM((128, 128), BF16),
        ],
        compiler_params=PARAMS,
        name="second",
    )(slot, scaled, half_before, half, half_after, one, turned)
    row_mixture = lax.all_to_all(mixture, "probe", 0, 0, tiled=True)

    density, force = pl.pallas_call(
        sample_kernel,
        out_shape=(
            jax.ShapeDtypeStruct((16, 8, 15, 128), BF16),
            jax.ShapeDtypeStruct((8, NEAR, 128), F32),
        ),
        in_specs=[SMEM, SMEM] + [VMEM] * 7,
        out_specs=(VMEM, VMEM),
        scratch_shapes=[
            pltpu.VMEM((128, 512), BF16),
            pltpu.VMEM((NEAR + 1, 128, 128), F32),
            pltpu.VMEM((16 * SLOTS, 128), F32),
            pltpu.VMEM((NEAR + 1, 3, 8, 128), F32),
        ],
        compiler_params=PARAMS,
        name="sample",
    )(
        slot, probe_rank.reshape(1), row_mixture, all_before, all_own, all_after,
        near, slot_shift, rows,
    )
    force = jnp.sum(lax.all_to_all(force, "probe", 0, 0, tiled=True), axis=0)
    from_after = around(force[0:8], space_count, -1)
    from_before = around(force[16:24], space_count, 1)
    forces = force[8:16] + from_after + from_before
    return density, forces[:, :96].reshape(8, 3, 32)


def solution(mesh):
    in_specs = (P("space", None, None), P("space", "probe", None), P("space", None))
    out_specs = (P("probe", "space", None, None), P("space", None, None))
    return jax.shard_map(
        per_device, mesh=mesh, in_specs=in_specs, out_specs=out_specs, check_vma=False
    )
```

time: 369 us -> 141 us (0.38); the launches traced: 364 us -> 140 us
  blocking collectives: 116 us -> 29 us
  waiting for transfers between devices: 89.4 us -> 28.6 us
  local copies, waits for them, and re-layouts: 60.9 us -> 19.4 us
  other arithmetic: 40.7 us -> 0.72 us
  Pallas kernels: 0 us -> 23.9 us
  matrix products: 21.3 us -> 0 us
  starting transfers between devices: 20.3 us -> 37.8 us
  between operations: 14.4 us -> 0.8 us
    pmax x1 -> x0, blocking collectives: 84.3 us -> none  [per_device(): spectral = lax.pmax(jnp.max(row_sums), 'space')]
    all_gather x2 -> x0, waiting for transfers between devices: 64 us -> none  [the longest x1 39.5 us: per_device(): whole_mixture = lax.all_gather(mixture, 'probe', axis=1, tiled=True)]
    gather x18 -> x0, local copies, waits for them, and re-layouts: 42.1 us -> none  [the longest x15 39.5 us: per_slot(): gathered = near_all[column]]
    psum x1 -> x0, blocking collectives: 31.8 us -> none  [per_device(): pull_terms = lax.psum(pull_terms, 'probe')]
    all_to_all x0 -> x2, blocking collectives: none -> 29 us  [the longest x1 19.9 us: per_device(): lax.all_to_all(spread, 'probe', 0, 0, tiled=True).reshape(8, 8, 64, 128)]
    pallas_call x0 -> x5, Pallas kernels: none -> 23.9 us  [the longest x1 6.86 us: per_device(): pl.pallas_call(first_kernel, out_shape=(jax.ShapeDtypeStruct((8, 128, 204...]
    dot_general x20 -> x0, matrix products: 21.3 us -> none  [the longest x15 13.4 us: per_slot(): jnp.einsum('cpr,cpj->rcj', row_mixture, gathered, preferred_element_type=...]
    all_to_all x0 -> x2, starting transfers between devices: none -> 16.4 us  [the longest x1 10.1 us: per_device(): peaks = lax.all_to_all(peak, 'space', 0, 0, tiled=True)]
  transfers between devices with their start and end apart: 10 -> 12, of which waited for: 7 -> 5; matrix products, arithmetic and copies ran while one was open for 9% -> 3% of each run, Pallas kernels for 0% -> 13%
where the time goes in v1:
time: 141 us; the launch traced here: 140 us
  starting transfers between devices  37.8 us (27%)
  blocking collectives  29 us (21%)
  waiting for transfers between devices  28.6 us (20%)
  Pallas kernels  23.9 us (17%)
  local copies, waits for them, and re-layouts  19.4 us (14%)
    ppermute x10, waiting for transfers between devices, around(): lax.ppermute(block, 'space', [((i - distance) % size, i) for i in range(s...  23.4 us
    ppermute x10, starting transfers between devices, around(): lax.ppermute(block, 'space', [((i - distance) % size, i) for i in range(s...  21.4 us
    all_to_all x1, blocking collectives, per_device(): lax.all_to_all(spread, 'probe', 0, 0, tiled=True).reshape(8, 8, 64, 128)  19.9 us
    unnamed x40, local copies, waits for them, and re-layouts  16.5 us
    all_to_all x1, starting transfers between devices, per_device(): peaks = lax.all_to_all(peak, 'space', 0, 0, tiled=True)  10.1 us
    all_to_all x1, blocking collectives, per_device(): force = jnp.sum(lax.all_to_all(force, 'probe', 0, 0, tiled=True), axis=0)  9 us
    pallas_call x1, Pallas kernels, per_device(): pl.pallas_call(first_kernel, out_shape=(jax.ShapeDtypeStruct((8, 128, 204...  6.86 us
    all_to_all x1, starting transfers between devices, per_device(): row_mixture = lax.all_to_all(mixture, 'probe', 0, 0, tiled=True)  6.29 us
  transfers between devices with their start and end apart: 12, of which 5 were waited for; matrix products, arithmetic and copies ran while one was open for 3% of the time, Pallas kernels for 13%

profile of v1, /device:TPU:2, one launch (start us, length us, event | category | flops | bytes accessed | tf_op | source)
XLA Modules:
  0.0 140.1 jit_solution(10345761950596317196)
XLA Ops:
  0.6 1.1 broadcast_in_dim.18
  1.8 19.9 %all_to_all.26.own_ref = bf16[8,8,64,128]{3,2,1,0:T(8,128)(2,1)S(1)} all-to-all(bf16[8,8,64,128]{3,2,1,0:T(8,128)(2,1)S(1)} %broadcast_in_dim.18), channel_id=1, replica_groups=mesh['space'=32,'probe'=8] {'probe'}, dimensions={0} | all-to-all | bytes 2097152 | tf_op jit(solution)/shard_map/all_to_all | solution.py:327
  21.7 0.0 collective-permute-start.6
  21.7 6.0 %collective-permute-start.7 = (bf16[8,8,64,128]{3,2,1,0:T(8,128)(2,1)S(1)}, bf16[8,8,64,128]{3,2,1,0:T(8,128)(2,1)S(1)}, u32[]{:S(2)}, u32[]{:S(2)}) collective-permute-start(bf16[8,8,64,128]{3,2,1,0:T(8,128)(2,1)S(1)} %all_to_all.26.own_ref), channel_id=1, source_target_pairs={{8,0},{16,8},{24,16},{32,24},{40,32},{48,40},{56,48},{64,56},{72,6... | collective-permute-start | bytes 3145736 | tf_op jit(solution)/shard_map/ppermute | solution.py:293
  27.7 0.7 tile.4
  28.4 0.1 tile.10
  28.5 0.1 collective-permute-start
  28.6 6.0 %collective-permute-start.1 = (f32[8,8,128]{2,1,0:T(8,128)S(1)}, f32[8,8,128]{2,1,0:T(8,128)S(1)}, u32[]{:S(2)}, u32[]{:S(2)}) collective-permute-start(f32[8,8,128]{2,1,0:T(8,128)S(1)} %pad.9.own_ref), channel_id=1, source_target_pairs={{8,0},{16,8},{24,16},{32,24},{40,32},{48,40},{56,48},{64,56},{72,6... | collective-permute-start | bytes 98312 | tf_op jit(solution)/shard_map/ppermute | solution.py:293
  34.6 7.5 %collective-permute-done.before_ref = f32[8,8,128]{2,1,0:T(8,128)S(1)} collective-permute-done((f32[8,8,128]{2,1,0:T(8,128)S(1)}, f32[8,8,128]{2,1,0:T(8,128)S(1)}, u32[]{:S(2)}, u32[]{:S(2)}) %collective-permute-start) | collective-permute-done | bytes 32800 | tf_op jit(solution)/shard_map/ppermute | solution.py:293
  42.1 0.6 copy-done.14
  42.7 0.7 fusion.5
  43.4 0.7 copy.15
  44.1 7.9 %collective-permute-done.1.after_ref = f32[8,8,128]{2,1,0:T(8,128)S(1)} collective-permute-done((f32[8,8,128]{2,1,0:T(8,128)S(1)}, f32[8,8,128]{2,1,0:T(8,128)S(1)}, u32[]{:S(2)}, u32[]{:S(2)}) %collective-permute-start.1) | collective-permute-done | bytes 32800 | tf_op jit(solution)/shard_map/ppermute | solution.py:293
  52.0 0.6 copy-done.16
  52.6 0.2 broadcast_in_dim.9.row_ref
  52.8 0.8 copy-done.10
  53.5 0.7 copy-done.12
  54.3 0.8 copy-done.15
  55.0 0.8 copy-done.17
  55.8 2.5 %spectral.1 = (f32[25,8,128]{2,1,0:T(8,128)S(1)}, f32[32,128]{1,0:T(8,128)S(1)}) custom-call(s32[8,16]{1,0:T(8,128)S(1)} %pad.8.slot_ref, f32[8,8,128]{2,1,0:T(8,128)S(1)} %copy-done.15, f32[8,8,128]{2,1,0:T(8,128)S(1)} %copy-done.10, f32[8,8,128]{2,1,0:T(8,128)S(1)} %copy-done.17, f32[4,8,128]{2,1,0:T(8,128)S(1)} %copy-done.12, ...), custom_call_target="tpu_custom_call" | custom-call | tf_op jit(solution)/shard_map/spectral/pallas_call | solution.py:312
  58.3 0.6 copy-done.6
  58.9 0.6 copy-done.18
  59.5 10.1 %all-to-all-start = ((f32[32,1,128]{2,1,0:T(1,128)}), f32[32,1,128]{2,1,0:T(1,128)}, u32[]{:S(2)}, u32[]{:S(2)}) async-start(f32[32,1,128]{2,1,0:T(1,128)} %bitcast.8), calls=%async_computation | async-start | bytes 32768 | tf_op jit(solution)/shard_map/all_to_all | solution.py:323
  69.7 0.0 copy-start.3
  69.7 0.9 copy-done.3
  70.6 0.9 copy-done.7
  71.5 0.7 copy-done.13
  72.2 6.1 %build.1 = (f32[8,128,2048]{2,1,0:T(8,128)}, bf16[8,2048,64]{2,1,0:T(8,128)(2,1)S(1)}, f32[8,128,64]{2,1,0:T(8,128)S(1)}) custom-call(s32[8,16]{1,0:T(8,128)S(1)} %pad.8.slot_ref, f32[25,8,128]{2,1,0:T(8,128)S(1)} %copy-done.7, f32[4,8,128]{2,1,0:T(8,128)S(1)} %copy-done.13, f32[8,3,32,128]{3,2,1,0:T(8,128)S(1)} %broadcast_in_dim.9.row_ref, ...), custom_call_target="tpu_custom_call" | custom-call | tf_op jit(solution)/shard_map/build/pallas_call | solution.py:330
  78.3 2.0 %copy-done = bf16[8,2048,64]{2,1,0:T(8,128)(2,1)} copy-done((bf16[8,2048,64]{2,1,0:T(8,128)(2,1)}, bf16[8,2048,64]{2,1,0:T(8,128)(2,1)S(1)}, u32[]{:S(2)}) %copy-start) | copy-done | bytes 2097176
  80.3 0.8 copy-done.1
  81.1 6.9 %first.1 = (bf16[8,128,2048]{2,1,0:T(8,128)(2,1)S(1)}, f32[8,128,64]{2,1,0:T(8,128)S(1)}, bf16[4,128,128]{2,1,0:T(8,128)(2,1)S(1)}) custom-call(f32[32,128]{1,0:T(8,128)} %bitcast.3.peak_ref, f32[8,128,2048]{2,1,0:T(8,128)} %get-tuple-element.14.blocks_ref, bf16[8,2048,64]{2,1,0:T(8,128)(2,1)} %copy-done), custom_call_target="tpu_custom_call" | custom-call | tf_op jit(solution)/shard_map/first/pallas_call | solution.py:344
  88.0 0.3 collective-permute-start.4
  88.2 5.8 %collective-permute-start.5 = (bf16[4,128,128]{2,1,0:T(8,128)(2,1)S(1)}, bf16[4,128,128]{2,1,0:T(8,128)(2,1)S(1)}, u32[]{:S(2)}, u32[]{:S(2)}) collective-permute-start(bf16[4,128,128]{2,1,0:T(8,128)(2,1)S(1)} %get-tuple-element.17.own_ref), channel_id=1, source_target_pairs={{8,0},{16,8},{24,16},{32,24},{40,32},{48,40},{56,48},{64,56},{72,6... | collective-permute-start | bytes 393224 | tf_op jit(solution)/shard_map/ppermute | solution.py:293
  94.0 2.7 %collective-permute-done.4.before_ref = bf16[4,128,128]{2,1,0:T(8,128)(2,1)S(1)} collective-permute-done((bf16[4,128,128]{2,1,0:T(8,128)(2,1)S(1)}, bf16[4,128,128]{2,1,0:T(8,128)(2,1)S(1)}, u32[]{:S(2)}, u32[]{:S(2)}) %collective-permute-start.4) | collective-permute-done | bytes 131104 | tf_op jit(solution)/shard_map/ppermute | solution.py:293
  96.7 3.3 %second.1 = bf16[8,64,128]{2,1,0:T(8,128)(2,1)S(1)} custom-call(s32[8,16]{1,0:T(8,128)S(1)} %pad.8.slot_ref, bf16[8,128,2048]{2,1,0:T(8,128)(2,1)S(1)} %get-tuple-element.16.scaled_ref, bf16[4,128,128]{2,1,0:T(8,128)(2,1)S(1)} %collective-permute-done.4.before_ref, bf16[4,128,128]{2,1,0:T(8,128)(2,1)S(1)} %get-tuple-element.17.own_ref, ...), custom_call_target="tpu_custom_call" | custom-call | tf_op jit(solution)/shard_map/second/pallas_call | solution.py:358
  100.0 0.7 copy-done.4
  100.7 6.3 %all-to-all-start.1 = ((bf16[8,64,128]{2,1,0:T(8,128)(2,1)}), bf16[8,64,128]{2,1,0:T(8,128)(2,1)}, u32[]{:S(2)}, u32[]{:S(2)}) async-start(bf16[8,64,128]{2,1,0:T(8,128)(2,1)} %copy-done.4), calls=%async_computation.1 | async-start | bytes 262144 | tf_op jit(solution)/shard_map/all_to_all | solution.py:371
  107.0 5.2 %all-to-all-done.1.mixture_ref = bf16[8,64,128]{2,1,0:T(8,128)(2,1)} async-done(((bf16[8,64,128]{2,1,0:T(8,128)(2,1)}), bf16[8,64,128]{2,1,0:T(8,128)(2,1)}, u32[]{:S(2)}, u32[]{:S(2)}) %all-to-all-start.1) | async-done | bytes 131104 | tf_op jit(solution)/shard_map/all_to_all | solution.py:371
  112.2 0.9 copy-done.8
  113.1 0.8 copy-done.11
  113.9 5.1 %sample.1 = (bf16[16,8,15,128]{3,2,1,0:T(8,128)(2,1)S(1)}, f32[8,24,128]{2,1,0:T(8,128)S(1)}) custom-call(s32[8,16]{1,0:T(8,128)S(1)} %pad.8.slot_ref, s32[1]{0:T(128)} %bitcast.rank_ref, bf16[8,64,128]{2,1,0:T(8,128)(2,1)} %all-to-all-done.1.mixture_ref, bf16[8,8,64,128]{3,2,1,0:T(8,128)(2,1)S(1)} %collective-permute-done.6.before_ref, ...), custom_call_target="tpu_custom_call" | custom-call | tf_op jit(solution)/shard_map/sample/pallas_call | solution.py:373
  119.1 0.8 copy-done.5
  119.8 9.0 %all_to_all.27 = f32[8,24,128]{2,1,0:T(8,128)S(1)} all-to-all(f32[8,24,128]{2,1,0:T(8,128)S(1)} %get-tuple-element.21), channel_id=1, replica_groups=mesh['space'=32,'probe'=8] {'probe'}, dimensions={0} | all-to-all | bytes 196608 | tf_op jit(solution)/shard_map/all_to_all | solution.py:393
  128.9 3.3 %collective-permute-start.8 = (f32[8,128]{1,0:T(8,128)S(1)}, f32[8,128]{1,0:T(8,128)S(1)}, u32[]{:S(2)}, u32[]{:S(2)}) collective-permute-start(f32[8,128]{1,0:T(8,128)S(1)} %get-tuple-element.28), channel_id=1, source_target_pairs={{8,0},{16,8},{24,16},{32,24},{40,32},{48,40},{56,48},{64,56},{72,6... | collective-permute-start | bytes 12296 | tf_op jit(solution)/shard_map/ppermute | solution.py:293
  132.2 2.0 %copy.17 = bf16[16,8,15,128]{3,1,2,0:T(8,128)(2,1)} copy(bf16[16,8,15,128]{3,2,1,0:T(8,128)(2,1)} %copy-done.5) | data formatting | bytes 983040
  134.1 5.3 %collective-permute-done.9 = f32[8,128]{1,0:T(8,128)S(1)} collective-permute-done((f32[8,128]{1,0:T(8,128)S(1)}, f32[8,128]{1,0:T(8,128)S(1)}, u32[]{:S(2)}, u32[]{:S(2)}) %collective-permute-start.9) | collective-permute-done | bytes 4128 | tf_op jit(solution)/shard_map/ppermute | solution.py:293
  139.4 0.1 reshape.19
  139.5 0.6 copy.18
  (36 shorter events, 0.1 us)
Async XLA Ops:
  21.7 90.4 %collective-permute-start.6 = (bf16[8,8,64,128]{3,2,1,0:T(8,128)(2,1)S(1)}, bf16[8,8,64,128]{3,2,1,0:T(8,128)(2,1)S(1)}, u32[]{:S(2)}, u32[]{:S(2)}) collective-permute-start(bf16[8,8,64,128]{3,2,1,0:T(8,128)(2,1)S(1)} %all_to_all.26.own_ref), channel_id=1, source_target_pairs={{248,0},{0,8},{8,16},{16,24},{24,32},{32,40},{40,48},{48,56},{56,6... | collective-permute-start | bytes 3145736 | tf_op jit(solution)/shard_map/ppermute | solution.py:293
  21.7 90.4 %collective-permute-start.7 = (bf16[8,8,64,128]{3,2,1,0:T(8,128)(2,1)S(1)}, bf16[8,8,64,128]{3,2,1,0:T(8,128)(2,1)S(1)}, u32[]{:S(2)}, u32[]{:S(2)}) collective-permute-start(bf16[8,8,64,128]{3,2,1,0:T(8,128)(2,1)S(1)} %all_to_all.26.own_ref), channel_id=1, source_target_pairs={{8,0},{16,8},{24,16},{32,24},{40,32},{48,40},{56,48},{64,56},{72,6... | collective-permute-start | bytes 3145736 | tf_op jit(solution)/shard_map/ppermute | solution.py:293
  28.5 15.6 %copy-start.9 = (f32[8,8,128]{2,1,0:T(8,128)}, f32[8,8,128]{2,1,0:T(8,128)S(1)}, u32[]{:S(2)}) copy-start(f32[8,8,128]{2,1,0:T(8,128)S(1)} %pad.9.own_ref) | copy-start | bytes 98308
  28.5 13.6 %collective-permute-start = (f32[8,8,128]{2,1,0:T(8,128)S(1)}, f32[8,8,128]{2,1,0:T(8,128)S(1)}, u32[]{:S(2)}, u32[]{:S(2)}) collective-permute-start(f32[8,8,128]{2,1,0:T(8,128)S(1)} %pad.9.own_ref), channel_id=1, source_target_pairs={{248,0},{0,8},{8,16},{16,24},{24,32},{32,40},{40,48},{48,56},{56,6... | collective-permute-start | bytes 98312 | tf_op jit(solution)/shard_map/ppermute | solution.py:293
  28.6 23.4 %collective-permute-start.1 = (f32[8,8,128]{2,1,0:T(8,128)S(1)}, f32[8,8,128]{2,1,0:T(8,128)S(1)}, u32[]{:S(2)}, u32[]{:S(2)}) collective-permute-start(f32[8,8,128]{2,1,0:T(8,128)S(1)} %pad.9.own_ref), channel_id=1, source_target_pairs={{8,0},{16,8},{24,16},{32,24},{40,32},{48,40},{56,48},{64,56},{72,6... | collective-permute-start | bytes 98312 | tf_op jit(solution)/shard_map/ppermute | solution.py:293
  34.6 35.1 %collective-permute-start.2 = (bf16[8,64,128]{2,1,0:T(8,128)(2,1)}, bf16[8,64,128]{2,1,0:T(8,128)(2,1)}, u32[]{:S(2)}, u32[]{:S(2)}) collective-permute-start(bf16[8,64,128]{2,1,0:T(8,128)(2,1)} %own_ref.1), channel_id=1, source_target_pairs={{248,0},{0,8},{8,16},{16,24},{24,32},{32,40},{40,48},{48,56},{56,6... | collective-permute-start | bytes 393224 | tf_op jit(solution)/shard_map/ppermute | solution.py:293
  42.1 0.6 copy-start.14
  42.7 27.0 %collective-permute-start.3 = (bf16[8,64,128]{2,1,0:T(8,128)(2,1)}, bf16[8,64,128]{2,1,0:T(8,128)(2,1)}, u32[]{:S(2)}, u32[]{:S(2)}) collective-permute-start(bf16[8,64,128]{2,1,0:T(8,128)(2,1)} %own_ref.1), channel_id=1, source_target_pairs={{8,0},{16,8},{24,16},{32,24},{40,32},{48,40},{56,48},{64,56},{72,6... | collective-permute-start | bytes 393224 | tf_op jit(solution)/shard_map/ppermute | solution.py:293
  52.0 0.6 copy-start.16
  52.8 0.8 copy-start.10
  53.5 0.7 copy-start.12
  54.2 0.8 copy-start.15
  55.0 0.8 copy-start.17
  58.3 0.6 copy-start.6
  58.9 0.6 copy-start.18
  59.5 21.6 %all-to-all-start = ((f32[32,1,128]{2,1,0:T(1,128)}), f32[32,1,128]{2,1,0:T(1,128)}, u32[]{:S(2)}, u32[]{:S(2)}) async-start(f32[32,1,128]{2,1,0:T(1,128)} %bitcast.8), calls=%async_computation | async-start | bytes 32768 | tf_op jit(solution)/shard_map/all_to_all | solution.py:323
  69.7 0.9 copy-start.3
  70.6 0.9 copy-start.7
  71.5 0.7 copy-start.13
  78.2 2.0 %copy-start = (bf16[8,2048,64]{2,1,0:T(8,128)(2,1)}, bf16[8,2048,64]{2,1,0:T(8,128)(2,1)S(1)}, u32[]{:S(2)}) copy-start(bf16[8,2048,64]{2,1,0:T(8,128)(2,1)S(1)} %get-tuple-element.15.operand_ref) | copy-start | bytes 6291460
  80.3 0.8 copy-start.1
  81.1 15.6 %copy-start.2 = (f32[8,128,64]{2,1,0:T(8,128)S(1)}, f32[8,128,64]{2,1,0:T(8,128)}, u32[]{:S(2)}) copy-start(f32[8,128,64]{2,1,0:T(8,128)} %copy-done.1) | copy-start | bytes 786436
  88.0 8.7 %collective-permute-start.4 = (bf16[4,128,128]{2,1,0:T(8,128)(2,1)S(1)}, bf16[4,128,128]{2,1,0:T(8,128)(2,1)S(1)}, u32[]{:S(2)}, u32[]{:S(2)}) collective-permute-start(bf16[4,128,128]{2,1,0:T(8,128)(2,1)S(1)} %get-tuple-element.17.own_ref), channel_id=1, source_target_pairs={{248,0},{0,8},{8,16},{16,24},{24,32},{32,40},{40,48},{48,56},{56,6... | collective-permute-start | bytes 393224 | tf_op jit(solution)/shard_map/ppermute | solution.py:293
  88.2 8.5 %collective-permute-start.5 = (bf16[4,128,128]{2,1,0:T(8,128)(2,1)S(1)}, bf16[4,128,128]{2,1,0:T(8,128)(2,1)S(1)}, u32[]{:S(2)}, u32[]{:S(2)}) collective-permute-start(bf16[4,128,128]{2,1,0:T(8,128)(2,1)S(1)} %get-tuple-element.17.own_ref), channel_id=1, source_target_pairs={{8,0},{16,8},{24,16},{32,24},{40,32},{48,40},{56,48},{64,56},{72,6... | collective-permute-start | bytes 393224 | tf_op jit(solution)/shard_map/ppermute | solution.py:293
  100.0 0.7 copy-start.4
  100.7 11.5 %all-to-all-start.1 = ((bf16[8,64,128]{2,1,0:T(8,128)(2,1)}), bf16[8,64,128]{2,1,0:T(8,128)(2,1)}, u32[]{:S(2)}, u32[]{:S(2)}) async-start(bf16[8,64,128]{2,1,0:T(8,128)(2,1)} %copy-done.4), calls=%async_computation.1 | async-start | bytes 262144 | tf_op jit(solution)/shard_map/all_to_all | solution.py:371
  112.2 0.9 copy-start.8
  113.1 0.8 copy-start.11
  119.0 0.8 copy-start.5
  128.9 5.3 %collective-permute-start.8 = (f32[8,128]{1,0:T(8,128)S(1)}, f32[8,128]{1,0:T(8,128)S(1)}, u32[]{:S(2)}, u32[]{:S(2)}) collective-permute-start(f32[8,128]{1,0:T(8,128)S(1)} %get-tuple-element.28), channel_id=1, source_target_pairs={{8,0},{16,8},{24,16},{32,24},{40,32},{48,40},{56,48},{64,56},{72,6... | collective-permute-start | bytes 12296 | tf_op jit(solution)/shard_map/ppermute | solution.py:293
  132.2 7.3 %collective-permute-start.9 = (f32[8,128]{1,0:T(8,128)S(1)}, f32[8,128]{1,0:T(8,128)S(1)}, u32[]{:S(2)}, u32[]{:S(2)}) collective-permute-start(f32[8,128]{1,0:T(8,128)S(1)} %get-tuple-element.29), channel_id=1, source_target_pairs={{248,0},{0,8},{8,16},{16,24},{24,32},{32,40},{40,48},{48,56},{56,6... | collective-permute-start | bytes 12296 | tf_op jit(solution)/shard_map/ppermute | solution.py:293

commit v2 on v1

v2 whole, which is shorter than its diff:
```python
import functools
import math

import jax
import jax.numpy as jnp
import numpy as np
from jax import lax
from jax.experimental import pallas as pl
from jax.experimental.pallas import tpu as pltpu
from jax.sharding import PartitionSpec as P

SS_SIGMA = -1.938
SP_SIGMA = 1.745
PP_SIGMA = 3.05
PP_PI = -1.075
BOND_LENGTH = 2.35
SOFT_SQUARE = 0.25
CELL_EDGE = 10.86
COEFF_ZERO = 0.6
COEFF_ONE = -0.7
COEFF_TWO = 0.45

PP_SUM = PP_SIGMA - PP_PI
BOND_SQUARE = BOND_LENGTH * BOND_LENGTH
NEAR = 24
DEAD = 24
FAR = 1000.0
SLOTS = 16
F32 = jnp.float32
BF16 = jnp.bfloat16
WHOLE = pl.BlockSpec()
SMEM = pl.BlockSpec(memory_space=pltpu.SMEM)


def params(mebibytes):
    return pltpu.CompilerParams(vmem_limit_bytes=mebibytes * 1024 * 1024)


def slot_offsets():
    half = CELL_EDGE / 2.0
    table = [[0.0, 0.0, 0.0]]
    for sign_x in (-1.0, 1.0):
        for sign_y in (-1.0, 1.0):
            for sign_z in (-1.0, 1.0):
                table.append([sign_x * half, sign_y * half, sign_z * half])
    for axis_pick in range(3):
        for sign_a in (1.0, -1.0):
            entry = [0.0, 0.0, 0.0]
            entry[axis_pick] = sign_a * CELL_EDGE
            table.append(entry)
    table.append([0.0, 0.0, 0.0])
    return np.array(table, dtype=np.float32)


def fill_shifts(shift_ref):
    lane = lanes()
    table = slot_offsets()
    for g in range(4):
        for x in range(3):
            v = [float(table[4 * g + t, x]) for t in range(4)]
            shift_ref[g, x : x + 1, :] = jnp.where(
                lane < 32, v[0], jnp.where(lane < 64, v[1], jnp.where(lane < 96, v[2], v[3]))
            )


def lanes():
    return lax.broadcasted_iota(jnp.int32, (1, 128), 1)


def bond(columns, rows):
    d = [columns[x : x + 1, :] - rows[x] for x in range(3)]
    rho_square = d[0] * d[0] + d[1] * d[1] + d[2] * d[2] + SOFT_SQUARE
    inverse = lax.rsqrt(rho_square)
    radial = jnp.exp(1.0 - rho_square / BOND_SQUARE)
    return d, [v * inverse for v in d], radial, inverse


def four_slots(near_ref, slot_ref, shift_ref, c, g, lane):
    v = [near_ref[slot_ref[c, 4 * g + t]] for t in range(4)]
    joined = jnp.where(
        lane < 32, v[0], jnp.where(lane < 64, v[1], jnp.where(lane < 96, v[2], v[3]))
    )
    return joined + shift_ref[g]


def spectral_kernel(
    slot_ref, before_ref, own_ref, after_ref, near_ref, row_ref, peak_ref, shift_ref
):
    fill_shifts(shift_ref)
    for part, ref in enumerate((before_ref, own_ref, after_ref)):
        for x in range(3):
            coords = ref[x].astype(F32)
            wide = jnp.concatenate([coords] * 4, axis=1)
            for n in range(8):
                near_ref[8 * part + n, x : x + 1, :] = wide[n : n + 1, :]
            if part == 1:
                upright = wide.T
                for c in range(8):
                    row_ref[c, x] = jnp.broadcast_to(upright[0:32, c : c + 1], (32, 128))
    near_ref[DEAD] = jnp.full((8, 128), FAR, F32)
    lane = lanes()

    def one_cluster(c, peak):
        rows = [row_ref[c, x] for x in range(3)]
        sums = [jnp.zeros((32, 128), F32) for _ in range(4)]
        for g in range(4):
            columns = four_slots(near_ref, slot_ref, shift_ref, c, g, lane)
            _, cosine, radial, _ = bond(columns, rows)
            size = [jnp.abs(v) for v in cosine]
            sums[0] += (-SS_SIGMA + SP_SIGMA * (size[0] + size[1] + size[2])) * radial
            cross = {}
            for a in range(3):
                for b in range(a, 3):
                    product = cosine[a] * cosine[b] * PP_SUM
                    cross[a, b] = cross[b, a] = jnp.abs(product + PP_PI if a == b else product)
            for a in range(3):
                sums[1 + a] += (
                    SP_SIGMA * size[a] + cross[a, 0] + cross[a, 1] + cross[a, 2]
                ) * radial
        for v in sums:
            peak = jnp.maximum(peak, jnp.sum(v, axis=1, keepdims=True))
        return peak

    peak = lax.fori_loop(0, 8, one_cluster, jnp.zeros((32, 1), F32))
    peak_ref[...] = jnp.broadcast_to(jnp.max(peak), peak_ref.shape)


def gather_operand(slot_ref, source_ref, target_ref, c):
    for k in range(SLOTS):
        n = slot_ref[c, k]
        for b in range(4):
            low = 512 * (k // 4) + 128 * b + 32 * (k % 4)
            target_ref[low : low + 32, :] = source_ref[n, 32 * b : 32 * b + 32, :]


def first_kernel(
    slot_ref, peak_ref, near_ref, row_ref, before_ref, own_ref, after_ref,
    scaled_ref, operand_ref, turned_ref, one_ref, half_ref, probe_ref, shift_ref,
):
    fill_shifts(shift_ref)
    lane = lanes()
    inverse_peak = 1.0 / jnp.max(peak_ref[...])
    for part, ref in enumerate((before_ref, own_ref, after_ref)):
        for c in range(8):
            turned = ref[c].astype(F32).T
            if part == 1:
                turned_ref[c] = turned
            probe_ref[8 * part + c] = turned.astype(BF16)
    probe_ref[DEAD] = jnp.zeros((128, 64), BF16)

    def one_pair(pair, carry):
        for side in range(2):
            c = pair + 4 * side
            rows = [row_ref[c, x] for x in range(3)]
            gather_operand(slot_ref, probe_ref, operand_ref.at[c], c)
            for g in range(4):
                columns = four_slots(near_ref, slot_ref, shift_ref, c, g, lane)
                _, cosine, radial, _ = bond(columns, rows)
                radial = radial * inverse_peak
                place = functools.partial(block_at, scaled_ref, c, g)
                place(0, 0, SS_SIGMA * radial)
                sp = SP_SIGMA * radial
                pp = PP_SUM * radial
                pi = PP_PI * radial
                for a in range(3):
                    wave = cosine[a] * sp
                    place(0, a + 1, wave)
                    place(a + 1, 0, -wave)
                    leaning = cosine[a] * pp
                    for b in range(a, 3):
                        value = leaning * cosine[b]
                        if a == b:
                            place(a + 1, a + 1, value + pi)
                        else:
                            place(a + 1, b + 1, value)
                            place(b + 1, a + 1, value)
            one = jnp.dot(scaled_ref[c], operand_ref[c], preferred_element_type=F32)
            one_ref[c] = one
            half_ref[pair, :, 64 * side : 64 * side + 64] = one.astype(BF16)
        return carry

    lax.fori_loop(0, 4, one_pair, 0)


def block_at(scaled_ref, c, g, a, b, value):
    low = 512 * g + 128 * b
    scaled_ref[c, 32 * a : 32 * a + 32, low : low + 128] = value.astype(BF16)


def second_kernel(
    slot_ref, near_ref, row_ref, scaled_ref, operand_ref, turned_ref, one_ref,
    before_ref, own_ref, after_ref, send_ref, half_ref, gathered_ref, pull_ref, shift_ref,
):
    fill_shifts(shift_ref)
    lane = lanes()
    for part, ref in enumerate((before_ref, own_ref, after_ref)):
        for pair in range(4):
            half_ref[8 * part + pair] = ref[pair, :, 0:64]
            half_ref[8 * part + pair + 4] = ref[pair, :, 64:128]
    half_ref[DEAD] = jnp.zeros((128, 64), BF16)
    pull_ref[...] = jnp.zeros_like(pull_ref)
    on_row = lax.broadcasted_iota(jnp.int32, (32, 128), 0) == lax.broadcasted_iota(
        jnp.int32, (32, 128), 1
    )

    def one_pair(pair, carry):
        for side in range(2):
            c = pair + 4 * side
            gather_operand(slot_ref, half_ref, gathered_ref.at[side], c)
            two = jnp.dot(scaled_ref[c], gathered_ref[side], preferred_element_type=F32)
            probe = turned_ref[c]
            term_two = 2.0 * two - probe
            mixture = COEFF_ZERO * probe + COEFF_ONE * one_ref[c] + COEFF_TWO * term_two
            mixture = mixture.astype(BF16)
            wide = mixture.astype(F32)
            for q in range(8):
                send_ref[
                    q, pl.ds(pl.multiple_of(16 * pair, 16), 16), 64 * side : 64 * side + 64
                ] = wide[16 * q : 16 * q + 16, :]
            rows = [row_ref[c, x] for x in range(3)]
            own = [jnp.zeros((32, 128), F32) for _ in range(3)]
            for g in range(4):
                sample = lax.dot_general(
                    mixture,
                    operand_ref[c, 512 * g : 512 * g + 512, :],
                    (((1,), (1,)), ((), ())),
                    preferred_element_type=F32,
                )
                columns = four_slots(near_ref, slot_ref, shift_ref, c, g, lane)
                pulls = pair_pulls(sample, columns, rows)
                for x in range(3):
                    own[x] = own[x] + pulls[x]
                    folded = jnp.sum(pulls[x].reshape(4, 8, 128), axis=0)
                    for t in range(4):
                        n = slot_ref[c, 4 * g + t]
                        pull_ref[n, x] = pull_ref[n, x] - jnp.where(lane // 32 == t, folded, 0.0)
            for x in range(3):
                whole = jnp.broadcast_to(jnp.sum(own[x], axis=1, keepdims=True), (32, 128))
                placed = jnp.where(on_row, whole, 0.0)
                pull_ref[8 + c, x] = pull_ref[8 + c, x] + jnp.sum(
                    placed.reshape(4, 8, 128), axis=0
                )
        return carry

    lax.fori_loop(0, 4, one_pair, 0)

    total = jnp.sum(pull_ref[0:24], axis=2).reshape(72, 128)
    total = total + pltpu.roll(total, 64, 1)
    total = total + pltpu.roll(total, 32, 1)
    total = (total * (1.0 / 512.0)).reshape(24, 3, 128)
    joined = jnp.where(lane < 32, total[:, 0], jnp.where(lane < 64, total[:, 1], total[:, 2]))
    for q in range(8):
        send_ref[q, 64:88, :] = joined


def pair_pulls(sample, columns, rows):
    part = lambda a, b: sample[32 * a : 32 * a + 32, 128 * b : 128 * b + 128]
    d, cosine, radial, inverse = bond(columns, rows)
    mixed = [SP_SIGMA * (part(0, 1 + x) - part(1 + x, 0)) for x in range(3)]
    double = [2.0 * PP_SUM * part(1 + x, 1 + x) for x in range(3)]
    cross = {}
    for a, b in ((0, 1), (0, 2), (1, 2)):
        cross[a, b] = cross[b, a] = PP_SUM * (part(1 + a, 1 + b) + part(1 + b, 1 + a))
    bent = []
    for a in range(3):
        b, c = [x for x in range(3) if x != a]
        bent.append(double[a] * cosine[a] + cross[a, b] * cosine[b] + cross[a, c] * cosine[c])
    still = SS_SIGMA * part(0, 0) + PP_PI * (part(1, 1) + part(2, 2) + part(3, 3))
    straight = mixed[0] * cosine[0] + mixed[1] * cosine[1] + mixed[2] * cosine[2]
    curved = bent[0] * cosine[0] + bent[1] * cosine[1] + bent[2] * cosine[2]
    value = still + straight + 0.5 * curved
    across = radial * inverse
    inward = radial * value * (-2.0 / BOND_SQUARE) - across * inverse * (straight + curved)
    return [across * (mixed[x] + bent[x]) + inward * d[x] for x in range(3)]


def sample_kernel(
    slot_ref, received_ref, before_ref, own_ref, after_ref, density_ref, left_ref, sample_ref, turn_ref
):
    for q in range(8):
        block = received_ref[q, 0:64, :].astype(BF16)
        left_ref[0:64, 64 * q : 64 * q + 64] = block[:, 0:64]
        left_ref[64:128, 64 * q : 64 * q + 64] = block[:, 64:128]
    left = left_ref[...]
    scale = 1.0 / math.sqrt(512.0)
    for part, ref in enumerate((before_ref, own_ref, after_ref)):
        for pair in range(4):
            c = 2 * pair
            right = jnp.concatenate(
                [ref[:, c].reshape(512, 128), ref[:, c + 1].reshape(512, 128)], axis=1
            )
            product = jnp.dot(left, right, preferred_element_type=F32) * scale
            sample_ref[8 * part + c] = product[:, 0:128]
            sample_ref[8 * part + c + 1] = product[:, 128:256]
    sample_ref[DEAD] = jnp.zeros((128, 128), F32)
    for c in range(8):
        for k in range(15):
            turn_ref[pl.ds(8 * k + c, 16, stride=120), :] = sample_ref[
                slot_ref[c, k], 16 * c : 16 * c + 16, :
            ]
    for r in range(16):
        density_ref[r] = turn_ref[120 * r : 120 * r + 120].astype(BF16).reshape(15, 8, 128)


def around(block, size, distance):
    return lax.ppermute(block, "space", [((i - distance) % size, i) for i in range(size)])


def per_device(positions, probes, neighbours):
    space_count = lax.axis_size("space")
    space_rank = lax.axis_index("space")
    both = lambda block: (around(block, space_count, 1), around(block, space_count, -1))

    pos_own = positions.transpose(1, 0, 2)
    pos_before, pos_after = both(pos_own)
    probe_before, probe_after = both(probes)
    spread = jnp.broadcast_to(probes[None], (8,) + probes.shape)
    all_own = lax.all_to_all(spread, "probe", 0, 0, tiled=True).reshape(8, 8, 64, 128)

    pos_before, pos_after, all_own = lax.optimization_barrier((pos_before, pos_after, all_own))
    all_before, all_after = both(all_own)

    present = neighbours >= 0
    slot = (neighbours // 8 - space_rank + 1) % space_count * 8 + neighbours % 8
    slot = jnp.pad(jnp.where(present, slot, DEAD), ((0, 0), (0, 1)), constant_values=DEAD)

    near, rows, peak = pl.pallas_call(
        spectral_kernel,
        out_shape=(
            jax.ShapeDtypeStruct((NEAR + 1, 8, 128), F32),
            jax.ShapeDtypeStruct((8, 3, 32, 128), F32),
            jax.ShapeDtypeStruct((space_count, 128), F32),
        ),
        in_specs=[SMEM] + [WHOLE] * 3,
        out_specs=(WHOLE,) * 3,
        scratch_shapes=[pltpu.VMEM((4, 8, 128), F32)],
        compiler_params=params(4),
        name="spectral",
    )(slot, pos_before, pos_own, pos_after)
    peaks = lax.all_to_all(peak, "space", 0, 0, tiled=True)

    scaled, operand, turned, one, half = pl.pallas_call(
        first_kernel,
        out_shape=(
            jax.ShapeDtypeStruct((8, 128, 2048), BF16),
            jax.ShapeDtypeStruct((8, 2048, 64), BF16),
            jax.ShapeDtypeStruct((8, 128, 64), F32),
            jax.ShapeDtypeStruct((8, 128, 64), F32),
            jax.ShapeDtypeStruct((4, 128, 128), BF16),
        ),
        in_specs=[SMEM] + [WHOLE] * 6,
        out_specs=(WHOLE,) * 5,
        scratch_shapes=[pltpu.VMEM((NEAR + 1, 128, 64), BF16), pltpu.VMEM((4, 8, 128), F32)],
        compiler_params=params(16),
        name="first",
    )(slot, peaks, near, rows, probe_before, probes, probe_after)
    half_before, half_after = both(half)
    half_before, half_after, all_before, all_after = lax.optimization_barrier(
        (half_before, half_after, all_before, all_after)
    )

    send = pl.pallas_call(
        second_kernel,
        out_shape=jax.ShapeDtypeStruct((8, 88, 128), F32),
        in_specs=[SMEM] + [WHOLE] * 9,
        out_specs=WHOLE,
        scratch_shapes=[
            pltpu.VMEM((NEAR + 1, 128, 64), BF16),
            pltpu.VMEM((2, 2048, 64), BF16),
            pltpu.VMEM((NEAR + 1, 3, 8, 128), F32),
            pltpu.VMEM((4, 8, 128), F32),
        ],
        compiler_params=params(16),
        name="second",
    )(slot, near, rows, scaled, operand, turned, one, half_before, half, half_after)
    received = lax.all_to_all(send, "probe", 0, 0, tiled=True)
    force = jnp.sum(received[:, 64:88], axis=0)
    from_after = around(force[0:8], space_count, -1)
    from_before = around(force[16:24], space_count, 1)

    density = pl.pallas_call(
        sample_kernel,
        out_shape=jax.ShapeDtypeStruct((16, 15, 8, 128), BF16),
        in_specs=[SMEM] + [WHOLE] * 4,
        out_specs=WHOLE,
        scratch_shapes=[
            pltpu.VMEM((128, 512), BF16),
            pltpu.VMEM((NEAR + 1, 128, 128), F32),
            pltpu.VMEM((16 * 120, 128), F32),
        ],
        compiler_params=params(16),
        name="sample",
    )(slot, received, all_before, all_own, all_after)
    forces = force[8:16] + from_after + from_before
    forces = jnp.stack([forces[:, 32 * x : 32 * x + 32] for x in range(3)])
    return density.transpose(0, 2, 1, 3), forces.transpose(1, 0, 2)


def solution(mesh):
    in_specs = (P("space", None, None), P("space", "probe", None), P("space", None))
    out_specs = (P("probe", "space", None, None), P("space", None, None))
    return jax.shard_map(
        per_device, mesh=mesh, in_specs=in_specs, out_specs=out_specs, check_vma=False
    )
```

time: 141 us -> 105 us (0.74)
  blocking collectives: 29 us -> 12.3 us
  starting transfers between devices: 37.8 us -> 25.3 us
  waiting for transfers between devices: 28.6 us -> 40.8 us
  local copies, waits for them, and re-layouts: 19.4 us -> 8.14 us
  Pallas kernels: 23.9 us -> 16.3 us
    ppermute x10, waiting for transfers between devices: 23.4 us -> 40.8 us  [around(): lax.ppermute(block, 'space', [((i - distance) % size, i) for i in range(s...]
    all_to_all x2 -> x1, blocking collectives: 29 us -> 12.3 us  [per_device(): received = lax.all_to_all(send, 'probe', 0, 0, tiled=True)]
    unnamed x40 -> x16, local copies, waits for them, and re-layouts: 16.5 us -> 5.9 us
    ppermute x10, starting transfers between devices: 21.4 us -> 14.6 us  [around(): lax.ppermute(block, 'space', [((i - distance) % size, i) for i in range(s...]
    all_to_all x1, starting transfers between devices: 10.1 us -> 4.48 us  [per_device(): peaks = lax.all_to_all(peak, 'space', 0, 0, tiled=True)]
    pallas_call x3 -> x2, Pallas kernels: 14.5 us -> 8.98 us  [the longest x1 6.62 us: per_device(): pl.pallas_call(second_kernel, out_shape=jax.ShapeDtypeStruct((8, 88, 128)...]
    all_to_all x1, waiting for transfers between devices: 5.17 us -> 0.01 us  [per_device(): lax.all_to_all(spread, 'probe', 0, 0, tiled=True).reshape(8, 8, 64, 128)]
    pallas_call x1, Pallas kernels: 6.86 us -> 4.58 us  [per_device(): pl.pallas_call(first_kernel, out_shape=(jax.ShapeDtypeStruct((8, 128, 204...]
  transfers between devices with their start and end apart: 12 -> 12, of which waited for: 5 -> 6; matrix products, arithmetic and copies ran while one was open for 3% -> 1% of each run, Pallas kernels for 13% -> 9%
where the time goes in v2:
time: 105 us
  waiting for transfers between devices  40.8 us (39%)
  starting transfers between devices  25.3 us (24%)
  Pallas kernels  16.3 us (16%)
  blocking collectives  12.3 us (12%)
  local copies, waits for them, and re-layouts  8.14 us (8%)
  other arithmetic  1.33 us (1%)
    ppermute x10, waiting for transfers between devices, around(): lax.ppermute(block, 'space', [((i - distance) % size, i) for i in range(s...  40.8 us
    ppermute x10, starting transfers between devices, around(): lax.ppermute(block, 'space', [((i - distance) % size, i) for i in range(s...  14.6 us
    all_to_all x1, blocking collectives, per_device(): received = lax.all_to_all(send, 'probe', 0, 0, tiled=True)  12.3 us
    pallas_call x1, Pallas kernels, per_device(): pl.pallas_call(second_kernel, out_shape=jax.ShapeDtypeStruct((8, 88, 128)...  6.62 us
    all_to_all x1, starting transfers between devices, per_device(): lax.all_to_all(spread, 'probe', 0, 0, tiled=True).reshape(8, 8, 64, 128)  6.18 us
    unnamed x16, local copies, waits for them, and re-layouts  5.9 us
    pallas_call x1, Pallas kernels, per_device(): pl.pallas_call(first_kernel, out_shape=(jax.ShapeDtypeStruct((8, 128, 204...  4.58 us
    all_to_all x1, starting transfers between devices, per_device(): peaks = lax.all_to_all(peak, 'space', 0, 0, tiled=True)  4.48 us
  transfers between devices with their start and end apart: 12, of which 6 were waited for; matrix products, arithmetic and copies ran while one was open for 1% of the time, Pallas kernels for 9%

profile of v2, /device:TPU:2, one launch (start us, length us, event | category | flops | bytes accessed | tf_op | source)
XLA Modules:
  0.0 105.0 jit_solution(7622521427960283625)
XLA Ops:
  0.6 2.2 %broadcast_in_dim.11 = bf16[8,8,64,128]{3,2,1,0:T(8,128)(2,1)} broadcast(bf16[8,64,128]{2,1,0:T(8,128)(2,1)} %own_ref.1), dimensions={1,2,3} | broadcast | bytes 1179648 | tf_op jit(solution)/shard_map/broadcast_in_dim | solution.py:317
  2.8 6.2 %all-to-all-start = ((bf16[8,8,64,128]{3,2,1,0:T(8,128)(2,1)}), bf16[8,8,64,128]{3,2,1,0:T(8,128)(2,1)S(1)}, u32[]{:S(2)}, u32[]{:S(2)}) async-start(bf16[8,8,64,128]{3,2,1,0:T(8,128)(2,1)} %broadcast_in_dim.11), calls=%async_computation | async-start | bytes 2097152 | tf_op jit(solution)/shard_map/all_to_all | solution.py:318
  9.0 6.7 %collective-permute-start.1 = (bf16[3,8,32]{2,1,0:T(8,128)(2,1)}, bf16[3,8,32]{2,1,0:T(8,128)(2,1)S(1)}, u32[]{:S(2)}, u32[]{:S(2)}) collective-permute-start(bf16[3,8,32]{2,1,0:T(8,128)(2,1)} %bitcast.15), channel_id=1, source_target_pairs={{8,0},{16,8},{24,16},{32,24},{40,32},{48,40},{56,48},{64,56},{72,6... | collective-permute-start | bytes 4616 | tf_op jit(solution)/shard_map/ppermute | solution.py:306
  15.7 0.0 collective-permute-start
  15.7 1.6 %collective-permute-done.1.after_ref = bf16[3,8,32]{2,1,0:T(8,128)(2,1)S(1)} collective-permute-done((bf16[3,8,32]{2,1,0:T(8,128)(2,1)}, bf16[3,8,32]{2,1,0:T(8,128)(2,1)S(1)}, u32[]{:S(2)}, u32[]{:S(2)}) %collective-permute-start.1) | collective-permute-done | bytes 1568 | tf_op jit(solution)/shard_map/ppermute | solution.py:306
  17.3 9.9 %collective-permute-done.before_ref = bf16[3,8,32]{2,1,0:T(8,128)(2,1)S(1)} collective-permute-done((bf16[3,8,32]{2,1,0:T(8,128)(2,1)}, bf16[3,8,32]{2,1,0:T(8,128)(2,1)S(1)}, u32[]{:S(2)}, u32[]{:S(2)}) %collective-permute-start) | collective-permute-done | bytes 1568 | tf_op jit(solution)/shard_map/ppermute | solution.py:306
  27.1 0.0 copy-start.6
  27.1 0.6 copy-done.6
  27.7 0.0 all-to-all-done.own_ref
  27.7 0.4 collective-permute-start.7
  28.1 0.1 collective-permute-start.6
  28.2 0.0 collective-permute-start.2
  28.2 6.0 %collective-permute-start.3 = (bf16[8,64,128]{2,1,0:T(8,128)(2,1)}, bf16[8,64,128]{2,1,0:T(8,128)(2,1)}, u32[]{:S(2)}, u32[]{:S(2)}) collective-permute-start(bf16[8,64,128]{2,1,0:T(8,128)(2,1)} %own_ref.1), channel_id=1, source_target_pairs={{8,0},{16,8},{24,16},{32,24},{40,32},{48,40},{56,48},{64,56},{72,6... | collective-permute-start | bytes 393224 | tf_op jit(solution)/shard_map/ppermute | solution.py:306
  34.2 0.7 fusion.5
  34.9 0.0 copy-start.5
  34.9 0.7 copy-done.5
  35.6 0.0 copy-start.7
  35.6 0.7 copy-done.7
  36.3 2.8 %spectral.1 = (f32[25,8,128]{2,1,0:T(8,128)S(1)}, f32[8,3,32,128]{3,2,1,0:T(8,128)S(1)}, f32[32,128]{1,0:T(8,128)S(1)}) custom-call(s32[8,16]{1,0:T(8,128)S(1)} %pad.4.slot_ref, bf16[3,8,32]{2,1,0:T(8,128)(2,1)S(1)} %copy-done.7, bf16[3,8,32]{2,1,0:T(8,128)(2,1)S(1)} %bitcast.17, bf16[3,8,32]{2,1,0:T(8,128)(2,1)S(1)} %collective-permute-done.1.after_ref), custom_call_target="tpu_custom_call" | custom-call | tf_op jit(solution)/shard_map/spectral/pallas_call | solution.py:327
  39.1 0.0 copy-start.1
  39.1 0.6 copy-done.1
  39.7 0.0 copy-start.4
  39.7 0.6 copy-done.4
  40.3 4.5 %all-to-all-start.1 = ((f32[32,1,128]{2,1,0:T(1,128)}), f32[32,1,128]{2,1,0:T(1,128)}, u32[]{:S(2)}, u32[]{:S(2)}) async-start(f32[32,1,128]{2,1,0:T(1,128)} %bitcast.14), calls=%async_computation.1 | async-start | bytes 32768 | tf_op jit(solution)/shard_map/all_to_all | solution.py:340
  44.8 16.2 %collective-permute-done.2.before_ref = bf16[8,64,128]{2,1,0:T(8,128)(2,1)} collective-permute-done((bf16[8,64,128]{2,1,0:T(8,128)(2,1)}, bf16[8,64,128]{2,1,0:T(8,128)(2,1)}, u32[]{:S(2)}, u32[]{:S(2)}) %collective-permute-start.2) | collective-permute-done | bytes 131104 | tf_op jit(solution)/shard_map/ppermute | solution.py:306
  61.0 0.0 collective-permute-done.3.after_ref
  61.0 0.0 all-to-all-done.1
  61.0 0.0 copy-start
  61.0 0.9 copy-done
  61.9 0.0 copy-start.2
  61.9 0.9 copy-done.2
  62.8 4.6 %first.1 = (bf16[8,128,2048]{2,1,0:T(8,128)(2,1)S(1)}, bf16[8,2048,64]{2,1,0:T(8,128)(2,1)S(1)}, f32[8,128,64]{2,1,0:T(8,128)S(1)}, f32[8,128,64]{2,1,0:T(8,128)S(1)}, bf16[4,128,128]{2,1,0:T(8,128)(2,1)S(1)}) custom-call(s32[8,16]{1,0:T(8,128)S(1)} %pad.4.slot_ref, f32[32,128]{1,0:T(8,128)} %bitcast.3.peak_ref, f32[25,8,128]{2,1,0:T(8,128)S(1)} %copy-done.2, ...), custom_call_target="tpu_custom_call" | custom-call | tf_op jit(solution)/shard_map/first/pallas_call | solution.py:342
  67.4 0.8 collective-permute-start.5
  68.3 0.0 collective-permute-start.4
  68.3 3.9 %collective-permute-done.5.after_ref = bf16[4,128,128]{2,1,0:T(8,128)(2,1)S(1)} collective-permute-done((bf16[4,128,128]{2,1,0:T(8,128)(2,1)S(1)}, bf16[4,128,128]{2,1,0:T(8,128)(2,1)S(1)}, u32[]{:S(2)}, u32[]{:S(2)}) %collective-permute-start.5) | collective-permute-done | bytes 131104 | tf_op jit(solution)/shard_map/ppermute | solution.py:306
  72.2 4.8 %collective-permute-done.4.before_ref = bf16[4,128,128]{2,1,0:T(8,128)(2,1)S(1)} collective-permute-done((bf16[4,128,128]{2,1,0:T(8,128)(2,1)S(1)}, bf16[4,128,128]{2,1,0:T(8,128)(2,1)S(1)}, u32[]{:S(2)}, u32[]{:S(2)}) %collective-permute-start.4) | collective-permute-done | bytes 131104 | tf_op jit(solution)/shard_map/ppermute | solution.py:306
  77.0 0.0 collective-permute-done.7.after_ref
  77.0 0.0 collective-permute-done.6.before_ref
  77.0 0.9 copy-done.3
  77.9 6.6 %second.1 = f32[8,88,128]{2,1,0:T(8,128)S(1)} custom-call(s32[8,16]{1,0:T(8,128)S(1)} %pad.4.slot_ref, f32[25,8,128]{2,1,0:T(8,128)S(1)} %copy-done.3, f32[8,3,32,128]{3,2,1,0:T(8,128)S(1)} %get-tuple-element.20.row_ref, bf16[8,128,2048]{2,1,0:T(8,128)(2,1)S(1)} %get-tuple-element.22.scaled_ref, bf16[8,2048,64]{2,1,0:T(8,128)(2,1)S(1)} %get-tuple-element.23.operand_ref, ...), custom_call_target="tpu_custom_call" | custom-call | tf_op jit(solution)/shard_map/second/pallas_call | solution.py:362
  84.5 12.3 %all_to_all.21.received_ref = f32[8,88,128]{2,1,0:T(8,128)S(1)} all-to-all(f32[8,88,128]{2,1,0:T(8,128)S(1)} %second.1), channel_id=1, replica_groups=mesh['space'=32,'probe'=8] {'probe'}, dimensions={0} | all-to-all | bytes 720896 | tf_op jit(solution)/shard_map/all_to_all | solution.py:376
  96.9 0.1 collective-permute-start.8
  97.0 0.5 collective-permute-start.9
  97.5 2.4 %sample.1 = bf16[16,15,8,128]{3,2,1,0:T(8,128)(2,1)} custom-call(s32[8,16]{1,0:T(8,128)S(1)} %pad.4.slot_ref, f32[8,88,128]{2,1,0:T(8,128)S(1)} %all_to_all.21.received_ref, bf16[8,8,64,128]{3,2,1,0:T(8,128)(2,1)S(1)} %collective-permute-done.6.before_ref, bf16[8,8,64,128]{3,2,1,0:T(8,128)(2,1)S(1)} %all-to-all-done.own_ref, ...), custom_call_target="tpu_custom_call" | custom-call | tf_op jit(solution)/shard_map/sample/pallas_call | solution.py:381
  99.8 0.0 collective-permute-done.8
  99.8 4.5 %collective-permute-done.9 = f32[8,128]{1,0:T(8,128)S(1)} collective-permute-done((f32[8,128]{1,0:T(8,128)S(1)}, f32[8,128]{1,0:T(8,128)S(1)}, u32[]{:S(2)}, u32[]{:S(2)}) %collective-permute-start.9) | collective-permute-done | bytes 4128 | tf_op jit(solution)/shard_map/ppermute | solution.py:306
  104.3 0.1 slice_bitcast_fusion.2
  104.4 0.6 maximum_bitcast_fusion
  (5 shorter events, 0.0 us)
Async XLA Ops:
  2.8 24.9 %all-to-all-start = ((bf16[8,8,64,128]{3,2,1,0:T(8,128)(2,1)}), bf16[8,8,64,128]{3,2,1,0:T(8,128)(2,1)S(1)}, u32[]{:S(2)}, u32[]{:S(2)}) async-start(bf16[8,8,64,128]{3,2,1,0:T(8,128)(2,1)} %broadcast_in_dim.11), calls=%async_computation | async-start | bytes 2097152 | tf_op jit(solution)/shard_map/all_to_all | solution.py:318
  9.0 8.3 %collective-permute-start.1 = (bf16[3,8,32]{2,1,0:T(8,128)(2,1)}, bf16[3,8,32]{2,1,0:T(8,128)(2,1)S(1)}, u32[]{:S(2)}, u32[]{:S(2)}) collective-permute-start(bf16[3,8,32]{2,1,0:T(8,128)(2,1)} %bitcast.15), channel_id=1, source_target_pairs={{8,0},{16,8},{24,16},{32,24},{40,32},{48,40},{56,48},{64,56},{72,6... | collective-permute-start | bytes 4616 | tf_op jit(solution)/shard_map/ppermute | solution.py:306
  15.7 11.4 %collective-permute-start = (bf16[3,8,32]{2,1,0:T(8,128)(2,1)}, bf16[3,8,32]{2,1,0:T(8,128)(2,1)S(1)}, u32[]{:S(2)}, u32[]{:S(2)}) collective-permute-start(bf16[3,8,32]{2,1,0:T(8,128)(2,1)} %bitcast.16), channel_id=1, source_target_pairs={{248,0},{0,8},{8,16},{16,24},{24,32},{32,40},{40,48},{48,56},{56,6... | collective-permute-start | bytes 4616 | tf_op jit(solution)/shard_map/ppermute | solution.py:306
  27.1 0.6 copy-start.6
  27.7 49.3 %collective-permute-start.7 = (bf16[8,8,64,128]{3,2,1,0:T(8,128)(2,1)S(1)}, bf16[8,8,64,128]{3,2,1,0:T(8,128)(2,1)S(1)}, u32[]{:S(2)}, u32[]{:S(2)}) collective-permute-start(bf16[8,8,64,128]{3,2,1,0:T(8,128)(2,1)S(1)} %all-to-all-done.own_ref), channel_id=1, source_target_pairs={{8,0},{16,8},{24,16},{32,24},{40,32},{48,40},{56,48},{64,56},{72,6... | collective-permute-start | bytes 3145736 | tf_op jit(solution)/shard_map/ppermute | solution.py:306
  28.1 48.9 %collective-permute-start.6 = (bf16[8,8,64,128]{3,2,1,0:T(8,128)(2,1)S(1)}, bf16[8,8,64,128]{3,2,1,0:T(8,128)(2,1)S(1)}, u32[]{:S(2)}, u32[]{:S(2)}) collective-permute-start(bf16[8,8,64,128]{3,2,1,0:T(8,128)(2,1)S(1)} %all-to-all-done.own_ref), channel_id=1, source_target_pairs={{248,0},{0,8},{8,16},{16,24},{24,32},{32,40},{40,48},{48,56},{56,6... | collective-permute-start | bytes 3145736 | tf_op jit(solution)/shard_map/ppermute | solution.py:306
  28.2 32.8 %collective-permute-start.2 = (bf16[8,64,128]{2,1,0:T(8,128)(2,1)}, bf16[8,64,128]{2,1,0:T(8,128)(2,1)}, u32[]{:S(2)}, u32[]{:S(2)}) collective-permute-start(bf16[8,64,128]{2,1,0:T(8,128)(2,1)} %own_ref.1), channel_id=1, source_target_pairs={{248,0},{0,8},{8,16},{16,24},{24,32},{32,40},{40,48},{48,56},{56,6... | collective-permute-start | bytes 393224 | tf_op jit(solution)/shard_map/ppermute | solution.py:306
  28.2 32.8 %collective-permute-start.3 = (bf16[8,64,128]{2,1,0:T(8,128)(2,1)}, bf16[8,64,128]{2,1,0:T(8,128)(2,1)}, u32[]{:S(2)}, u32[]{:S(2)}) collective-permute-start(bf16[8,64,128]{2,1,0:T(8,128)(2,1)} %own_ref.1), channel_id=1, source_target_pairs={{8,0},{16,8},{24,16},{32,24},{40,32},{48,40},{56,48},{64,56},{72,6... | collective-permute-start | bytes 393224 | tf_op jit(solution)/shard_map/ppermute | solution.py:306
  34.9 0.7 copy-start.5
  35.6 0.7 copy-start.7
  39.1 0.6 copy-start.1
  39.7 0.6 copy-start.4
  40.3 20.7 %all-to-all-start.1 = ((f32[32,1,128]{2,1,0:T(1,128)}), f32[32,1,128]{2,1,0:T(1,128)}, u32[]{:S(2)}, u32[]{:S(2)}) async-start(f32[32,1,128]{2,1,0:T(1,128)} %bitcast.14), calls=%async_computation.1 | async-start | bytes 32768 | tf_op jit(solution)/shard_map/all_to_all | solution.py:340
  61.0 0.9 copy-start
  61.9 0.9 copy-start.2
  67.4 4.7 %collective-permute-start.5 = (bf16[4,128,128]{2,1,0:T(8,128)(2,1)S(1)}, bf16[4,128,128]{2,1,0:T(8,128)(2,1)S(1)}, u32[]{:S(2)}, u32[]{:S(2)}) collective-permute-start(bf16[4,128,128]{2,1,0:T(8,128)(2,1)S(1)} %get-tuple-element.26.own_ref), channel_id=1, source_target_pairs={{8,0},{16,8},{24,16},{32,24},{40,32},{48,40},{56,48},{64,56},{72,6... | collective-permute-start | bytes 393224 | tf_op jit(solution)/shard_map/ppermute | solution.py:306
  68.3 8.7 %collective-permute-start.4 = (bf16[4,128,128]{2,1,0:T(8,128)(2,1)S(1)}, bf16[4,128,128]{2,1,0:T(8,128)(2,1)S(1)}, u32[]{:S(2)}, u32[]{:S(2)}) collective-permute-start(bf16[4,128,128]{2,1,0:T(8,128)(2,1)S(1)} %get-tuple-element.26.own_ref), channel_id=1, source_target_pairs={{248,0},{0,8},{8,16},{16,24},{24,32},{32,40},{40,48},{48,56},{56,6... | collective-permute-start | bytes 393224 | tf_op jit(solution)/shard_map/ppermute | solution.py:306
  77.0 0.9 copy-start.3
  96.9 3.0 %collective-permute-start.8 = (f32[8,128]{1,0:T(8,128)S(1)}, f32[8,128]{1,0:T(8,128)S(1)}, u32[]{:S(2)}, u32[]{:S(2)}) collective-permute-start(f32[8,128]{1,0:T(8,128)S(1)} %get-tuple-element.32), channel_id=1, source_target_pairs={{8,0},{16,8},{24,16},{32,24},{40,32},{48,40},{56,48},{64,56},{72,6... | collective-permute-start | bytes 12296 | tf_op jit(solution)/shard_map/ppermute | solution.py:306
  97.0 7.3 %collective-permute-start.9 = (f32[8,128]{1,0:T(8,128)S(1)}, f32[8,128]{1,0:T(8,128)S(1)}, u32[]{:S(2)}, u32[]{:S(2)}) collective-permute-start(f32[8,128]{1,0:T(8,128)S(1)} %get-tuple-element.33), channel_id=1, source_target_pairs={{248,0},{0,8},{8,16},{16,24},{24,32},{32,40},{40,48},{48,56},{56,6... | collective-permute-start | bytes 12296 | tf_op jit(solution)/shard_map/ppermute | solution.py:306

commit v3 on v2

--- a/solution.py
+++ b/solution.py
@@ -30,6 +30,9 @@
 BF16 = jnp.bfloat16
 WHOLE = pl.BlockSpec()
 SMEM = pl.BlockSpec(memory_space=pltpu.SMEM)
+HBM = pl.BlockSpec(memory_space=pltpu.MemorySpace.HBM)
+HEAVY = pl.CostEstimate(flops=0, transcendentals=0, bytes_accessed=60_000_000)
+LIGHT = pl.CostEstimate(flops=0, transcendentals=0, bytes_accessed=0)
 
 
 def params(mebibytes):
@@ -84,12 +87,20 @@
 
 
 def spectral_kernel(
-    slot_ref, before_ref, own_ref, after_ref, near_ref, row_ref, peak_ref, shift_ref
+    slot_ref, before_ref, own_ref, after_ref, near_out, row_out, peak_out,
+    coord_ref, near_ref, row_ref, peak_ref, shift_ref, in_sem, out_sem,
 ):
+    copies = [
+        pltpu.make_async_copy(ref, coord_ref.at[part], in_sem.at[part])
+        for part, ref in enumerate((before_ref, own_ref, after_ref))
+    ]
+    for copy in copies:
+        copy.start()
     fill_shifts(shift_ref)
-    for part, ref in enumerate((before_ref, own_ref, after_ref)):
+    for part in range(3):
+        copies[part].wait()
         for x in range(3):
-            coords = ref[x].astype(F32)
+            coords = coord_ref[part, x].astype(F32)
             wide = jnp.concatenate([coords] * 4, axis=1)
             for n in range(8):
                 near_ref[8 * part + n, x : x + 1, :] = wide[n : n + 1, :]
@@ -98,6 +109,12 @@
                 for c in range(8):
                     row_ref[c, x] = jnp.broadcast_to(upright[0:32, c : c + 1], (32, 128))
     near_ref[DEAD] = jnp.full((8, 128), FAR, F32)
+    kept = [
+        pltpu.make_async_copy(near_ref, near_out, out_sem.at[0]),
+        pltpu.make_async_copy(row_ref, row_out, out_sem.at[1]),
+    ]
+    for copy in kept:
+        copy.start()
     lane = lanes()
 
     def one_cluster(c, peak):
@@ -123,6 +140,11 @@
 
     peak = lax.fori_loop(0, 8, one_cluster, jnp.zeros((32, 1), F32))
     peak_ref[...] = jnp.broadcast_to(jnp.max(peak), peak_ref.shape)
+    copy = pltpu.make_async_copy(peak_ref, peak_out, out_sem.at[2])
+    copy.start()
+    copy.wait()
+    for copy in kept:
+        copy.wait()
 
 
 def gather_operand(slot_ref, source_ref, target_ref, c):
@@ -134,19 +156,34 @@
 
 
 def first_kernel(
-    slot_ref, peak_ref, near_ref, row_ref, before_ref, own_ref, after_ref,
-    scaled_ref, operand_ref, turned_ref, one_ref, half_ref, probe_ref, shift_ref,
+    slot_ref, peak_in, near_in, row_in, before_ref, own_ref, after_ref,
+    scaled_ref, operand_ref, turned_ref, one_ref, half_ref,
+    peak_ref, near_ref, row_ref, flat_ref, probe_ref, shift_ref, sem,
 ):
+    pieces = [
+        pltpu.make_async_copy(ref, flat_ref.at[part], sem.at[part])
+        for part, ref in enumerate((before_ref, own_ref, after_ref))
+    ]
+    copies = [
+        pltpu.make_async_copy(peak_in, peak_ref, sem.at[3]),
+        pltpu.make_async_copy(near_in, near_ref, sem.at[4]),
+        pltpu.make_async_copy(row_in, row_ref, sem.at[5]),
+    ]
+    for copy in pieces + copies:
+        copy.start()
     fill_shifts(shift_ref)
     lane = lanes()
-    inverse_peak = 1.0 / jnp.max(peak_ref[...])
-    for part, ref in enumerate((before_ref, own_ref, after_ref)):
+    for part in range(3):
+        pieces[part].wait()
         for c in range(8):
-            turned = ref[c].astype(F32).T
+            turned = flat_ref[part, c].astype(F32).T
             if part == 1:
                 turned_ref[c] = turned
             probe_ref[8 * part + c] = turned.astype(BF16)
     probe_ref[DEAD] = jnp.zeros((128, 64), BF16)
+    for copy in copies:
+        copy.wait()
+    inverse_peak = 1.0 / jnp.max(peak_ref[...])
 
     def one_pair(pair, carry):
         for side in range(2):
@@ -188,9 +225,16 @@
 
 
 def second_kernel(
-    slot_ref, near_ref, row_ref, scaled_ref, operand_ref, turned_ref, one_ref,
-    before_ref, own_ref, after_ref, send_ref, half_ref, gathered_ref, pull_ref, shift_ref,
+    slot_ref, near_in, row_in, scaled_ref, operand_ref, turned_ref, one_ref,
+    before_ref, own_ref, after_ref, send_ref,
+    near_ref, row_ref, half_ref, gathered_ref, pull_ref, shift_ref, sem,
 ):
+    copies = [
+        pltpu.make_async_copy(near_in, near_ref, sem.at[0]),
+        pltpu.make_async_copy(row_in, row_ref, sem.at[1]),
+    ]
+    for copy in copies:
+        copy.start()
     fill_shifts(shift_ref)
     lane = lanes()
     for part, ref in enumerate((before_ref, own_ref, after_ref)):
@@ -199,6 +243,8 @@
             half_ref[8 * part + pair + 4] = ref[pair, :, 64:128]
     half_ref[DEAD] = jnp.zeros((128, 64), BF16)
     pull_ref[...] = jnp.zeros_like(pull_ref)
+    for copy in copies:
+        copy.wait()
     on_row = lax.broadcasted_iota(jnp.int32, (32, 128), 0) == lax.broadcasted_iota(
         jnp.int32, (32, 128), 1
     )
@@ -317,9 +363,6 @@
     spread = jnp.broadcast_to(probes[None], (8,) + probes.shape)
     all_own = lax.all_to_all(spread, "probe", 0, 0, tiled=True).reshape(8, 8, 64, 128)
 
-    pos_before, pos_after, all_own = lax.optimization_barrier((pos_before, pos_after, all_own))
-    all_before, all_after = both(all_own)
-
     present = neighbours >= 0
     slot = (neighbours // 8 - space_rank + 1) % space_count * 8 + neighbours % 8
     slot = jnp.pad(jnp.where(present, slot, DEAD), ((0, 0), (0, 1)), constant_values=DEAD)
@@ -331,13 +374,27 @@
             jax.ShapeDtypeStruct((8, 3, 32, 128), F32),
             jax.ShapeDtypeStruct((space_count, 128), F32),
         ),
-        in_specs=[SMEM] + [WHOLE] * 3,
-        out_specs=(WHOLE,) * 3,
-        scratch_shapes=[pltpu.VMEM((4, 8, 128), F32)],
+        in_specs=[SMEM] + [HBM] * 3,
+        out_specs=(HBM,) * 3,
+        scratch_shapes=[
+            pltpu.VMEM((3, 3, 8, 32), BF16),
+            pltpu.VMEM((NEAR + 1, 8, 128), F32),
+            pltpu.VMEM((8, 3, 32, 128), F32),
+            pltpu.VMEM((space_count, 128), F32),
+            pltpu.VMEM((4, 8, 128), F32),
+            pltpu.SemaphoreType.DMA((3,)),
+            pltpu.SemaphoreType.DMA((3,)),
+        ],
+        cost_estimate=HEAVY,
         compiler_params=params(4),
         name="spectral",
     )(slot, pos_before, pos_own, pos_after)
+    peak, all_own, probe_before, probe_after = lax.optimization_barrier(
+        (peak, all_own, probe_before, probe_after)
+    )
     peaks = lax.all_to_all(peak, "space", 0, 0, tiled=True)
+    peaks, all_own = lax.optimization_barrier((peaks, all_own))
+    all_before, all_after = both(all_own)
 
     scaled, operand, turned, one, half = pl.pallas_call(
         first_kernel,
@@ -348,31 +405,42 @@
             jax.ShapeDtypeStruct((8, 128, 64), F32),
             jax.ShapeDtypeStruct((4, 128, 128), BF16),
         ),
-        in_specs=[SMEM] + [WHOLE] * 6,
+        in_specs=[SMEM] + [HBM] * 6,
         out_specs=(WHOLE,) * 5,
-        scratch_shapes=[pltpu.VMEM((NEAR + 1, 128, 64), BF16), pltpu.VMEM((4, 8, 128), F32)],
+        scratch_shapes=[
+            pltpu.VMEM((space_count, 128), F32),
+            pltpu.VMEM((NEAR + 1, 8, 128), F32),
+            pltpu.VMEM((8, 3, 32, 128), F32),
+            pltpu.VMEM((3, 8, 64, 128), BF16),
+            pltpu.VMEM((NEAR + 1, 128, 64), BF16),
+            pltpu.VMEM((4, 8, 128), F32),
+            pltpu.SemaphoreType.DMA((6,)),
+        ],
+        cost_estimate=LIGHT,
         compiler_params=params(16),
         name="first",
     )(slot, peaks, near, rows, probe_before, probes, probe_after)
     half_before, half_after = both(half)
-    half_before, half_after, all_before, all_after = lax.optimization_barrier(
-        (half_before, half_after, all_before, all_after)
-    )
 
     send = pl.pallas_call(
         second_kernel,
         out_shape=jax.ShapeDtypeStruct((8, 88, 128), F32),
-        in_specs=[SMEM] + [WHOLE] * 9,
+        in_specs=[SMEM, HBM, HBM] + [WHOLE] * 7,
         out_specs=WHOLE,
+        cost_estimate=LIGHT,
         scratch_shapes=[
+            pltpu.VMEM((NEAR + 1, 8, 128), F32),
+            pltpu.VMEM((8, 3, 32, 128), F32),
             pltpu.VMEM((NEAR + 1, 128, 64), BF16),
             pltpu.VMEM((2, 2048, 64), BF16),
             pltpu.VMEM((NEAR + 1, 3, 8, 128), F32),
             pltpu.VMEM((4, 8, 128), F32),
+            pltpu.SemaphoreType.DMA((2,)),
         ],
         compiler_params=params(16),
         name="second",
     )(slot, near, rows, scaled, operand, turned, one, half_before, half, half_after)
+    send, all_before, all_after = lax.optimization_barrier((send, all_before, all_after))
     received = lax.all_to_all(send, "probe", 0, 0, tiled=True)
     force = jnp.sum(received[:, 64:88], axis=0)
     from_after = around(force[0:8], space_count, -1)

time: 105 us -> 109 us (1.038)
  waiting for transfers between devices: 40.8 us -> 25.3 us
  blocking collectives: 12.3 us -> 23.8 us
  starting transfers between devices: 25.3 us -> 35.4 us
  local copies, waits for them, and re-layouts: 8.14 us -> 3.82 us
  Pallas kernels: 16.3 us -> 18.1 us
    ppermute x10, waiting for transfers between devices: 40.8 us -> 25.3 us  [around(): lax.ppermute(block, 'space', [((i - distance) % size, i) for i in range(s...]
    ppermute x10, starting transfers between devices: 14.6 us -> 29.2 us  [around(): lax.ppermute(block, 'space', [((i - distance) % size, i) for i in range(s...]
    all_to_all x0 -> x1, blocking collectives: none -> 12.8 us  [per_device(): peaks = lax.all_to_all(peak, 'space', 0, 0, tiled=True)]
    all_to_all x1 -> x0, starting transfers between devices: 4.48 us -> none  [per_device(): peaks = lax.all_to_all(peak, 'space', 0, 0, tiled=True)]
    unnamed x16 -> x4, local copies, waits for them, and re-layouts: 5.9 us -> 1.6 us
    all_to_all x1, blocking collectives: 12.3 us -> 11 us  [per_device(): received = lax.all_to_all(send, 'probe', 0, 0, tiled=True)]
  transfers between devices with their start and end apart: 12 -> 11, of which waited for: 6 -> 3; matrix products, arithmetic and copies ran while one was open for 1% -> 1% of each run, Pallas kernels for 9% -> 17%
where the time goes in v3:
time: 109 us; the launch traced here: 108 us
  starting transfers between devices  35.4 us (32%)
  waiting for transfers between devices  25.3 us (23%)
  blocking collectives  23.8 us (22%)
  Pallas kernels  18.1 us (17%)
  local copies, waits for them, and re-layouts  3.82 us (4%)
  other arithmetic  1.33 us (1%)
    ppermute x10, starting transfers between devices, around(): lax.ppermute(block, 'space', [((i - distance) % size, i) for i in range(s...  29.2 us
    ppermute x10, waiting for transfers between devices, around(): lax.ppermute(block, 'space', [((i - distance) % size, i) for i in range(s...  25.3 us
    all_to_all x1, blocking collectives, per_device(): peaks = lax.all_to_all(peak, 'space', 0, 0, tiled=True)  12.8 us
    all_to_all x1, blocking collectives, per_device(): received = lax.all_to_all(send, 'probe', 0, 0, tiled=True)  11 us
    pallas_call x1, Pallas kernels, per_device(): pl.pallas_call(second_kernel, out_shape=jax.ShapeDtypeStruct((8, 88, 128)...  7 us
    all_to_all x1, starting transfers between devices, per_device(): lax.all_to_all(spread, 'probe', 0, 0, tiled=True).reshape(8, 8, 64, 128)  6.18 us
    pallas_call x1, Pallas kernels, per_device(): pl.pallas_call(first_kernel, out_shape=(jax.ShapeDtypeStruct((8, 128, 204...  5.38 us
    pallas_call x1, Pallas kernels, per_device(): pl.pallas_call(spectral_kernel, out_shape=(jax.ShapeDtypeStruct((NEAR + 1...  3.32 us
  transfers between devices with their start and end apart: 11, of which 3 were waited for; matrix products, arithmetic and copies ran while one was open for 1% of the time, Pallas kernels for 17%

profile of v3, /device:TPU:2, one launch (start us, length us, event | category | flops | bytes accessed | tf_op | source)
XLA Modules:
  0.0 108.4 jit_solution(7867051618443540170)
XLA Ops:
  0.6 2.1 %broadcast_in_dim.11 = bf16[8,8,64,128]{3,2,1,0:T(8,128)(2,1)} broadcast(bf16[8,64,128]{2,1,0:T(8,128)(2,1)} %own_ref.1), dimensions={1,2,3} | broadcast | bytes 1179648 | tf_op jit(solution)/shard_map/broadcast_in_dim | solution.py:363
  2.8 6.2 %all-to-all-start = ((bf16[8,8,64,128]{3,2,1,0:T(8,128)(2,1)}), bf16[8,8,64,128]{3,2,1,0:T(8,128)(2,1)S(1)}, u32[]{:S(2)}, u32[]{:S(2)}) async-start(bf16[8,8,64,128]{3,2,1,0:T(8,128)(2,1)} %broadcast_in_dim.11), calls=%async_computation | async-start | bytes 2097152 | tf_op jit(solution)/shard_map/all_to_all | solution.py:364
  9.0 0.0 collective-permute-start
  9.0 6.7 %collective-permute-start.1 = (bf16[3,8,32]{2,1,0:T(8,128)(2,1)}, bf16[3,8,32]{2,1,0:T(8,128)(2,1)S(1)}, u32[]{:S(2)}, u32[]{:S(2)}) collective-permute-start(bf16[3,8,32]{2,1,0:T(8,128)(2,1)} %bitcast.17), channel_id=1, source_target_pairs={{8,0},{16,8},{24,16},{32,24},{40,32},{48,40},{56,48},{64,56},{72,6... | collective-permute-start | bytes 4616 | tf_op jit(solution)/shard_map/ppermute | solution.py:352
  15.7 0.0 collective-permute-start.2
  15.7 6.0 %collective-permute-start.3 = (bf16[8,64,128]{2,1,0:T(8,128)(2,1)}, bf16[8,64,128]{2,1,0:T(8,128)(2,1)S(1)}, u32[]{:S(2)}, u32[]{:S(2)}) collective-permute-start(bf16[8,64,128]{2,1,0:T(8,128)(2,1)} %own_ref.1), channel_id=1, source_target_pairs={{8,0},{16,8},{24,16},{32,24},{40,32},{48,40},{56,48},{64,56},{72,6... | collective-permute-start | bytes 393224 | tf_op jit(solution)/shard_map/ppermute | solution.py:352
  21.7 0.7 fusion.5
  22.4 6.1 %collective-permute-done.before_ref = bf16[3,8,32]{2,1,0:T(8,128)(2,1)S(1)} collective-permute-done((bf16[3,8,32]{2,1,0:T(8,128)(2,1)}, bf16[3,8,32]{2,1,0:T(8,128)(2,1)S(1)}, u32[]{:S(2)}, u32[]{:S(2)}) %collective-permute-start) | collective-permute-done | bytes 1568 | tf_op jit(solution)/shard_map/ppermute | solution.py:352
  28.5 0.0 collective-permute-done.1.after_ref
  28.5 0.0 copy-start.1
  28.5 0.7 copy-done.1
  29.2 3.3 %spectral.1 = (f32[25,8,128]{2,1,0:T(8,128)S(1)}, f32[8,3,32,128]{3,2,1,0:T(8,128)S(1)}, f32[32,128]{1,0:T(8,128)S(1)}) custom-call(s32[8,16]{1,0:T(8,128)S(1)} %pad.4.slot_ref, bf16[3,8,32]{2,1,0:T(8,128)(2,1)S(1)} %collective-permute-done.before_ref, bf16[3,8,32]{2,1,0:T(8,128)(2,1)S(1)} %bitcast.18, bf16[3,8,32]{2,1,0:T(8,128)(2,1)S(1)} %collective-permute-done.1.after_ref), custom_call_target="tpu_custom_call" | custom-call | bytes 60000000 | tf_op jit(solution)/shard_map/spectral/pallas_call | solution.py:370
  32.5 0.0 collective-permute-done.2.before_ref
  32.5 0.0 collective-permute-done.3.after_ref
  32.6 0.0 all-to-all-done.own_ref
  32.6 12.8 %all_to_all.22 = f32[32,1,128]{2,1,0:T(1,128)S(1)} all-to-all(f32[32,1,128]{2,1,0:T(1,128)S(1)} %bitcast.15), channel_id=1, replica_groups=mesh['space'=32,'probe'=8] {'space'}, dimensions={0} | all-to-all | bytes 32768 | tf_op jit(solution)/shard_map/all_to_all | solution.py:395
  45.4 0.0 collective-permute-start.6
  45.4 6.0 %collective-permute-start.7 = (bf16[8,8,64,128]{3,2,1,0:T(8,128)(2,1)S(1)}, bf16[8,8,64,128]{3,2,1,0:T(8,128)(2,1)S(1)}, u32[]{:S(2)}, u32[]{:S(2)}) collective-permute-start(bf16[8,8,64,128]{3,2,1,0:T(8,128)(2,1)S(1)} %all-to-all-done.own_ref), channel_id=1, source_target_pairs={{8,0},{16,8},{24,16},{32,24},{40,32},{48,40},{56,48},{64,56},{72,6... | collective-permute-start | bytes 3145736 | tf_op jit(solution)/shard_map/ppermute | solution.py:352
  51.3 0.0 copy-start
  51.3 0.9 copy-done
  52.2 5.4 %first.1 = (bf16[8,128,2048]{2,1,0:T(8,128)(2,1)S(1)}, bf16[8,2048,64]{2,1,0:T(8,128)(2,1)S(1)}, f32[8,128,64]{2,1,0:T(8,128)S(1)}, f32[8,128,64]{2,1,0:T(8,128)S(1)}, bf16[4,128,128]{2,1,0:T(8,128)(2,1)S(1)}) custom-call(s32[8,16]{1,0:T(8,128)S(1)} %pad.4.slot_ref, f32[32,128]{1,0:T(8,128)S(1)} %bitcast.14, f32[25,8,128]{2,1,0:T(8,128)S(1)} %get-tuple-element.19.near_in, ...), custom_call_target="tpu_custom_call" | custom-call | tf_op jit(solution)/shard_map/first/pallas_call | solution.py:399
  57.6 0.1 collective-permute-start.4
  57.7 6.0 %collective-permute-start.5 = (bf16[4,128,128]{2,1,0:T(8,128)(2,1)S(1)}, bf16[4,128,128]{2,1,0:T(8,128)(2,1)S(1)}, u32[]{:S(2)}, u32[]{:S(2)}) collective-permute-start(bf16[4,128,128]{2,1,0:T(8,128)(2,1)S(1)} %get-tuple-element.31.own_ref), channel_id=1, source_target_pairs={{8,0},{16,8},{24,16},{32,24},{40,32},{48,40},{56,48},{64,56},{72,6... | collective-permute-start | bytes 393224 | tf_op jit(solution)/shard_map/ppermute | solution.py:352
  63.7 14.3 %collective-permute-done.4.before_ref = bf16[4,128,128]{2,1,0:T(8,128)(2,1)S(1)} collective-permute-done((bf16[4,128,128]{2,1,0:T(8,128)(2,1)S(1)}, bf16[4,128,128]{2,1,0:T(8,128)(2,1)S(1)}, u32[]{:S(2)}, u32[]{:S(2)}) %collective-permute-start.4) | collective-permute-done | bytes 131104 | tf_op jit(solution)/shard_map/ppermute | solution.py:352
  77.9 0.0 collective-permute-done.5.after_ref
  77.9 7.0 %second.1 = f32[8,88,128]{2,1,0:T(8,128)S(1)} custom-call(s32[8,16]{1,0:T(8,128)S(1)} %pad.4.slot_ref, f32[25,8,128]{2,1,0:T(8,128)S(1)} %get-tuple-element.19.near_in, f32[8,3,32,128]{3,2,1,0:T(8,128)S(1)} %get-tuple-element.20.row_in, bf16[8,128,2048]{2,1,0:T(8,128)(2,1)S(1)} %get-tuple-element.27.scaled_ref, ...), custom_call_target="tpu_custom_call" | custom-call | tf_op jit(solution)/shard_map/second/pallas_call | solution.py:425
  84.9 0.0 collective-permute-done.6.before_ref
  84.9 0.0 collective-permute-done.7.after_ref
  85.0 11.0 %all_to_all.23.received_ref = f32[8,88,128]{2,1,0:T(8,128)S(1)} all-to-all(f32[8,88,128]{2,1,0:T(8,128)S(1)} %second.1), channel_id=1, replica_groups=mesh['space'=32,'probe'=8] {'probe'}, dimensions={0} | all-to-all | bytes 720896 | tf_op jit(solution)/shard_map/all_to_all | solution.py:444
  96.0 4.5 %collective-permute-start.8 = (f32[8,128]{1,0:T(8,128)S(1)}, f32[8,128]{1,0:T(8,128)S(1)}, u32[]{:S(2)}, u32[]{:S(2)}) collective-permute-start(f32[8,128]{1,0:T(8,128)S(1)} %get-tuple-element.36), channel_id=1, source_target_pairs={{8,0},{16,8},{24,16},{32,24},{40,32},{48,40},{56,48},{64,56},{72,6... | collective-permute-start | bytes 12296 | tf_op jit(solution)/shard_map/ppermute | solution.py:352
  100.5 0.0 collective-permute-start.9
  100.5 2.4 %sample.1 = bf16[16,15,8,128]{3,2,1,0:T(8,128)(2,1)} custom-call(s32[8,16]{1,0:T(8,128)S(1)} %pad.4.slot_ref, f32[8,88,128]{2,1,0:T(8,128)S(1)} %all_to_all.23.received_ref, bf16[8,8,64,128]{3,2,1,0:T(8,128)(2,1)S(1)} %collective-permute-done.6.before_ref, bf16[8,8,64,128]{3,2,1,0:T(8,128)(2,1)S(1)} %all-to-all-done.own_ref, ...), custom_call_target="tpu_custom_call" | custom-call | tf_op jit(solution)/shard_map/sample/pallas_call | solution.py:449
  102.8 0.0 collective-permute-done.8
  102.8 4.9 %collective-permute-done.9 = f32[8,128]{1,0:T(8,128)S(1)} collective-permute-done((f32[8,128]{1,0:T(8,128)S(1)}, f32[8,128]{1,0:T(8,128)S(1)}, u32[]{:S(2)}, u32[]{:S(2)}) %collective-permute-start.9) | collective-permute-done | bytes 4128 | tf_op jit(solution)/shard_map/ppermute | solution.py:352
  107.7 0.1 slice_bitcast_fusion.2
  107.8 0.6 maximum_bitcast_fusion
  (4 shorter events, 0.0 us)
Async XLA Ops:
  2.8 29.8 %all-to-all-start = ((bf16[8,8,64,128]{3,2,1,0:T(8,128)(2,1)}), bf16[8,8,64,128]{3,2,1,0:T(8,128)(2,1)S(1)}, u32[]{:S(2)}, u32[]{:S(2)}) async-start(bf16[8,8,64,128]{3,2,1,0:T(8,128)(2,1)} %broadcast_in_dim.11), calls=%async_computation | async-start | bytes 2097152 | tf_op jit(solution)/shard_map/all_to_all | solution.py:364
  9.0 19.5 %collective-permute-start = (bf16[3,8,32]{2,1,0:T(8,128)(2,1)}, bf16[3,8,32]{2,1,0:T(8,128)(2,1)S(1)}, u32[]{:S(2)}, u32[]{:S(2)}) collective-permute-start(bf16[3,8,32]{2,1,0:T(8,128)(2,1)} %bitcast.16), channel_id=1, source_target_pairs={{248,0},{0,8},{8,16},{16,24},{24,32},{32,40},{40,48},{48,56},{56,6... | collective-permute-start | bytes 4616 | tf_op jit(solution)/shard_map/ppermute | solution.py:352
  9.0 19.5 %collective-permute-start.1 = (bf16[3,8,32]{2,1,0:T(8,128)(2,1)}, bf16[3,8,32]{2,1,0:T(8,128)(2,1)S(1)}, u32[]{:S(2)}, u32[]{:S(2)}) collective-permute-start(bf16[3,8,32]{2,1,0:T(8,128)(2,1)} %bitcast.17), channel_id=1, source_target_pairs={{8,0},{16,8},{24,16},{32,24},{40,32},{48,40},{56,48},{64,56},{72,6... | collective-permute-start | bytes 4616 | tf_op jit(solution)/shard_map/ppermute | solution.py:352
  15.7 16.8 %collective-permute-start.2 = (bf16[8,64,128]{2,1,0:T(8,128)(2,1)}, bf16[8,64,128]{2,1,0:T(8,128)(2,1)S(1)}, u32[]{:S(2)}, u32[]{:S(2)}) collective-permute-start(bf16[8,64,128]{2,1,0:T(8,128)(2,1)} %own_ref.1), channel_id=1, source_target_pairs={{248,0},{0,8},{8,16},{16,24},{24,32},{32,40},{40,48},{48,56},{56,6... | collective-permute-start | bytes 393224 | tf_op jit(solution)/shard_map/ppermute | solution.py:352
  15.7 16.9 %collective-permute-start.3 = (bf16[8,64,128]{2,1,0:T(8,128)(2,1)}, bf16[8,64,128]{2,1,0:T(8,128)(2,1)S(1)}, u32[]{:S(2)}, u32[]{:S(2)}) collective-permute-start(bf16[8,64,128]{2,1,0:T(8,128)(2,1)} %own_ref.1), channel_id=1, source_target_pairs={{8,0},{16,8},{24,16},{32,24},{40,32},{48,40},{56,48},{64,56},{72,6... | collective-permute-start | bytes 393224 | tf_op jit(solution)/shard_map/ppermute | solution.py:352
  28.5 0.7 copy-start.1
  45.4 39.6 %collective-permute-start.6 = (bf16[8,8,64,128]{3,2,1,0:T(8,128)(2,1)S(1)}, bf16[8,8,64,128]{3,2,1,0:T(8,128)(2,1)S(1)}, u32[]{:S(2)}, u32[]{:S(2)}) collective-permute-start(bf16[8,8,64,128]{3,2,1,0:T(8,128)(2,1)S(1)} %all-to-all-done.own_ref), channel_id=1, source_target_pairs={{248,0},{0,8},{8,16},{16,24},{24,32},{32,40},{40,48},{48,56},{56,6... | collective-permute-start | bytes 3145736 | tf_op jit(solution)/shard_map/ppermute | solution.py:352
  45.4 39.6 %collective-permute-start.7 = (bf16[8,8,64,128]{3,2,1,0:T(8,128)(2,1)S(1)}, bf16[8,8,64,128]{3,2,1,0:T(8,128)(2,1)S(1)}, u32[]{:S(2)}, u32[]{:S(2)}) collective-permute-start(bf16[8,8,64,128]{3,2,1,0:T(8,128)(2,1)S(1)} %all-to-all-done.own_ref), channel_id=1, source_target_pairs={{8,0},{16,8},{24,16},{32,24},{40,32},{48,40},{56,48},{64,56},{72,6... | collective-permute-start | bytes 3145736 | tf_op jit(solution)/shard_map/ppermute | solution.py:352
  51.3 0.9 copy-start
  57.6 20.3 %collective-permute-start.4 = (bf16[4,128,128]{2,1,0:T(8,128)(2,1)S(1)}, bf16[4,128,128]{2,1,0:T(8,128)(2,1)S(1)}, u32[]{:S(2)}, u32[]{:S(2)}) collective-permute-start(bf16[4,128,128]{2,1,0:T(8,128)(2,1)S(1)} %get-tuple-element.31.own_ref), channel_id=1, source_target_pairs={{248,0},{0,8},{8,16},{16,24},{24,32},{32,40},{40,48},{48,56},{56,6... | collective-permute-start | bytes 393224 | tf_op jit(solution)/shard_map/ppermute | solution.py:352
  57.7 20.2 %collective-permute-start.5 = (bf16[4,128,128]{2,1,0:T(8,128)(2,1)S(1)}, bf16[4,128,128]{2,1,0:T(8,128)(2,1)S(1)}, u32[]{:S(2)}, u32[]{:S(2)}) collective-permute-start(bf16[4,128,128]{2,1,0:T(8,128)(2,1)S(1)} %get-tuple-element.31.own_ref), channel_id=1, source_target_pairs={{8,0},{16,8},{24,16},{32,24},{40,32},{48,40},{56,48},{64,56},{72,6... | collective-permute-start | bytes 393224 | tf_op jit(solution)/shard_map/ppermute | solution.py:352
  96.0 6.9 %collective-permute-start.8 = (f32[8,128]{1,0:T(8,128)S(1)}, f32[8,128]{1,0:T(8,128)S(1)}, u32[]{:S(2)}, u32[]{:S(2)}) collective-permute-start(f32[8,128]{1,0:T(8,128)S(1)} %get-tuple-element.36), channel_id=1, source_target_pairs={{8,0},{16,8},{24,16},{32,24},{40,32},{48,40},{56,48},{64,56},{72,6... | collective-permute-start | bytes 12296 | tf_op jit(solution)/shard_map/ppermute | solution.py:352
  100.5 7.3 %collective-permute-start.9 = (f32[8,128]{1,0:T(8,128)S(1)}, f32[8,128]{1,0:T(8,128)S(1)}, u32[]{:S(2)}, u32[]{:S(2)}) collective-permute-start(f32[8,128]{1,0:T(8,128)S(1)} %get-tuple-element.37), channel_id=1, source_target_pairs={{248,0},{0,8},{8,16},{16,24},{24,32},{32,40},{40,48},{48,56},{56,6... | collective-permute-start | bytes 12296 | tf_op jit(solution)/shard_map/ppermute | solution.py:352

commit v4 on v3

--- a/solution.py
+++ b/solution.py
@@ -91,7 +91,7 @@
     coord_ref, near_ref, row_ref, peak_ref, shift_ref, in_sem, out_sem,
 ):
     copies = [
-        pltpu.make_async_copy(ref, coord_ref.at[part], in_sem.at[part])
+        pltpu.make_async_copy(ref.at[512:536], coord_ref.at[part], in_sem.at[part])
         for part, ref in enumerate((before_ref, own_ref, after_ref))
     ]
     for copy in copies:
@@ -100,7 +100,7 @@
     for part in range(3):
         copies[part].wait()
         for x in range(3):
-            coords = coord_ref[part, x].astype(F32)
+            coords = coord_ref[part, 8 * x : 8 * x + 8, 0:32].astype(F32)
             wide = jnp.concatenate([coords] * 4, axis=1)
             for n in range(8):
                 near_ref[8 * part + n, x : x + 1, :] = wide[n : n + 1, :]
@@ -161,7 +161,7 @@
     peak_ref, near_ref, row_ref, flat_ref, probe_ref, shift_ref, sem,
 ):
     pieces = [
-        pltpu.make_async_copy(ref, flat_ref.at[part], sem.at[part])
+        pltpu.make_async_copy(ref.at[0:512], flat_ref.at[part], sem.at[part])
         for part, ref in enumerate((before_ref, own_ref, after_ref))
     ]
     copies = [
@@ -176,7 +176,7 @@
     for part in range(3):
         pieces[part].wait()
         for c in range(8):
-            turned = flat_ref[part, c].astype(F32).T
+            turned = flat_ref[part, 64 * c : 64 * c + 64].astype(F32).T
             if part == 1:
                 turned_ref[c] = turned
             probe_ref[8 * part + c] = turned.astype(BF16)
@@ -320,20 +320,22 @@
     return [across * (mixed[x] + bent[x]) + inward * d[x] for x in range(3)]
 
 
-def sample_kernel(
-    slot_ref, received_ref, before_ref, own_ref, after_ref, density_ref, left_ref, sample_ref, turn_ref
-):
+def sample_kernel(slot_ref, received_ref, near_ref, density_ref, left_ref, sample_ref, turn_ref):
     for q in range(8):
         block = received_ref[q, 0:64, :].astype(BF16)
         left_ref[0:64, 64 * q : 64 * q + 64] = block[:, 0:64]
         left_ref[64:128, 64 * q : 64 * q + 64] = block[:, 64:128]
     left = left_ref[...]
     scale = 1.0 / math.sqrt(512.0)
-    for part, ref in enumerate((before_ref, own_ref, after_ref)):
+    for part in range(3):
         for pair in range(4):
             c = 2 * pair
             right = jnp.concatenate(
-                [ref[:, c].reshape(512, 128), ref[:, c + 1].reshape(512, 128)], axis=1
+                [
+                    near_ref[:, part, 64 * n : 64 * n + 64, :].reshape(512, 128)
+                    for n in (c, c + 1)
+                ],
+                axis=1,
             )
             product = jnp.dot(left, right, preferred_element_type=F32) * scale
             sample_ref[8 * part + c] = product[:, 0:128]
@@ -357,11 +359,10 @@
     space_rank = lax.axis_index("space")
     both = lambda block: (around(block, space_count, 1), around(block, space_count, -1))
 
-    pos_own = positions.transpose(1, 0, 2)
-    pos_before, pos_after = both(pos_own)
-    probe_before, probe_after = both(probes)
-    spread = jnp.broadcast_to(probes[None], (8,) + probes.shape)
-    all_own = lax.all_to_all(spread, "probe", 0, 0, tiled=True).reshape(8, 8, 64, 128)
+    coords = jnp.pad(positions.transpose(1, 0, 2), ((0, 0), (0, 0), (0, 96)))
+    own = jnp.concatenate([probes.reshape(512, 128), coords.reshape(24, 128)])
+    before, after = both(own)
+    near_all = lax.all_gather(jnp.stack([before, own, after]), "probe")
 
     present = neighbours >= 0
     slot = (neighbours // 8 - space_rank + 1) % space_count * 8 + neighbours % 8
@@ -377,7 +378,7 @@
         in_specs=[SMEM] + [HBM] * 3,
         out_specs=(HBM,) * 3,
         scratch_shapes=[
-            pltpu.VMEM((3, 3, 8, 32), BF16),
+            pltpu.VMEM((3, 24, 128), BF16),
             pltpu.VMEM((NEAR + 1, 8, 128), F32),
             pltpu.VMEM((8, 3, 32, 128), F32),
             pltpu.VMEM((space_count, 128), F32),
@@ -388,13 +389,8 @@
         cost_estimate=HEAVY,
         compiler_params=params(4),
         name="spectral",
-    )(slot, pos_before, pos_own, pos_after)
-    peak, all_own, probe_before, probe_after = lax.optimization_barrier(
-        (peak, all_own, probe_before, probe_after)
-    )
+    )(slot, before, own, after)
     peaks = lax.all_to_all(peak, "space", 0, 0, tiled=True)
-    peaks, all_own = lax.optimization_barrier((peaks, all_own))
-    all_before, all_after = both(all_own)
 
     scaled, operand, turned, one, half = pl.pallas_call(
         first_kernel,
@@ -411,7 +407,7 @@
             pltpu.VMEM((space_count, 128), F32),
             pltpu.VMEM((NEAR + 1, 8, 128), F32),
             pltpu.VMEM((8, 3, 32, 128), F32),
-            pltpu.VMEM((3, 8, 64, 128), BF16),
+            pltpu.VMEM((3, 512, 128), BF16),
             pltpu.VMEM((NEAR + 1, 128, 64), BF16),
             pltpu.VMEM((4, 8, 128), F32),
             pltpu.SemaphoreType.DMA((6,)),
@@ -419,7 +415,7 @@
         cost_estimate=LIGHT,
         compiler_params=params(16),
         name="first",
-    )(slot, peaks, near, rows, probe_before, probes, probe_after)
+    )(slot, peaks, near, rows, before, own, after)
     half_before, half_after = both(half)
 
     send = pl.pallas_call(
@@ -440,7 +436,6 @@
         compiler_params=params(16),
         name="second",
     )(slot, near, rows, scaled, operand, turned, one, half_before, half, half_after)
-    send, all_before, all_after = lax.optimization_barrier((send, all_before, all_after))
     received = lax.all_to_all(send, "probe", 0, 0, tiled=True)
     force = jnp.sum(received[:, 64:88], axis=0)
     from_after = around(force[0:8], space_count, -1)
@@ -449,7 +444,7 @@
     density = pl.pallas_call(
         sample_kernel,
         out_shape=jax.ShapeDtypeStruct((16, 15, 8, 128), BF16),
-        in_specs=[SMEM] + [WHOLE] * 4,
+        in_specs=[SMEM, WHOLE, WHOLE],
         out_specs=WHOLE,
         scratch_shapes=[
             pltpu.VMEM((128, 512), BF16),
@@ -458,7 +453,7 @@
         ],
         compiler_params=params(16),
         name="sample",
-    )(slot, received, all_before, all_own, all_after)
+    )(slot, received, near_all)
     forces = force[8:16] + from_after + from_before
     forces = jnp.stack([forces[:, 32 * x : 32 * x + 32] for x in range(3)])
     return density.transpose(0, 2, 1, 3), forces.transpose(1, 0, 2)

time: 109 us -> 119 us (1.092); the launches traced: 108 us -> 117 us
  starting transfers between devices: 35.4 us -> 19.2 us
  between operations: 0.73 us -> 14.1 us
  blocking collectives: 23.8 us -> 33.4 us
  other arithmetic: 1.33 us -> 3.07 us
    ppermute x10 -> x6, starting transfers between devices: 29.2 us -> 19.2 us  [around(): lax.ppermute(block, 'space', [((i - distance) % size, i) for i in range(s...]
    all_gather x0 -> x1, waiting for transfers between devices: none -> 9.07 us  [per_device(): near_all = lax.all_gather(jnp.stack([before, own, after]), 'probe')]
    ppermute x10 -> x6, waiting for transfers between devices: 25.3 us -> 16.8 us  [around(): lax.ppermute(block, 'space', [((i - distance) % size, i) for i in range(s...]
    all_to_all x1 -> x0, starting transfers between devices: 6.18 us -> none  [per_device(): lax.all_to_all(spread, 'probe', 0, 0, tiled=True).reshape(8, 8, 64, 128)]
    all_to_all x1, blocking collectives: 12.8 us -> 18.7 us  [per_device(): peaks = lax.all_to_all(peak, 'space', 0, 0, tiled=True)]
    all_to_all x1, blocking collectives: 11 us -> 14.7 us  [per_device(): received = lax.all_to_all(send, 'probe', 0, 0, tiled=True)]
    broadcast_in_dim x1 -> x0, local copies, waits for them, and re-layouts: 2.14 us -> none  [per_device(): spread = jnp.broadcast_to(probes[None], (8,) + probes.shape)]
    another operation x0 -> x2, other arithmetic: none -> 1.73 us  [per_device(): near_all = lax.all_gather(jnp.stack([before, own, after]), 'probe')]
  transfers between devices with their start and end apart: 11 -> 7, of which waited for: 3 -> 6; matrix products, arithmetic and copies ran while one was open for 1% -> 1% of each run, Pallas kernels for 17% -> 13%
where the time goes in v4:
time: 119 us; the launch traced here: 117 us
  blocking collectives  33.4 us (28%)
  waiting for transfers between devices  25.9 us (22%)
  starting transfers between devices  19.2 us (16%)
  Pallas kernels  18.1 us (15%)
  between operations  14.1 us (12%)
  other arithmetic  3.07 us (3%)
  local copies, waits for them, and re-layouts  2.71 us (2%)
    ppermute x6, starting transfers between devices, around(): lax.ppermute(block, 'space', [((i - distance) % size, i) for i in range(s...  19.2 us
    all_to_all x1, blocking collectives, per_device(): peaks = lax.all_to_all(peak, 'space', 0, 0, tiled=True)  18.7 us
    ppermute x6, waiting for transfers between devices, around(): lax.ppermute(block, 'space', [((i - distance) % size, i) for i in range(s...  16.8 us
    all_to_all x1, blocking collectives, per_device(): received = lax.all_to_all(send, 'probe', 0, 0, tiled=True)  14.7 us
    all_gather x1, waiting for transfers between devices, per_device(): near_all = lax.all_gather(jnp.stack([before, own, after]), 'probe')  9.07 us
    pallas_call x1, Pallas kernels, per_device(): pl.pallas_call(second_kernel, out_shape=jax.ShapeDtypeStruct((8, 88, 128)...  7.01 us
    pallas_call x1, Pallas kernels, per_device(): pl.pallas_call(first_kernel, out_shape=(jax.ShapeDtypeStruct((8, 128, 204...  5.37 us
    pallas_call x1, Pallas kernels, per_device(): pl.pallas_call(spectral_kernel, out_shape=(jax.ShapeDtypeStruct((NEAR + 1...  3.33 us
  transfers between devices with their start and end apart: 7, of which 6 were waited for; matrix products, arithmetic and copies ran while one was open for 1% of the time, Pallas kernels for 13%

profile of v4, /device:TPU:2, one launch (start us, length us, event | category | flops | bytes accessed | tf_op | source)
XLA Modules:
  0.0 116.5 jit_solution(10364655191632427184)
XLA Ops:
  7.2 0.0 all-gather.3.cloned.1.call-start
  7.2 0.7 pad_bitcast_fusion
  7.9 0.9 fusion.8
  8.8 0.1 collective-permute-start
  8.9 8.3 %collective-permute-start.1 = (bf16[536,128]{1,0:T(8,128)(2,1)S(1)}, bf16[536,128]{1,0:T(8,128)(2,1)S(1)}, u32[]{:S(2)}, u32[]{:S(2)}) collective-permute-start(bf16[536,128]{1,0:T(8,128)(2,1)S(1)} %get-tuple-element.19.own_ref), channel_id=1, source_target_pairs={{8,0},{16,8},{24,16},{32,24},{40,32},{48,40},{56,48},{64,56},{72,6... | collective-permute-start | bytes 411656 | tf_op jit(solution)/shard_map/ppermute | solution.py:354
  17.2 2.7 %collective-permute-done.before_ref = bf16[536,128]{1,0:T(8,128)(2,1)S(1)} collective-permute-done((bf16[536,128]{1,0:T(8,128)(2,1)S(1)}, bf16[536,128]{1,0:T(8,128)(2,1)S(1)}, u32[]{:S(2)}, u32[]{:S(2)}) %collective-permute-start) | collective-permute-done | bytes 137248 | tf_op jit(solution)/shard_map/ppermute | solution.py:354
  19.9 1.3 %collective-permute-done.1.after_ref = bf16[536,128]{1,0:T(8,128)(2,1)S(1)} collective-permute-done((bf16[536,128]{1,0:T(8,128)(2,1)S(1)}, bf16[536,128]{1,0:T(8,128)(2,1)S(1)}, u32[]{:S(2)}, u32[]{:S(2)}) %collective-permute-start.1) | collective-permute-done | bytes 137248 | tf_op jit(solution)/shard_map/ppermute | solution.py:354
  21.3 0.8 pad_maximum_fusion
  22.1 0.0 all-gather.3.cloned.1.call-update
  22.1 0.7 fusion.5
  22.8 3.3 %spectral.1 = (f32[25,8,128]{2,1,0:T(8,128)S(1)}, f32[8,3,32,128]{3,2,1,0:T(8,128)S(1)}, f32[32,128]{1,0:T(8,128)S(1)}) custom-call(s32[8,16]{1,0:T(8,128)S(1)} %pad.8.slot_ref, bf16[536,128]{1,0:T(8,128)(2,1)S(1)} %collective-permute-done.before_ref, bf16[536,128]{1,0:T(8,128)(2,1)S(1)} %get-tuple-element.19.own_ref, ...), custom_call_target="tpu_custom_call" | custom-call | bytes 60000000 | tf_op jit(solution)/shard_map/spectral/pallas_call | solution.py:371
  26.1 18.7 %all_to_all.16 = f32[32,1,128]{2,1,0:T(1,128)S(1)} all-to-all(f32[32,1,128]{2,1,0:T(1,128)S(1)} %bitcast.26), channel_id=1, replica_groups=mesh['space'=32,'probe'=8] {'space'}, dimensions={0} | all-to-all | bytes 32768 | tf_op jit(solution)/shard_map/all_to_all | solution.py:393
  44.9 5.4 %first.1 = (bf16[8,128,2048]{2,1,0:T(8,128)(2,1)S(1)}, bf16[8,2048,64]{2,1,0:T(8,128)(2,1)S(1)}, f32[8,128,64]{2,1,0:T(8,128)S(1)}, f32[8,128,64]{2,1,0:T(8,128)S(1)}, bf16[4,128,128]{2,1,0:T(8,128)(2,1)S(1)}) custom-call(s32[8,16]{1,0:T(8,128)S(1)} %pad.8.slot_ref, f32[32,128]{1,0:T(8,128)S(1)} %bitcast.25, f32[25,8,128]{2,1,0:T(8,128)S(1)} %get-tuple-element.10.near_in, ...), custom_call_target="tpu_custom_call" | custom-call | tf_op jit(solution)/shard_map/first/pallas_call | solution.py:395
  50.2 0.1 collective-permute-start.2
  50.3 6.0 %collective-permute-start.3 = (bf16[4,128,128]{2,1,0:T(8,128)(2,1)S(1)}, bf16[4,128,128]{2,1,0:T(8,128)(2,1)S(1)}, u32[]{:S(2)}, u32[]{:S(2)}) collective-permute-start(bf16[4,128,128]{2,1,0:T(8,128)(2,1)S(1)} %get-tuple-element.17.own_ref), channel_id=1, source_target_pairs={{8,0},{16,8},{24,16},{32,24},{40,32},{48,40},{56,48},{64,56},{72,6... | collective-permute-start | bytes 393224 | tf_op jit(solution)/shard_map/ppermute | solution.py:354
  56.3 5.4 %collective-permute-done.2.before_ref = bf16[4,128,128]{2,1,0:T(8,128)(2,1)S(1)} collective-permute-done((bf16[4,128,128]{2,1,0:T(8,128)(2,1)S(1)}, bf16[4,128,128]{2,1,0:T(8,128)(2,1)S(1)}, u32[]{:S(2)}, u32[]{:S(2)}) %collective-permute-start.2) | collective-permute-done | bytes 131104 | tf_op jit(solution)/shard_map/ppermute | solution.py:354
  61.7 0.0 collective-permute-done.3.after_ref
  61.7 7.0 %second.1 = f32[8,88,128]{2,1,0:T(8,128)S(1)} custom-call(s32[8,16]{1,0:T(8,128)S(1)} %pad.8.slot_ref, f32[25,8,128]{2,1,0:T(8,128)S(1)} %get-tuple-element.10.near_in, f32[8,3,32,128]{3,2,1,0:T(8,128)S(1)} %get-tuple-element.11.row_in, bf16[8,128,2048]{2,1,0:T(8,128)(2,1)S(1)} %get-tuple-element.13.scaled_ref, ...), custom_call_target="tpu_custom_call" | custom-call | tf_op jit(solution)/shard_map/second/pallas_call | solution.py:421
  68.7 14.7 %all_to_all.17.received_ref = f32[8,88,128]{2,1,0:T(8,128)S(1)} all-to-all(f32[8,88,128]{2,1,0:T(8,128)S(1)} %second.1), channel_id=1, replica_groups=mesh['space'=32,'probe'=8] {'probe'}, dimensions={0} | all-to-all | bytes 720896 | tf_op jit(solution)/shard_map/all_to_all | solution.py:439
  83.5 4.8 %collective-permute-start.4 = (f32[8,128]{1,0:T(8,128)S(1)}, f32[8,128]{1,0:T(8,128)S(1)}, u32[]{:S(2)}, u32[]{:S(2)}) collective-permute-start(f32[8,128]{1,0:T(8,128)S(1)} %get-tuple-element.20), channel_id=1, source_target_pairs={{8,0},{16,8},{24,16},{32,24},{40,32},{48,40},{56,48},{64,56},{72,6... | collective-permute-start | bytes 12296 | tf_op jit(solution)/shard_map/ppermute | solution.py:354
  88.3 0.0 collective-permute-start.5
  88.3 1.3 %collective-permute-done.4 = f32[8,128]{1,0:T(8,128)S(1)} collective-permute-done((f32[8,128]{1,0:T(8,128)S(1)}, f32[8,128]{1,0:T(8,128)S(1)}, u32[]{:S(2)}, u32[]{:S(2)}) %collective-permute-start.4) | collective-permute-done | bytes 4128 | tf_op jit(solution)/shard_map/ppermute | solution.py:354
  89.6 6.0 %collective-permute-done.5 = f32[8,128]{1,0:T(8,128)S(1)} collective-permute-done((f32[8,128]{1,0:T(8,128)S(1)}, f32[8,128]{1,0:T(8,128)S(1)}, u32[]{:S(2)}, u32[]{:S(2)}) %collective-permute-start.5) | collective-permute-done | bytes 4128 | tf_op jit(solution)/shard_map/ppermute | solution.py:354
  95.6 0.1 slice_bitcast_fusion.2
  95.7 0.6 maximum_bitcast_fusion
  96.3 9.1 %all-gather.3.cloned.1.call-done = bf16[24,536,128]{2,1,0:T(8,128)(2,1)} async-done(((bf16[3,536,128]{2,1,0:T(8,128)(2,1)}), bf16[24,536,128]{2,1,0:T(8,128)(2,1)}) %all-gather.3.cloned.1.call-update) | async-done | bytes 3293200 | tf_op jit(solution)/shard_map/all_gather | solution.py:365
  105.4 0.0 copy-start
  105.4 1.9 %copy-done = bf16[24,536,128]{2,1,0:T(8,128)(2,1)S(1)} copy-done((bf16[24,536,128]{2,1,0:T(8,128)(2,1)S(1)}, bf16[24,536,128]{2,1,0:T(8,128)(2,1)}, u32[]{:S(2)}) %copy-start) | copy-done | bytes 3293208
  107.3 2.4 %sample.1 = bf16[16,15,8,128]{3,2,1,0:T(8,128)(2,1)} custom-call(s32[8,16]{1,0:T(8,128)S(1)} %pad.8.slot_ref, f32[8,88,128]{2,1,0:T(8,128)S(1)} %all_to_all.17.received_ref, bf16[8,3,536,128]{3,2,1,0:T(8,128)(2,1)S(1)} %bitcast.22), custom_call_target="tpu_custom_call" | custom-call | tf_op jit(solution)/shard_map/sample/pallas_call | solution.py:444
  (4 shorter events, 0.0 us)
Async XLA Ops:
  7.2 98.2 %all-gather.3.cloned.1.call-start = ((), (), s32[]{:S(2)}) async-start(), calls=%async_computation.2 | async-start | bytes 3704832 | tf_op jit(solution)/shard_map/all_gather | solution.py:365
  8.8 11.1 %collective-permute-start = (bf16[536,128]{1,0:T(8,128)(2,1)S(1)}, bf16[536,128]{1,0:T(8,128)(2,1)S(1)}, u32[]{:S(2)}, u32[]{:S(2)}) collective-permute-start(bf16[536,128]{1,0:T(8,128)(2,1)S(1)} %get-tuple-element.19.own_ref), channel_id=1, source_target_pairs={{248,0},{0,8},{8,16},{16,24},{24,32},{32,40},{40,48},{48,56},{56,6... | collective-permute-start | bytes 411656 | tf_op jit(solution)/shard_map/ppermute | solution.py:354
  8.9 12.3 %collective-permute-start.1 = (bf16[536,128]{1,0:T(8,128)(2,1)S(1)}, bf16[536,128]{1,0:T(8,128)(2,1)S(1)}, u32[]{:S(2)}, u32[]{:S(2)}) collective-permute-start(bf16[536,128]{1,0:T(8,128)(2,1)S(1)} %get-tuple-element.19.own_ref), channel_id=1, source_target_pairs={{8,0},{16,8},{24,16},{32,24},{40,32},{48,40},{56,48},{64,56},{72,6... | collective-permute-start | bytes 411656 | tf_op jit(solution)/shard_map/ppermute | solution.py:354
  50.2 11.5 %collective-permute-start.2 = (bf16[4,128,128]{2,1,0:T(8,128)(2,1)S(1)}, bf16[4,128,128]{2,1,0:T(8,128)(2,1)S(1)}, u32[]{:S(2)}, u32[]{:S(2)}) collective-permute-start(bf16[4,128,128]{2,1,0:T(8,128)(2,1)S(1)} %get-tuple-element.17.own_ref), channel_id=1, source_target_pairs={{248,0},{0,8},{8,16},{16,24},{24,32},{32,40},{40,48},{48,56},{56,6... | collective-permute-start | bytes 393224 | tf_op jit(solution)/shard_map/ppermute | solution.py:354
  50.3 11.4 %collective-permute-start.3 = (bf16[4,128,128]{2,1,0:T(8,128)(2,1)S(1)}, bf16[4,128,128]{2,1,0:T(8,128)(2,1)S(1)}, u32[]{:S(2)}, u32[]{:S(2)}) collective-permute-start(bf16[4,128,128]{2,1,0:T(8,128)(2,1)S(1)} %get-tuple-element.17.own_ref), channel_id=1, source_target_pairs={{8,0},{16,8},{24,16},{32,24},{40,32},{48,40},{56,48},{64,56},{72,6... | collective-permute-start | bytes 393224 | tf_op jit(solution)/shard_map/ppermute | solution.py:354
  83.5 6.1 %collective-permute-start.4 = (f32[8,128]{1,0:T(8,128)S(1)}, f32[8,128]{1,0:T(8,128)S(1)}, u32[]{:S(2)}, u32[]{:S(2)}) collective-permute-start(f32[8,128]{1,0:T(8,128)S(1)} %get-tuple-element.20), channel_id=1, source_target_pairs={{8,0},{16,8},{24,16},{32,24},{40,32},{48,40},{56,48},{64,56},{72,6... | collective-permute-start | bytes 12296 | tf_op jit(solution)/shard_map/ppermute | solution.py:354
  88.3 7.3 %collective-permute-start.5 = (f32[8,128]{1,0:T(8,128)S(1)}, f32[8,128]{1,0:T(8,128)S(1)}, u32[]{:S(2)}, u32[]{:S(2)}) collective-permute-start(f32[8,128]{1,0:T(8,128)S(1)} %get-tuple-element.21), channel_id=1, source_target_pairs={{248,0},{0,8},{8,16},{16,24},{24,32},{32,40},{40,48},{48,56},{56,6... | collective-permute-start | bytes 12296 | tf_op jit(solution)/shard_map/ppermute | solution.py:354
  105.4 1.9 %copy-start = (bf16[24,536,128]{2,1,0:T(8,128)(2,1)S(1)}, bf16[24,536,128]{2,1,0:T(8,128)(2,1)}, u32[]{:S(2)}) copy-start(bf16[24,536,128]{2,1,0:T(8,128)(2,1)} %all-gather.3.cloned.1.call-done) | copy-start | bytes 9879556
Sparse Core Ops, SparseCore 0:
  22.2 83.1 all-gather.2

commit v5 on v4

--- a/solution.py
+++ b/solution.py
@@ -320,26 +320,43 @@
     return [across * (mixed[x] + bent[x]) + inward * d[x] for x in range(3)]
 
 
-def sample_kernel(slot_ref, received_ref, near_ref, density_ref, left_ref, sample_ref, turn_ref):
-    for q in range(8):
-        block = received_ref[q, 0:64, :].astype(BF16)
-        left_ref[0:64, 64 * q : 64 * q + 64] = block[:, 0:64]
-        left_ref[64:128, 64 * q : 64 * q + 64] = block[:, 64:128]
+def sample_kernel(
+    slot_ref, place_ref, received_ref, *refs
+):
+    pieces, swapped = refs[0:4], refs[4:8]
+    density_ref, left_ref, sample_ref, turn_ref = refs[8:]
+    rank, core = place_ref[0], place_ref[1]
+    for distance in range(4):
+        source = (rank - 2 * distance + 8) % 8
+        for e in range(2):
+            q = source if e == 0 else source + 1 - 2 * (source % 2)
+            low = 64 * (2 * distance + e)
+            block = received_ref[q, 0:64, :].astype(BF16)
+            left_ref[0:64, low : low + 64] = block[:, 0:64]
+            left_ref[64:128, low : low + 64] = block[:, 64:128]
     left = left_ref[...]
     scale = 1.0 / math.sqrt(512.0)
-    for part in range(3):
+    sides = ((pieces, 0, 16 * core), (pieces, 1, 8), (swapped, 1, 16 - 16 * core))
+    for source_refs, index, base in sides:
         for pair in range(4):
             c = 2 * pair
             right = jnp.concatenate(
                 [
-                    near_ref[:, part, 64 * n : 64 * n + 64, :].reshape(512, 128)
+                    jnp.concatenate(
+                        [
+                            ref[e, index, 64 * n : 64 * n + 64, :]
+                            for ref in source_refs
+                            for e in range(2)
+                        ],
+                        axis=0,
+                    )
                     for n in (c, c + 1)
                 ],
                 axis=1,
             )
             product = jnp.dot(left, right, preferred_element_type=F32) * scale
-            sample_ref[8 * part + c] = product[:, 0:128]
-            sample_ref[8 * part + c + 1] = product[:, 128:256]
+            sample_ref[base + c] = product[:, 0:128]
+            sample_ref[base + c + 1] = product[:, 128:256]
     sample_ref[DEAD] = jnp.zeros((128, 128), F32)
     for c in range(8):
         for k in range(15):
@@ -354,6 +371,10 @@
     return lax.ppermute(block, "space", [((i - distance) % size, i) for i in range(size)])
 
 
+def along_probe(block, target):
+    return lax.ppermute(block, "probe", [(i, target(i)) for i in range(8)])
+
+
 def per_device(positions, probes, neighbours):
     space_count = lax.axis_size("space")
     space_rank = lax.axis_index("space")
@@ -362,7 +383,9 @@
     coords = jnp.pad(positions.transpose(1, 0, 2), ((0, 0), (0, 0), (0, 96)))
     own = jnp.concatenate([probes.reshape(512, 128), coords.reshape(24, 128)])
     before, after = both(own)
-    near_all = lax.all_gather(jnp.stack([before, own, after]), "probe")
+    core = space_rank % 2
+    pair = jnp.stack([jnp.where(core == 0, before, after)[:512], own[:512]])
+    across = along_probe(pair, lambda i: i ^ 1)
 
     present = neighbours >= 0
     slot = (neighbours // 8 - space_rank + 1) % space_count * 8 + neighbours % 8
@@ -391,6 +414,12 @@
         name="spectral",
     )(slot, before, own, after)
     peaks = lax.all_to_all(peak, "space", 0, 0, tiled=True)
+    peaks, pair, across = lax.optimization_barrier((peaks, pair, across))
+    quad = jnp.stack([pair, across])
+    pieces = [quad] + [
+        along_probe(quad, lambda i, distance=distance: (i + 2 * distance) % 8)
+        for distance in range(1, 4)
+    ]
 
     scaled, operand, turned, one, half = pl.pallas_call(
         first_kernel,
@@ -436,6 +465,10 @@
         compiler_params=params(16),
         name="second",
     )(slot, near, rows, scaled, operand, turned, one, half_before, half, half_after)
+    send, pieces = lax.optimization_barrier((send, pieces))
+    swapped = [
+        lax.ppermute(piece, "space", [(i, i ^ 1) for i in range(space_count)]) for piece in pieces
+    ]
     received = lax.all_to_all(send, "probe", 0, 0, tiled=True)
     force = jnp.sum(received[:, 64:88], axis=0)
     from_after = around(force[0:8], space_count, -1)
@@ -444,7 +477,7 @@
     density = pl.pallas_call(
         sample_kernel,
         out_shape=jax.ShapeDtypeStruct((16, 15, 8, 128), BF16),
-        in_specs=[SMEM, WHOLE, WHOLE],
+        in_specs=[SMEM, SMEM] + [WHOLE] * 9,
         out_specs=WHOLE,
         scratch_shapes=[
             pltpu.VMEM((128, 512), BF16),
@@ -453,7 +486,9 @@
         ],
         compiler_params=params(16),
         name="sample",
-    )(slot, received, near_all)
+    )(
+        slot, jnp.stack([lax.axis_index("probe"), core]), received, *pieces, *swapped
+    )
     forces = force[8:16] + from_after + from_before
     forces = jnp.stack([forces[:, 32 * x : 32 * x + 32] for x in range(3)])
     return density.transpose(0, 2, 1, 3), forces.transpose(1, 0, 2)

time: 119 us -> 88.3 us (0.74); the launches traced: 117 us -> 87.9 us
  blocking collectives: 33.4 us -> 18.6 us
  waiting for transfers between devices: 25.9 us -> 11.6 us
  starting transfers between devices: 19.2 us -> 33.1 us
  between operations: 14.1 us -> 0.75 us
  local copies, waits for them, and re-layouts: 2.71 us -> 0.78 us
  Pallas kernels: 18.1 us -> 19.7 us
    all_to_all x1 -> x0, blocking collectives: 14.7 us -> none  [per_device(): received = lax.all_to_all(send, 'probe', 0, 0, tiled=True)]
    ppermute x6, waiting for transfers between devices: 16.8 us -> 5.93 us  [around(): lax.ppermute(block, 'space', [((i - distance) % size, i) for i in range(s...]
    all_gather x1 -> x0, waiting for transfers between devices: 9.07 us -> none  [per_device(): near_all = lax.all_gather(jnp.stack([before, own, after]), 'probe')]
    ppermute x0 -> x8, starting transfers between devices: none -> 8.09 us  [the longest x4 7.07 us: along_probe(): return lax.ppermute(block, 'probe', [(i, target(i)) for i in range(8)])]
    all_to_all x0 -> x1, waiting for transfers between devices: none -> 5.44 us  [per_device(): received = lax.all_to_all(send, 'probe', 0, 0, tiled=True)]
    all_to_all x0 -> x1, starting transfers between devices: none -> 4.62 us  [per_device(): received = lax.all_to_all(send, 'probe', 0, 0, tiled=True)]
    unnamed x2 -> x0, local copies, waits for them, and re-layouts: 1.93 us -> none
    ppermute x6, starting transfers between devices: 19.2 us -> 20.4 us  [around(): lax.ppermute(block, 'space', [((i - distance) % size, i) for i in range(s...]
  transfers between devices with their start and end apart: 7 -> 15, of which waited for: 6 -> 5; matrix products, arithmetic and copies ran while one was open for 1% -> 1% of each run, Pallas kernels for 13% -> 22%
where the time goes in v5:
time: 88.3 us; the launch traced here: 87.9 us
  starting transfers between devices  33.1 us (37%)
  Pallas kernels  19.7 us (22%)
  blocking collectives  18.6 us (21%)
  waiting for transfers between devices  11.6 us (13%)
  other arithmetic  3.32 us (4%)
    ppermute x6, starting transfers between devices, around(): lax.ppermute(block, 'space', [((i - distance) % size, i) for i in range(s...  20.4 us
    all_to_all x1, blocking collectives, per_device(): peaks = lax.all_to_all(peak, 'space', 0, 0, tiled=True)  18.6 us
    pallas_call x1, Pallas kernels, per_device(): pl.pallas_call(second_kernel, out_shape=jax.ShapeDtypeStruct((8, 88, 128)...  7.78 us
    ppermute x4, starting transfers between devices, along_probe(): return lax.ppermute(block, 'probe', [(i, target(i)) for i in range(8)])  7.07 us
    ppermute x6, waiting for transfers between devices, around(): lax.ppermute(block, 'space', [((i - distance) % size, i) for i in range(s...  5.93 us
    all_to_all x1, waiting for transfers between devices, per_device(): received = lax.all_to_all(send, 'probe', 0, 0, tiled=True)  5.44 us
    pallas_call x1, Pallas kernels, per_device(): pl.pallas_call(first_kernel, out_shape=(jax.ShapeDtypeStruct((8, 128, 204...  5.37 us
    all_to_all x1, starting transfers between devices, per_device(): received = lax.all_to_all(send, 'probe', 0, 0, tiled=True)  4.62 us
  transfers between devices with their start and end apart: 15, of which 5 were waited for; matrix products, arithmetic and copies ran while one was open for 1% of the time, Pallas kernels for 22%

profile of v5, /device:TPU:2, one launch (start us, length us, event | category | flops | bytes accessed | tf_op | source)
XLA Modules:
  0.0 87.9 jit_solution(11456773953754891867)
XLA Ops:
  0.6 0.7 pad_bitcast_fusion
  1.3 0.9 %pad_maximum_fusion.2.own_ref = bf16[536,128]{1,0:T(8,128)(2,1)S(1)} fusion(bf16[24,128]{1,0:T(8,128)(2,1)S(1)} %pad_bitcast_fusion, bf16[512,128]{1,0:T(8,128)(2,1)} %bitcast.27), kind=kLoop, calls=%fused_computation.2 | loop fusion | flops 274432 | bytes 274432 | tf_op jit(solution)/shard_map/concatenate | solution.py:384
  2.2 0.1 collective-permute-start
  2.3 8.3 %collective-permute-start.1 = (bf16[536,128]{1,0:T(8,128)(2,1)S(1)}, bf16[536,128]{1,0:T(8,128)(2,1)S(1)}, u32[]{:S(2)}, u32[]{:S(2)}) collective-permute-start(bf16[536,128]{1,0:T(8,128)(2,1)S(1)} %pad_maximum_fusion.2.own_ref), channel_id=1, source_target_pairs={{8,0},{16,8},{24,16},{32,24},{40,32},{48,40},{56,48},{64,56},{72,6... | collective-permute-start | bytes 411656 | tf_op jit(solution)/shard_map/ppermute | solution.py:371
  10.6 2.7 %collective-permute-done.before_ref = bf16[536,128]{1,0:T(8,128)(2,1)S(1)} collective-permute-done((bf16[536,128]{1,0:T(8,128)(2,1)S(1)}, bf16[536,128]{1,0:T(8,128)(2,1)S(1)}, u32[]{:S(2)}, u32[]{:S(2)}) %collective-permute-start) | collective-permute-done | bytes 137248 | tf_op jit(solution)/shard_map/ppermute | solution.py:371
  13.3 0.4 collective-permute-done.1.after_ref
  13.8 0.9 %pad_maximum_fusion.1 = bf16[2,512,128]{2,1,0:T(8,128)(2,1)S(1)} fusion(bf16[1,512,128]{2,1,0:T(8,128)(2,1)} %bitcast.28, bf16[1,512,128]{2,1,0:T(8,128)(2,1)S(1)} %fusion), kind=kLoop, calls=%fused_computation.1 | loop fusion | flops 131072 | bytes 524288 | tf_op jit(solution)/shard_map/stack | solution.py:387
  14.7 2.2 %collective-permute-start.2 = (bf16[2,512,128]{2,1,0:T(8,128)(2,1)S(1)}, bf16[2,512,128]{2,1,0:T(8,128)(2,1)S(1)}, u32[]{:S(2)}, u32[]{:S(2)}) collective-permute-start(bf16[2,512,128]{2,1,0:T(8,128)(2,1)S(1)} %pad_maximum_fusion.1), channel_id=1, source_target_pairs={{0,1},{1,0},{2,3},{3,2},{4,5},{5,4},{6,7},{7,6},{8,9},{9,8},{10,11... | collective-permute-start | bytes 786440 | tf_op jit(solution)/shard_map/ppermute | solution.py:375
  17.0 0.7 fusion.6
  17.7 3.3 %spectral.1 = (f32[25,8,128]{2,1,0:T(8,128)S(1)}, f32[8,3,32,128]{3,2,1,0:T(8,128)S(1)}, f32[32,128]{1,0:T(8,128)S(1)}) custom-call(s32[8,16]{1,0:T(8,128)S(1)} %pad.8.slot_ref, bf16[536,128]{1,0:T(8,128)(2,1)S(1)} %collective-permute-done.before_ref, bf16[536,128]{1,0:T(8,128)(2,1)S(1)} %pad_maximum_fusion.2.own_ref, ...), custom_call_target="tpu_custom_call" | custom-call | bytes 60000000 | tf_op jit(solution)/shard_map/spectral/pallas_call | solution.py:394
  21.0 18.6 %all_to_all.17 = f32[32,1,128]{2,1,0:T(1,128)S(1)} all-to-all(f32[32,1,128]{2,1,0:T(1,128)S(1)} %bitcast.25), channel_id=1, replica_groups=mesh['space'=32,'probe'=8] {'space'}, dimensions={0} | all-to-all | bytes 32768 | tf_op jit(solution)/shard_map/all_to_all | solution.py:416
  39.6 0.0 collective-permute-done.2
  39.6 0.1 pad_maximum_fusion.refs_0_
  39.7 1.6 %collective-permute-start.5 = (bf16[2,2,512,128]{3,2,1,0:T(8,128)(2,1)S(1)}, bf16[2,2,512,128]{3,2,1,0:T(8,128)(2,1)S(1)}, u32[]{:S(2)}, u32[]{:S(2)}) collective-permute-start(bf16[2,2,512,128]{3,2,1,0:T(8,128)(2,1)S(1)} %pad_maximum_fusion.refs_0_), channel_id=1, source_target_pairs={{0,2},{1,3},{2,4},{3,5},{4,6},{5,7},{6,0},{7,1},{8,10},{9,11},{10,... | collective-permute-start | bytes 1572872 | tf_op jit(solution)/shard_map/ppermute | solution.py:375
  41.2 1.1 %collective-permute-start.6 = (bf16[2,2,512,128]{3,2,1,0:T(8,128)(2,1)S(1)}, bf16[2,2,512,128]{3,2,1,0:T(8,128)(2,1)S(1)}, u32[]{:S(2)}, u32[]{:S(2)}) collective-permute-start(bf16[2,2,512,128]{3,2,1,0:T(8,128)(2,1)S(1)} %pad_maximum_fusion.refs_0_), channel_id=1, source_target_pairs={{0,4},{1,5},{2,6},{3,7},{4,0},{5,1},{6,2},{7,3},{8,12},{9,13},{10,... | collective-permute-start | bytes 1572872 | tf_op jit(solution)/shard_map/ppermute | solution.py:375
  42.4 2.2 %collective-permute-start.7 = (bf16[2,2,512,128]{3,2,1,0:T(8,128)(2,1)S(1)}, bf16[2,2,512,128]{3,2,1,0:T(8,128)(2,1)S(1)}, u32[]{:S(2)}, u32[]{:S(2)}) collective-permute-start(bf16[2,2,512,128]{3,2,1,0:T(8,128)(2,1)S(1)} %pad_maximum_fusion.refs_0_), channel_id=1, source_target_pairs={{0,6},{1,7},{2,0},{3,1},{4,2},{5,3},{6,4},{7,5},{8,14},{9,15},{10,... | collective-permute-start | bytes 1572872 | tf_op jit(solution)/shard_map/ppermute | solution.py:375
  44.5 5.4 %first.1 = (bf16[8,128,2048]{2,1,0:T(8,128)(2,1)S(1)}, bf16[8,2048,64]{2,1,0:T(8,128)(2,1)S(1)}, f32[8,128,64]{2,1,0:T(8,128)S(1)}, f32[8,128,64]{2,1,0:T(8,128)S(1)}, bf16[4,128,128]{2,1,0:T(8,128)(2,1)S(1)}) custom-call(s32[8,16]{1,0:T(8,128)S(1)} %pad.8.slot_ref, f32[32,128]{1,0:T(8,128)S(1)} %bitcast.24, f32[25,8,128]{2,1,0:T(8,128)S(1)} %get-tuple-element.18.near_in, ...), custom_call_target="tpu_custom_call" | custom-call | tf_op jit(solution)/shard_map/first/pallas_call | solution.py:424
  49.9 0.1 collective-permute-start.3
  50.0 6.0 %collective-permute-start.4 = (bf16[4,128,128]{2,1,0:T(8,128)(2,1)S(1)}, bf16[4,128,128]{2,1,0:T(8,128)(2,1)S(1)}, u32[]{:S(2)}, u32[]{:S(2)}) collective-permute-start(bf16[4,128,128]{2,1,0:T(8,128)(2,1)S(1)} %get-tuple-element.26.own_ref), channel_id=1, source_target_pairs={{8,0},{16,8},{24,16},{32,24},{40,32},{48,40},{56,48},{64,56},{72,6... | collective-permute-start | bytes 393224 | tf_op jit(solution)/shard_map/ppermute | solution.py:371
  55.9 2.7 %collective-permute-done.3.before_ref = bf16[4,128,128]{2,1,0:T(8,128)(2,1)S(1)} collective-permute-done((bf16[4,128,128]{2,1,0:T(8,128)(2,1)S(1)}, bf16[4,128,128]{2,1,0:T(8,128)(2,1)S(1)}, u32[]{:S(2)}, u32[]{:S(2)}) %collective-permute-start.3) | collective-permute-done | bytes 131104 | tf_op jit(solution)/shard_map/ppermute | solution.py:371
  58.7 0.0 collective-permute-done.4.after_ref
  58.7 7.8 %second.1 = f32[8,88,128]{2,1,0:T(8,128)} custom-call(s32[8,16]{1,0:T(8,128)S(1)} %pad.8.slot_ref, f32[25,8,128]{2,1,0:T(8,128)S(1)} %get-tuple-element.18.near_in, f32[8,3,32,128]{3,2,1,0:T(8,128)S(1)} %get-tuple-element.19.row_in, bf16[8,128,2048]{2,1,0:T(8,128)(2,1)S(1)} %get-tuple-element.22.scaled_ref, ...), custom_call_target="tpu_custom_call" | custom-call | tf_op jit(solution)/shard_map/second/pallas_call | solution.py:450
  66.5 0.0 collective-permute-done.5.refs_1_
  66.5 0.0 collective-permute-done.6.refs_2_
  66.5 0.2 collective-permute-done.7.refs_3_
  66.7 4.6 %all-to-all-start.1 = ((f32[8,88,128]{2,1,0:T(8,128)}), f32[8,88,128]{2,1,0:T(8,128)S(1)}, u32[]{:S(2)}, u32[]{:S(2)}) async-start(f32[8,88,128]{2,1,0:T(8,128)} %second.1), calls=%async_computation.1 | async-start | bytes 720896 | tf_op jit(solution)/shard_map/all_to_all | solution.py:472
  71.4 0.0 collective-permute-start.8
  71.4 0.5 collective-permute-start.9
  71.9 0.0 collective-permute-start.10
  71.9 0.5 collective-permute-start.11
  72.4 5.4 %all-to-all-done.1.received_ref = f32[8,88,128]{2,1,0:T(8,128)S(1)} async-done(((f32[8,88,128]{2,1,0:T(8,128)}), f32[8,88,128]{2,1,0:T(8,128)S(1)}, u32[]{:S(2)}, u32[]{:S(2)}) %all-to-all-start.1) | async-done | bytes 360480 | tf_op jit(solution)/shard_map/all_to_all | solution.py:472
  77.8 0.1 collective-permute-start.13
  77.9 0.0 collective-permute-done.8.refs_4_
  78.0 5.9 %collective-permute-start.12 = (f32[8,128]{1,0:T(8,128)S(1)}, f32[8,128]{1,0:T(8,128)S(1)}, u32[]{:S(2)}, u32[]{:S(2)}) collective-permute-start(f32[8,128]{1,0:T(8,128)S(1)} %get-tuple-element.34), channel_id=1, source_target_pairs={{8,0},{16,8},{24,16},{32,24},{40,32},{48,40},{56,48},{64,56},{72,6... | collective-permute-start | bytes 12296 | tf_op jit(solution)/shard_map/ppermute | solution.py:371
  83.9 0.1 pad_add_fusion.place_ref
  84.0 0.0 collective-permute-done.9.refs_5_
  84.0 0.0 collective-permute-done.10.refs_6_
  84.0 0.0 collective-permute-done.11.refs_7_
  84.0 3.2 %sample.1 = bf16[16,15,8,128]{3,2,1,0:T(8,128)(2,1)} custom-call(s32[8,16]{1,0:T(8,128)S(1)} %pad.8.slot_ref, s32[2]{0:T(128)S(1)} %pad_add_fusion.place_ref, f32[8,88,128]{2,1,0:T(8,128)S(1)} %all-to-all-done.1.received_ref, bf16[2,2,512,128]{3,2,1,0:T(8,128)(2,1)S(1)} %pad_maximum_fusion.refs_0_, ...), custom_call_target="tpu_custom_call" | custom-call | tf_op jit(solution)/shard_map/sample/pallas_call | solution.py:477
  87.2 0.0 collective-permute-done.13
  87.2 0.0 collective-permute-done.12
  87.2 0.1 slice_bitcast_fusion.2
  87.2 0.6 maximum_bitcast_fusion
  (5 shorter events, 0.0 us)
Async XLA Ops:
  2.2 11.1 %collective-permute-start = (bf16[536,128]{1,0:T(8,128)(2,1)S(1)}, bf16[536,128]{1,0:T(8,128)(2,1)S(1)}, u32[]{:S(2)}, u32[]{:S(2)}) collective-permute-start(bf16[536,128]{1,0:T(8,128)(2,1)S(1)} %pad_maximum_fusion.2.own_ref), channel_id=1, source_target_pairs={{248,0},{0,8},{8,16},{16,24},{24,32},{32,40},{40,48},{48,56},{56,6... | collective-permute-start | bytes 411656 | tf_op jit(solution)/shard_map/ppermute | solution.py:371
  2.3 11.4 %collective-permute-start.1 = (bf16[536,128]{1,0:T(8,128)(2,1)S(1)}, bf16[536,128]{1,0:T(8,128)(2,1)S(1)}, u32[]{:S(2)}, u32[]{:S(2)}) collective-permute-start(bf16[536,128]{1,0:T(8,128)(2,1)S(1)} %pad_maximum_fusion.2.own_ref), channel_id=1, source_target_pairs={{8,0},{16,8},{24,16},{32,24},{40,32},{48,40},{56,48},{64,56},{72,6... | collective-permute-start | bytes 411656 | tf_op jit(solution)/shard_map/ppermute | solution.py:371
  14.7 24.9 %collective-permute-start.2 = (bf16[2,512,128]{2,1,0:T(8,128)(2,1)S(1)}, bf16[2,512,128]{2,1,0:T(8,128)(2,1)S(1)}, u32[]{:S(2)}, u32[]{:S(2)}) collective-permute-start(bf16[2,512,128]{2,1,0:T(8,128)(2,1)S(1)} %pad_maximum_fusion.1), channel_id=1, source_target_pairs={{0,1},{1,0},{2,3},{3,2},{4,5},{5,4},{6,7},{7,6},{8,9},{9,8},{10,11... | collective-permute-start | bytes 786440 | tf_op jit(solution)/shard_map/ppermute | solution.py:375
  39.7 26.8 %collective-permute-start.5 = (bf16[2,2,512,128]{3,2,1,0:T(8,128)(2,1)S(1)}, bf16[2,2,512,128]{3,2,1,0:T(8,128)(2,1)S(1)}, u32[]{:S(2)}, u32[]{:S(2)}) collective-permute-start(bf16[2,2,512,128]{3,2,1,0:T(8,128)(2,1)S(1)} %pad_maximum_fusion.refs_0_), channel_id=1, source_target_pairs={{0,2},{1,3},{2,4},{3,5},{4,6},{5,7},{6,0},{7,1},{8,10},{9,11},{10,... | collective-permute-start | bytes 1572872 | tf_op jit(solution)/shard_map/ppermute | solution.py:375
  41.2 25.3 %collective-permute-start.6 = (bf16[2,2,512,128]{3,2,1,0:T(8,128)(2,1)S(1)}, bf16[2,2,512,128]{3,2,1,0:T(8,128)(2,1)S(1)}, u32[]{:S(2)}, u32[]{:S(2)}) collective-permute-start(bf16[2,2,512,128]{3,2,1,0:T(8,128)(2,1)S(1)} %pad_maximum_fusion.refs_0_), channel_id=1, source_target_pairs={{0,4},{1,5},{2,6},{3,7},{4,0},{5,1},{6,2},{7,3},{8,12},{9,13},{10,... | collective-permute-start | bytes 1572872 | tf_op jit(solution)/shard_map/ppermute | solution.py:375
  42.4 24.4 %collective-permute-start.7 = (bf16[2,2,512,128]{3,2,1,0:T(8,128)(2,1)S(1)}, bf16[2,2,512,128]{3,2,1,0:T(8,128)(2,1)S(1)}, u32[]{:S(2)}, u32[]{:S(2)}) collective-permute-start(bf16[2,2,512,128]{3,2,1,0:T(8,128)(2,1)S(1)} %pad_maximum_fusion.refs_0_), channel_id=1, source_target_pairs={{0,6},{1,7},{2,0},{3,1},{4,2},{5,3},{6,4},{7,5},{8,14},{9,15},{10,... | collective-permute-start | bytes 1572872 | tf_op jit(solution)/shard_map/ppermute | solution.py:375
  49.9 8.8 %collective-permute-start.3 = (bf16[4,128,128]{2,1,0:T(8,128)(2,1)S(1)}, bf16[4,128,128]{2,1,0:T(8,128)(2,1)S(1)}, u32[]{:S(2)}, u32[]{:S(2)}) collective-permute-start(bf16[4,128,128]{2,1,0:T(8,128)(2,1)S(1)} %get-tuple-element.26.own_ref), channel_id=1, source_target_pairs={{248,0},{0,8},{8,16},{16,24},{24,32},{32,40},{40,48},{48,56},{56,6... | collective-permute-start | bytes 393224 | tf_op jit(solution)/shard_map/ppermute | solution.py:371
  50.0 8.7 %collective-permute-start.4 = (bf16[4,128,128]{2,1,0:T(8,128)(2,1)S(1)}, bf16[4,128,128]{2,1,0:T(8,128)(2,1)S(1)}, u32[]{:S(2)}, u32[]{:S(2)}) collective-permute-start(bf16[4,128,128]{2,1,0:T(8,128)(2,1)S(1)} %get-tuple-element.26.own_ref), channel_id=1, source_target_pairs={{8,0},{16,8},{24,16},{32,24},{40,32},{48,40},{56,48},{64,56},{72,6... | collective-permute-start | bytes 393224 | tf_op jit(solution)/shard_map/ppermute | solution.py:371
  66.7 11.1 %all-to-all-start.1 = ((f32[8,88,128]{2,1,0:T(8,128)}), f32[8,88,128]{2,1,0:T(8,128)S(1)}, u32[]{:S(2)}, u32[]{:S(2)}) async-start(f32[8,88,128]{2,1,0:T(8,128)} %second.1), calls=%async_computation.1 | async-start | bytes 720896 | tf_op jit(solution)/shard_map/all_to_all | solution.py:472
  71.4 6.6 %collective-permute-start.8 = (bf16[2,2,512,128]{3,2,1,0:T(8,128)(2,1)S(1)}, bf16[2,2,512,128]{3,2,1,0:T(8,128)(2,1)S(1)}, u32[]{:S(2)}, u32[]{:S(2)}) collective-permute-start(bf16[2,2,512,128]{3,2,1,0:T(8,128)(2,1)S(1)} %pad_maximum_fusion.refs_0_), channel_id=1, source_target_pairs={{0,8},{8,0},{16,24},{24,16},{32,40},{40,32},{48,56},{56,48},{64,72... | collective-permute-start | bytes 1572872 | tf_op jit(solution)/shard_map/ppermute | solution.py:470
  71.4 12.6 %collective-permute-start.9 = (bf16[2,2,512,128]{3,2,1,0:T(8,128)(2,1)S(1)}, bf16[2,2,512,128]{3,2,1,0:T(8,128)(2,1)}, u32[]{:S(2)}, u32[]{:S(2)}) collective-permute-start(bf16[2,2,512,128]{3,2,1,0:T(8,128)(2,1)S(1)} %collective-permute-done.5.refs_1_), channel_id=1, source_target_pairs={{0,8},{8,0},{16,24},{24,16},{32,40},{40,32},{48,56},{56,48},{64,72... | collective-permute-start | bytes 1572872 | tf_op jit(solution)/shard_map/ppermute | solution.py:470
  71.9 12.1 %collective-permute-start.10 = (bf16[2,2,512,128]{3,2,1,0:T(8,128)(2,1)S(1)}, bf16[2,2,512,128]{3,2,1,0:T(8,128)(2,1)}, u32[]{:S(2)}, u32[]{:S(2)}) collective-permute-start(bf16[2,2,512,128]{3,2,1,0:T(8,128)(2,1)S(1)} %collective-permute-done.6.refs_2_), channel_id=1, source_target_pairs={{0,8},{8,0},{16,24},{24,16},{32,40},{40,32},{48,56},{56,48},{64,72... | collective-permute-start | bytes 1572872 | tf_op jit(solution)/shard_map/ppermute | solution.py:470
  71.9 12.1 %collective-permute-start.11 = (bf16[2,2,512,128]{3,2,1,0:T(8,128)(2,1)S(1)}, bf16[2,2,512,128]{3,2,1,0:T(8,128)(2,1)}, u32[]{:S(2)}, u32[]{:S(2)}) collective-permute-start(bf16[2,2,512,128]{3,2,1,0:T(8,128)(2,1)S(1)} %collective-permute-done.7.refs_3_), channel_id=1, source_target_pairs={{0,8},{8,0},{16,24},{24,16},{32,40},{40,32},{48,56},{56,48},{64,72... | collective-permute-start | bytes 1572872 | tf_op jit(solution)/shard_map/ppermute | solution.py:470
  77.8 9.3 %collective-permute-start.13 = (f32[8,128]{1,0:T(8,128)S(1)}, f32[8,128]{1,0:T(8,128)S(1)}, u32[]{:S(2)}, u32[]{:S(2)}) collective-permute-start(f32[8,128]{1,0:T(8,128)S(1)} %get-tuple-element.35), channel_id=1, source_target_pairs={{248,0},{0,8},{8,16},{16,24},{24,32},{32,40},{40,48},{48,56},{56,6... | collective-permute-start | bytes 12296 | tf_op jit(solution)/shard_map/ppermute | solution.py:371
  78.0 9.2 %collective-permute-start.12 = (f32[8,128]{1,0:T(8,128)S(1)}, f32[8,128]{1,0:T(8,128)S(1)}, u32[]{:S(2)}, u32[]{:S(2)}) collective-permute-start(f32[8,128]{1,0:T(8,128)S(1)} %get-tuple-element.34), channel_id=1, source_target_pairs={{8,0},{16,8},{24,16},{32,24},{40,32},{48,40},{56,48},{64,56},{72,6... | collective-permute-start | bytes 12296 | tf_op jit(solution)/shard_map/ppermute | solution.py:371

commit v6 on v5

--- a/solution.py
+++ b/solution.py
@@ -155,24 +155,24 @@
             target_ref[low : low + 32, :] = source_ref[n, 32 * b : 32 * b + 32, :]
 
 
-def first_kernel(
-    slot_ref, peak_in, near_in, row_in, before_ref, own_ref, after_ref,
-    scaled_ref, operand_ref, turned_ref, one_ref, half_ref,
-    peak_ref, near_ref, row_ref, flat_ref, probe_ref, shift_ref, sem,
+def prepare_kernel(
+    slot_ref, before_ref, own_ref, after_ref, probe_ref, turned_ref, table_ref,
+    flat_ref, hot_ref, sem,
 ):
     pieces = [
         pltpu.make_async_copy(ref.at[0:512], flat_ref.at[part], sem.at[part])
         for part, ref in enumerate((before_ref, own_ref, after_ref))
     ]
-    copies = [
-        pltpu.make_async_copy(peak_in, peak_ref, sem.at[3]),
-        pltpu.make_async_copy(near_in, near_ref, sem.at[4]),
-        pltpu.make_async_copy(row_in, row_ref, sem.at[5]),
-    ]
-    for copy in pieces + copies:
+    for copy in pieces:
         copy.start()
-    fill_shifts(shift_ref)
     lane = lanes()
+    for t in range(4):
+        for c in range(8):
+            for g in range(4):
+                row = 32 * t + 4 * c + g
+                hot_ref[row : row + 1, :] = (lane == slot_ref[c, 4 * g + t]).astype(F32)
+    table_ref[...] = hot_ref[...].T[0:NEAR, :]
+    probe_ref[DEAD] = jnp.zeros((128, 64), BF16)
     for part in range(3):
         pieces[part].wait()
         for c in range(8):
@@ -180,7 +180,21 @@
             if part == 1:
                 turned_ref[c] = turned
             probe_ref[8 * part + c] = turned.astype(BF16)
-    probe_ref[DEAD] = jnp.zeros((128, 64), BF16)
+
+
+def first_kernel(
+    slot_ref, peak_in, near_in, row_in, probe_ref,
+    scaled_ref, operand_ref, one_ref, half_ref, peak_ref, near_ref, row_ref, shift_ref, sem,
+):
+    copies = [
+        pltpu.make_async_copy(peak_in, peak_ref, sem.at[0]),
+        pltpu.make_async_copy(near_in, near_ref, sem.at[1]),
+        pltpu.make_async_copy(row_in, row_ref, sem.at[2]),
+    ]
+    for copy in copies:
+        copy.start()
+    fill_shifts(shift_ref)
+    lane = lanes()
     for copy in copies:
         copy.wait()
     inverse_peak = 1.0 / jnp.max(peak_ref[...])
@@ -226,8 +240,8 @@
 
 def second_kernel(
     slot_ref, near_in, row_in, scaled_ref, operand_ref, turned_ref, one_ref,
-    before_ref, own_ref, after_ref, send_ref,
-    near_ref, row_ref, half_ref, gathered_ref, pull_ref, shift_ref, sem,
+    before_ref, own_ref, after_ref, table_ref, send_ref,
+    near_ref, row_ref, half_ref, gathered_ref, near_pull_ref, own_pull_ref, shift_ref, sem,
 ):
     copies = [
         pltpu.make_async_copy(near_in, near_ref, sem.at[0]),
@@ -242,7 +256,6 @@
             half_ref[8 * part + pair] = ref[pair, :, 0:64]
             half_ref[8 * part + pair + 4] = ref[pair, :, 64:128]
     half_ref[DEAD] = jnp.zeros((128, 64), BF16)
-    pull_ref[...] = jnp.zeros_like(pull_ref)
     for copy in copies:
         copy.wait()
     on_row = lax.broadcasted_iota(jnp.int32, (32, 128), 0) == lax.broadcasted_iota(
@@ -276,25 +289,38 @@
                 pulls = pair_pulls(sample, columns, rows)
                 for x in range(3):
                     own[x] = own[x] + pulls[x]
-                    folded = jnp.sum(pulls[x].reshape(4, 8, 128), axis=0)
-                    for t in range(4):
-                        n = slot_ref[c, 4 * g + t]
-                        pull_ref[n, x] = pull_ref[n, x] - jnp.where(lane // 32 == t, folded, 0.0)
+                    near_pull_ref[x, pl.ds(4 * c + g, 1), :] = jnp.sum(
+                        pulls[x], axis=0, keepdims=True
+                    )
             for x in range(3):
                 whole = jnp.broadcast_to(jnp.sum(own[x], axis=1, keepdims=True), (32, 128))
-                placed = jnp.where(on_row, whole, 0.0)
-                pull_ref[8 + c, x] = pull_ref[8 + c, x] + jnp.sum(
-                    placed.reshape(4, 8, 128), axis=0
+                own_pull_ref[x, pl.ds(c, 1), :] = jnp.sum(
+                    jnp.where(on_row, whole, 0.0), axis=0, keepdims=True
                 )
         return carry
 
     lax.fori_loop(0, 4, one_pair, 0)
 
-    total = jnp.sum(pull_ref[0:24], axis=2).reshape(72, 128)
-    total = total + pltpu.roll(total, 64, 1)
-    total = total + pltpu.roll(total, 32, 1)
-    total = (total * (1.0 / 512.0)).reshape(24, 3, 128)
-    joined = jnp.where(lane < 32, total[:, 0], jnp.where(lane < 64, total[:, 1], total[:, 2]))
+    stacked = jnp.concatenate(
+        [
+            jnp.concatenate(
+                [jnp.where(lane // 32 == t, near_pull_ref[x], 0.0) for x in range(3)], axis=1
+            )
+            for t in range(4)
+        ],
+        axis=0,
+    )
+    gathered = jnp.dot(
+        table_ref[...], stacked, precision=lax.Precision.HIGHEST, preferred_element_type=F32
+    )
+    total = [-gathered[:, 128 * x : 128 * x + 128] for x in range(3)]
+    nothing = jnp.zeros((8, 128), F32)
+    for x in range(3):
+        v = total[x] + jnp.concatenate([nothing, own_pull_ref[x], nothing], axis=0)
+        v = v + pltpu.roll(v, 64, 1)
+        v = v + pltpu.roll(v, 32, 1)
+        total[x] = v * (1.0 / 512.0)
+    joined = jnp.where(lane < 32, total[0], jnp.where(lane < 64, total[1], total[2]))
     for q in range(8):
         send_ref[q, 64:88, :] = joined
 
@@ -384,9 +410,6 @@
     own = jnp.concatenate([probes.reshape(512, 128), coords.reshape(24, 128)])
     before, after = both(own)
     core = space_rank % 2
-    pair = jnp.stack([jnp.where(core == 0, before, after)[:512], own[:512]])
-    across = along_probe(pair, lambda i: i ^ 1)
-
     present = neighbours >= 0
     slot = (neighbours // 8 - space_rank + 1) % space_count * 8 + neighbours % 8
     slot = jnp.pad(jnp.where(present, slot, DEAD), ((0, 0), (0, 1)), constant_values=DEAD)
@@ -413,44 +436,60 @@
         compiler_params=params(4),
         name="spectral",
     )(slot, before, own, after)
+    peak, held = lax.optimization_barrier((peak, (before, own, after)))
     peaks = lax.all_to_all(peak, "space", 0, 0, tiled=True)
-    peaks, pair, across = lax.optimization_barrier((peaks, pair, across))
-    quad = jnp.stack([pair, across])
-    pieces = [quad] + [
-        along_probe(quad, lambda i, distance=distance: (i + 2 * distance) % 8)
-        for distance in range(1, 4)
-    ]
-
-    scaled, operand, turned, one, half = pl.pallas_call(
+    probe_turned, turned, table = pl.pallas_call(
+        prepare_kernel,
+        out_shape=(
+            jax.ShapeDtypeStruct((NEAR + 1, 128, 64), BF16),
+            jax.ShapeDtypeStruct((8, 128, 64), F32),
+            jax.ShapeDtypeStruct((NEAR, 128), F32),
+        ),
+        in_specs=[SMEM] + [HBM] * 3,
+        out_specs=(WHOLE,) * 3,
+        scratch_shapes=[
+            pltpu.VMEM((3, 512, 128), BF16),
+            pltpu.VMEM((128, 128), F32),
+            pltpu.SemaphoreType.DMA((3,)),
+        ],
+        compiler_params=params(4),
+        name="prepare",
+    )(slot, *held)
+    pair = jnp.stack([jnp.where(core == 0, held[0], held[2])[:512], held[1][:512]])
+    peaks, pair, probe_turned = lax.optimization_barrier((peaks, pair, probe_turned))
+    across = along_probe(pair, lambda i: i ^ 1)
+    scaled, operand, one, half = pl.pallas_call(
         first_kernel,
         out_shape=(
             jax.ShapeDtypeStruct((8, 128, 2048), BF16),
             jax.ShapeDtypeStruct((8, 2048, 64), BF16),
             jax.ShapeDtypeStruct((8, 128, 64), F32),
-            jax.ShapeDtypeStruct((8, 128, 64), F32),
             jax.ShapeDtypeStruct((4, 128, 128), BF16),
         ),
-        in_specs=[SMEM] + [HBM] * 6,
-        out_specs=(WHOLE,) * 5,
+        in_specs=[SMEM] + [HBM] * 3 + [WHOLE],
+        out_specs=(WHOLE,) * 4,
         scratch_shapes=[
             pltpu.VMEM((space_count, 128), F32),
             pltpu.VMEM((NEAR + 1, 8, 128), F32),
             pltpu.VMEM((8, 3, 32, 128), F32),
-            pltpu.VMEM((3, 512, 128), BF16),
-            pltpu.VMEM((NEAR + 1, 128, 64), BF16),
             pltpu.VMEM((4, 8, 128), F32),
-            pltpu.SemaphoreType.DMA((6,)),
+            pltpu.SemaphoreType.DMA((3,)),
         ],
         cost_estimate=LIGHT,
         compiler_params=params(16),
         name="first",
-    )(slot, peaks, near, rows, before, own, after)
+    )(slot, peaks, near, rows, probe_turned)
     half_before, half_after = both(half)
-
+    half, pair, across = lax.optimization_barrier((half, pair, across))
+    quad = jnp.stack([pair, across])
+    pieces = [quad] + [
+        along_probe(quad, lambda i, distance=distance: (i + 2 * distance) % 8)
+        for distance in range(1, 4)
+    ]
     send = pl.pallas_call(
         second_kernel,
         out_shape=jax.ShapeDtypeStruct((8, 88, 128), F32),
-        in_specs=[SMEM, HBM, HBM] + [WHOLE] * 7,
+        in_specs=[SMEM, HBM, HBM] + [WHOLE] * 8,
         out_specs=WHOLE,
         cost_estimate=LIGHT,
         scratch_shapes=[
@@ -458,13 +497,14 @@
             pltpu.VMEM((8, 3, 32, 128), F32),
             pltpu.VMEM((NEAR + 1, 128, 64), BF16),
             pltpu.VMEM((2, 2048, 64), BF16),
-            pltpu.VMEM((NEAR + 1, 3, 8, 128), F32),
+            pltpu.VMEM((3, 32, 128), F32),
+            pltpu.VMEM((3, 8, 128), F32),
             pltpu.VMEM((4, 8, 128), F32),
             pltpu.SemaphoreType.DMA((2,)),
         ],
         compiler_params=params(16),
         name="second",
-    )(slot, near, rows, scaled, operand, turned, one, half_before, half, half_after)
+    )(slot, near, rows, scaled, operand, turned, one, half_before, half, half_after, table)
     send, pieces = lax.optimization_barrier((send, pieces))
     swapped = [
         lax.ppermute(piece, "space", [(i, i ^ 1) for i in range(space_count)]) for piece in pieces

time: 88.3 us -> 93 us (1.053)
  blocking collectives: 18.6 us -> 0 us
  waiting for transfers between devices: 11.6 us -> 28 us
  starting transfers between devices: 33.1 us -> 40.3 us
    all_to_all x1 -> x0, blocking collectives: 18.6 us -> none  [per_device(): peaks = lax.all_to_all(peak, 'space', 0, 0, tiled=True)]
    all_to_all x0 -> x1, starting transfers between devices: none -> 9.08 us  [per_device(): peaks = lax.all_to_all(peak, 'space', 0, 0, tiled=True)]
    ppermute x4, waiting for transfers between devices: 0.23 us -> 8.31 us  [along_probe(): return lax.ppermute(block, 'probe', [(i, target(i)) for i in range(8)])]
    all_to_all x0 -> x1, waiting for transfers between devices: none -> 7.96 us  [per_device(): peaks = lax.all_to_all(peak, 'space', 0, 0, tiled=True)]
    ppermute x4, starting transfers between devices: 7.07 us -> 5.28 us  [along_probe(): return lax.ppermute(block, 'probe', [(i, target(i)) for i in range(8)])]
    pallas_call x0 -> x1, Pallas kernels: none -> 1.67 us  [per_device(): pl.pallas_call(prepare_kernel, out_shape=(jax.ShapeDtypeStruct((NEAR + 1,...]
    pallas_call x1, Pallas kernels: 5.37 us -> 4.43 us  [per_device(): pl.pallas_call(first_kernel, out_shape=(jax.ShapeDtypeStruct((8, 128, 204...]
  transfers between devices with their start and end apart: 15 -> 16, of which waited for: 5 -> 8; matrix products, arithmetic and copies ran while one was open for 1% -> 1% of each run, Pallas kernels for 22% -> 18%
where the time goes in v6:
time: 93 us; the launch traced here: 92.7 us
  starting transfers between devices  40.3 us (43%)
  waiting for transfers between devices  28 us (30%)
  Pallas kernels  20.3 us (22%)
  other arithmetic  2.43 us (3%)
    ppermute x6, starting transfers between devices, around(): lax.ppermute(block, 'space', [((i - distance) % size, i) for i in range(s...  20.3 us
    all_to_all x1, starting transfers between devices, per_device(): peaks = lax.all_to_all(peak, 'space', 0, 0, tiled=True)  9.08 us
    ppermute x4, waiting for transfers between devices, along_probe(): return lax.ppermute(block, 'probe', [(i, target(i)) for i in range(8)])  8.31 us
    all_to_all x1, waiting for transfers between devices, per_device(): peaks = lax.all_to_all(peak, 'space', 0, 0, tiled=True)  7.96 us
    pallas_call x1, Pallas kernels, per_device(): pl.pallas_call(second_kernel, out_shape=jax.ShapeDtypeStruct((8, 88, 128)...  7.32 us
    ppermute x6, waiting for transfers between devices, around(): lax.ppermute(block, 'space', [((i - distance) % size, i) for i in range(s...  6.29 us
    all_to_all x1, waiting for transfers between devices, per_device(): received = lax.all_to_all(send, 'probe', 0, 0, tiled=True)  5.44 us
    ppermute x4, starting transfers between devices, along_probe(): return lax.ppermute(block, 'probe', [(i, target(i)) for i in range(8)])  5.28 us
  transfers between devices with their start and end apart: 16, of which 8 were waited for; matrix products, arithmetic and copies ran while one was open for 1% of the time, Pallas kernels for 18%

profile of v6, /device:TPU:2, one launch (start us, length us, event | category | flops | bytes accessed | tf_op | source)
XLA Modules:
  0.0 92.7 jit_solution(5435799989584422390)
XLA Ops:
  0.6 0.7 pad_bitcast_fusion
  1.3 0.9 pad_maximum_fusion.2.own_ref
  2.2 0.1 collective-permute-start
  2.3 8.3 %collective-permute-start.1 = (bf16[536,128]{1,0:T(8,128)(2,1)S(1)}, bf16[536,128]{1,0:T(8,128)(2,1)S(1)}, u32[]{:S(2)}, u32[]{:S(2)}) collective-permute-start(bf16[536,128]{1,0:T(8,128)(2,1)S(1)} %pad_maximum_fusion.2.own_ref), channel_id=1, source_target_pairs={{8,0},{16,8},{24,16},{32,24},{40,32},{48,40},{56,48},{64,56},{72,6... | collective-permute-start | bytes 411656 | tf_op jit(solution)/shard_map/ppermute | solution.py:397
  10.6 0.7 fusion.6
  11.3 2.0 %collective-permute-done.before_ref = bf16[536,128]{1,0:T(8,128)(2,1)S(1)} collective-permute-done((bf16[536,128]{1,0:T(8,128)(2,1)S(1)}, bf16[536,128]{1,0:T(8,128)(2,1)S(1)}, u32[]{:S(2)}, u32[]{:S(2)}) %collective-permute-start) | collective-permute-done | bytes 137248 | tf_op jit(solution)/shard_map/ppermute | solution.py:397
  13.3 1.3 %collective-permute-done.1.after_ref = bf16[536,128]{1,0:T(8,128)(2,1)S(1)} collective-permute-done((bf16[536,128]{1,0:T(8,128)(2,1)S(1)}, bf16[536,128]{1,0:T(8,128)(2,1)S(1)}, u32[]{:S(2)}, u32[]{:S(2)}) %collective-permute-start.1) | collective-permute-done | bytes 137248 | tf_op jit(solution)/shard_map/ppermute | solution.py:397
  14.7 3.9 %spectral.1 = (f32[25,8,128]{2,1,0:T(8,128)S(1)}, f32[8,3,32,128]{3,2,1,0:T(8,128)S(1)}, f32[32,128]{1,0:T(8,128)}) custom-call(s32[8,16]{1,0:T(8,128)S(1)} %pad.8.slot_ref, bf16[536,128]{1,0:T(8,128)(2,1)S(1)} %collective-permute-done.before_ref, bf16[536,128]{1,0:T(8,128)(2,1)S(1)} %pad_maximum_fusion.2.own_ref, ...), custom_call_target="tpu_custom_call" | custom-call | bytes 60000000 | tf_op jit(solution)/shard_map/spectral/pallas_call | solution.py:417
  18.6 9.1 %all-to-all-start = ((f32[32,1,128]{2,1,0:T(1,128)}), f32[32,1,128]{2,1,0:T(1,128)S(1)}, u32[]{:S(2)}, u32[]{:S(2)}) async-start(f32[32,1,128]{2,1,0:T(1,128)} %bitcast.6), calls=%async_computation | async-start | bytes 32768 | tf_op jit(solution)/shard_map/all_to_all | solution.py:440
  27.7 1.7 %prepare.1 = (bf16[25,128,64]{2,1,0:T(8,128)(2,1)S(1)}, f32[8,128,64]{2,1,0:T(8,128)S(1)}, f32[24,128]{1,0:T(8,128)S(1)}) custom-call(s32[8,16]{1,0:T(8,128)S(1)} %pad.8.slot_ref, bf16[536,128]{1,0:T(8,128)(2,1)S(1)} %collective-permute-done.before_ref, bf16[536,128]{1,0:T(8,128)(2,1)S(1)} %pad_maximum_fusion.2.own_ref, ...), custom_call_target="tpu_custom_call" | custom-call | tf_op jit(solution)/shard_map/prepare/pallas_call | solution.py:441
  29.4 8.0 %all-to-all-done = f32[32,1,128]{2,1,0:T(1,128)S(1)} async-done(((f32[32,1,128]{2,1,0:T(1,128)}), f32[32,1,128]{2,1,0:T(1,128)S(1)}, u32[]{:S(2)}, u32[]{:S(2)}) %all-to-all-start) | async-done | bytes 16416 | tf_op jit(solution)/shard_map/all_to_all | solution.py:440
  37.4 0.4 collective-permute-start.3
  37.8 4.4 %first.1 = (bf16[8,128,2048]{2,1,0:T(8,128)(2,1)S(1)}, bf16[8,2048,64]{2,1,0:T(8,128)(2,1)S(1)}, f32[8,128,64]{2,1,0:T(8,128)S(1)}, bf16[4,128,128]{2,1,0:T(8,128)(2,1)S(1)}) custom-call(s32[8,16]{1,0:T(8,128)S(1)} %pad.8.slot_ref, f32[32,128]{1,0:T(8,128)S(1)} %bitcast.25, f32[25,8,128]{2,1,0:T(8,128)S(1)} %get-tuple-element.27.near_in, ...), custom_call_target="tpu_custom_call" | custom-call | tf_op jit(solution)/shard_map/first/pallas_call | solution.py:461
  42.2 3.2 %collective-permute-done.3 = bf16[2,512,128]{2,1,0:T(8,128)(2,1)S(1)} collective-permute-done((bf16[2,512,128]{2,1,0:T(8,128)(2,1)S(1)}, bf16[2,512,128]{2,1,0:T(8,128)(2,1)S(1)}, u32[]{:S(2)}, u32[]{:S(2)}) %collective-permute-start.3) | collective-permute-done | bytes 262176 | tf_op jit(solution)/shard_map/ppermute | solution.py:401
  45.5 0.1 pad_maximum_fusion.refs_0_
  45.5 1.6 %collective-permute-start.5 = (bf16[2,2,512,128]{3,2,1,0:T(8,128)(2,1)S(1)}, bf16[2,2,512,128]{3,2,1,0:T(8,128)(2,1)S(1)}, u32[]{:S(2)}, u32[]{:S(2)}) collective-permute-start(bf16[2,2,512,128]{3,2,1,0:T(8,128)(2,1)S(1)} %pad_maximum_fusion.refs_0_), channel_id=1, source_target_pairs={{0,2},{1,3},{2,4},{3,5},{4,6},{5,7},{6,0},{7,1},{8,10},{9,11},{10,... | collective-permute-start | bytes 1572872 | tf_op jit(solution)/shard_map/ppermute | solution.py:401
  47.1 1.1 %collective-permute-start.6 = (bf16[2,2,512,128]{3,2,1,0:T(8,128)(2,1)S(1)}, bf16[2,2,512,128]{3,2,1,0:T(8,128)(2,1)S(1)}, u32[]{:S(2)}, u32[]{:S(2)}) collective-permute-start(bf16[2,2,512,128]{3,2,1,0:T(8,128)(2,1)S(1)} %pad_maximum_fusion.refs_0_), channel_id=1, source_target_pairs={{0,4},{1,5},{2,6},{3,7},{4,0},{5,1},{6,2},{7,3},{8,12},{9,13},{10,... | collective-permute-start | bytes 1572872 | tf_op jit(solution)/shard_map/ppermute | solution.py:401
  48.2 2.2 %collective-permute-start.7 = (bf16[2,2,512,128]{3,2,1,0:T(8,128)(2,1)S(1)}, bf16[2,2,512,128]{3,2,1,0:T(8,128)(2,1)S(1)}, u32[]{:S(2)}, u32[]{:S(2)}) collective-permute-start(bf16[2,2,512,128]{3,2,1,0:T(8,128)(2,1)S(1)} %pad_maximum_fusion.refs_0_), channel_id=1, source_target_pairs={{0,6},{1,7},{2,0},{3,1},{4,2},{5,3},{6,4},{7,5},{8,14},{9,15},{10,... | collective-permute-start | bytes 1572872 | tf_op jit(solution)/shard_map/ppermute | solution.py:401
  50.3 0.0 collective-permute-start.2
  50.3 6.0 %collective-permute-start.4 = (bf16[4,128,128]{2,1,0:T(8,128)(2,1)S(1)}, bf16[4,128,128]{2,1,0:T(8,128)(2,1)S(1)}, u32[]{:S(2)}, u32[]{:S(2)}) collective-permute-start(bf16[4,128,128]{2,1,0:T(8,128)(2,1)S(1)} %get-tuple-element.43.own_ref), channel_id=1, source_target_pairs={{8,0},{16,8},{24,16},{32,24},{40,32},{48,40},{56,48},{64,56},{72,6... | collective-permute-start | bytes 393224 | tf_op jit(solution)/shard_map/ppermute | solution.py:397
  56.3 2.7 %collective-permute-done.2.before_ref = bf16[4,128,128]{2,1,0:T(8,128)(2,1)S(1)} collective-permute-done((bf16[4,128,128]{2,1,0:T(8,128)(2,1)S(1)}, bf16[4,128,128]{2,1,0:T(8,128)(2,1)S(1)}, u32[]{:S(2)}, u32[]{:S(2)}) %collective-permute-start.2) | collective-permute-done | bytes 131104 | tf_op jit(solution)/shard_map/ppermute | solution.py:397
  59.1 0.2 collective-permute-done.4.after_ref
  59.3 7.3 %second.1 = f32[8,88,128]{2,1,0:T(8,128)} custom-call(s32[8,16]{1,0:T(8,128)S(1)} %pad.8.slot_ref, f32[25,8,128]{2,1,0:T(8,128)S(1)} %get-tuple-element.27.near_in, f32[8,3,32,128]{3,2,1,0:T(8,128)S(1)} %get-tuple-element.28.row_in, bf16[8,128,2048]{2,1,0:T(8,128)(2,1)S(1)} %get-tuple-element.37.scaled_ref, ...), custom_call_target="tpu_custom_call" | custom-call | tf_op jit(solution)/shard_map/second/pallas_call | solution.py:489
  66.6 0.0 collective-permute-done.5.refs_1_
  66.6 0.0 collective-permute-done.6.refs_2_
  66.6 5.1 %collective-permute-done.7.refs_3_ = bf16[2,2,512,128]{3,2,1,0:T(8,128)(2,1)S(1)} collective-permute-done((bf16[2,2,512,128]{3,2,1,0:T(8,128)(2,1)S(1)}, bf16[2,2,512,128]{3,2,1,0:T(8,128)(2,1)S(1)}, u32[]{:S(2)}, u32[]{:S(2)}) %collective-permute-start.7) | collective-permute-done | bytes 524320 | tf_op jit(solution)/shard_map/ppermute | solution.py:401
  71.7 4.6 %all-to-all-start.1 = ((f32[8,88,128]{2,1,0:T(8,128)}), f32[8,88,128]{2,1,0:T(8,128)S(1)}, u32[]{:S(2)}, u32[]{:S(2)}) async-start(f32[8,88,128]{2,1,0:T(8,128)} %second.1), calls=%async_computation.1 | async-start | bytes 720896 | tf_op jit(solution)/shard_map/all_to_all | solution.py:512
  76.3 0.0 collective-permute-start.8
  76.3 0.5 collective-permute-start.9
  76.8 0.0 collective-permute-start.10
  76.8 0.5 collective-permute-start.11
  77.3 5.4 %all-to-all-done.1.received_ref = f32[8,88,128]{2,1,0:T(8,128)S(1)} async-done(((f32[8,88,128]{2,1,0:T(8,128)}), f32[8,88,128]{2,1,0:T(8,128)S(1)}, u32[]{:S(2)}, u32[]{:S(2)}) %all-to-all-start.1) | async-done | bytes 360480 | tf_op jit(solution)/shard_map/all_to_all | solution.py:512
  82.8 0.1 collective-permute-start.13
  82.9 0.0 collective-permute-done.8.refs_4_
  82.9 5.9 %collective-permute-start.12 = (f32[8,128]{1,0:T(8,128)S(1)}, f32[8,128]{1,0:T(8,128)S(1)}, u32[]{:S(2)}, u32[]{:S(2)}) collective-permute-start(f32[8,128]{1,0:T(8,128)S(1)} %get-tuple-element.52), channel_id=1, source_target_pairs={{8,0},{16,8},{24,16},{32,24},{40,32},{48,40},{56,48},{64,56},{72,6... | collective-permute-start | bytes 12296 | tf_op jit(solution)/shard_map/ppermute | solution.py:397
  88.9 0.1 pad_add_fusion.place_ref
  88.9 0.0 collective-permute-done.9.refs_5_
  88.9 0.0 collective-permute-done.10.refs_6_
  88.9 0.0 collective-permute-done.11.refs_7_
  88.9 3.0 %sample.1 = bf16[16,15,8,128]{3,2,1,0:T(8,128)(2,1)} custom-call(s32[8,16]{1,0:T(8,128)S(1)} %pad.8.slot_ref, s32[2]{0:T(128)S(1)} %pad_add_fusion.place_ref, f32[8,88,128]{2,1,0:T(8,128)S(1)} %all-to-all-done.1.received_ref, bf16[2,2,512,128]{3,2,1,0:T(8,128)(2,1)S(1)} %pad_maximum_fusion.refs_0_, ...), custom_call_target="tpu_custom_call" | custom-call | tf_op jit(solution)/shard_map/sample/pallas_call | solution.py:517
  92.0 0.0 collective-permute-done.13
  92.0 0.0 collective-permute-done.12
  92.0 0.1 slice_bitcast_fusion.3
  92.0 0.6 maximum_bitcast_fusion
  (6 shorter events, 0.1 us)
Async XLA Ops:
  2.2 11.1 %collective-permute-start = (bf16[536,128]{1,0:T(8,128)(2,1)S(1)}, bf16[536,128]{1,0:T(8,128)(2,1)S(1)}, u32[]{:S(2)}, u32[]{:S(2)}) collective-permute-start(bf16[536,128]{1,0:T(8,128)(2,1)S(1)} %pad_maximum_fusion.2.own_ref), channel_id=1, source_target_pairs={{248,0},{0,8},{8,16},{16,24},{24,32},{32,40},{40,48},{48,56},{56,6... | collective-permute-start | bytes 411656 | tf_op jit(solution)/shard_map/ppermute | solution.py:397
  2.3 12.3 %collective-permute-start.1 = (bf16[536,128]{1,0:T(8,128)(2,1)S(1)}, bf16[536,128]{1,0:T(8,128)(2,1)S(1)}, u32[]{:S(2)}, u32[]{:S(2)}) collective-permute-start(bf16[536,128]{1,0:T(8,128)(2,1)S(1)} %pad_maximum_fusion.2.own_ref), channel_id=1, source_target_pairs={{8,0},{16,8},{24,16},{32,24},{40,32},{48,40},{56,48},{64,56},{72,6... | collective-permute-start | bytes 411656 | tf_op jit(solution)/shard_map/ppermute | solution.py:397
  18.6 18.8 %all-to-all-start = ((f32[32,1,128]{2,1,0:T(1,128)}), f32[32,1,128]{2,1,0:T(1,128)S(1)}, u32[]{:S(2)}, u32[]{:S(2)}) async-start(f32[32,1,128]{2,1,0:T(1,128)} %bitcast.6), calls=%async_computation | async-start | bytes 32768 | tf_op jit(solution)/shard_map/all_to_all | solution.py:440
  37.4 8.1 %collective-permute-start.3 = (bf16[2,512,128]{2,1,0:T(8,128)(2,1)S(1)}, bf16[2,512,128]{2,1,0:T(8,128)(2,1)S(1)}, u32[]{:S(2)}, u32[]{:S(2)}) collective-permute-start(bf16[2,512,128]{2,1,0:T(8,128)(2,1)S(1)} %pad_maximum_fusion.1), channel_id=1, source_target_pairs={{0,1},{1,0},{2,3},{3,2},{4,5},{5,4},{6,7},{7,6},{8,9},{9,8},{10,11... | collective-permute-start | bytes 786440 | tf_op jit(solution)/shard_map/ppermute | solution.py:401
  45.5 21.1 %collective-permute-start.5 = (bf16[2,2,512,128]{3,2,1,0:T(8,128)(2,1)S(1)}, bf16[2,2,512,128]{3,2,1,0:T(8,128)(2,1)S(1)}, u32[]{:S(2)}, u32[]{:S(2)}) collective-permute-start(bf16[2,2,512,128]{3,2,1,0:T(8,128)(2,1)S(1)} %pad_maximum_fusion.refs_0_), channel_id=1, source_target_pairs={{0,2},{1,3},{2,4},{3,5},{4,6},{5,7},{6,0},{7,1},{8,10},{9,11},{10,... | collective-permute-start | bytes 1572872 | tf_op jit(solution)/shard_map/ppermute | solution.py:401
  47.1 19.5 %collective-permute-start.6 = (bf16[2,2,512,128]{3,2,1,0:T(8,128)(2,1)S(1)}, bf16[2,2,512,128]{3,2,1,0:T(8,128)(2,1)S(1)}, u32[]{:S(2)}, u32[]{:S(2)}) collective-permute-start(bf16[2,2,512,128]{3,2,1,0:T(8,128)(2,1)S(1)} %pad_maximum_fusion.refs_0_), channel_id=1, source_target_pairs={{0,4},{1,5},{2,6},{3,7},{4,0},{5,1},{6,2},{7,3},{8,12},{9,13},{10,... | collective-permute-start | bytes 1572872 | tf_op jit(solution)/shard_map/ppermute | solution.py:401
  48.2 23.5 %collective-permute-start.7 = (bf16[2,2,512,128]{3,2,1,0:T(8,128)(2,1)S(1)}, bf16[2,2,512,128]{3,2,1,0:T(8,128)(2,1)S(1)}, u32[]{:S(2)}, u32[]{:S(2)}) collective-permute-start(bf16[2,2,512,128]{3,2,1,0:T(8,128)(2,1)S(1)} %pad_maximum_fusion.refs_0_), channel_id=1, source_target_pairs={{0,6},{1,7},{2,0},{3,1},{4,2},{5,3},{6,4},{7,5},{8,14},{9,15},{10,... | collective-permute-start | bytes 1572872 | tf_op jit(solution)/shard_map/ppermute | solution.py:401
  50.3 8.7 %collective-permute-start.2 = (bf16[4,128,128]{2,1,0:T(8,128)(2,1)S(1)}, bf16[4,128,128]{2,1,0:T(8,128)(2,1)S(1)}, u32[]{:S(2)}, u32[]{:S(2)}) collective-permute-start(bf16[4,128,128]{2,1,0:T(8,128)(2,1)S(1)} %get-tuple-element.43.own_ref), channel_id=1, source_target_pairs={{248,0},{0,8},{8,16},{16,24},{24,32},{32,40},{40,48},{48,56},{56,6... | collective-permute-start | bytes 393224 | tf_op jit(solution)/shard_map/ppermute | solution.py:397
  50.3 8.9 %collective-permute-start.4 = (bf16[4,128,128]{2,1,0:T(8,128)(2,1)S(1)}, bf16[4,128,128]{2,1,0:T(8,128)(2,1)S(1)}, u32[]{:S(2)}, u32[]{:S(2)}) collective-permute-start(bf16[4,128,128]{2,1,0:T(8,128)(2,1)S(1)} %get-tuple-element.43.own_ref), channel_id=1, source_target_pairs={{8,0},{16,8},{24,16},{32,24},{40,32},{48,40},{56,48},{64,56},{72,6... | collective-permute-start | bytes 393224 | tf_op jit(solution)/shard_map/ppermute | solution.py:397
  71.7 11.1 %all-to-all-start.1 = ((f32[8,88,128]{2,1,0:T(8,128)}), f32[8,88,128]{2,1,0:T(8,128)S(1)}, u32[]{:S(2)}, u32[]{:S(2)}) async-start(f32[8,88,128]{2,1,0:T(8,128)} %second.1), calls=%async_computation.1 | async-start | bytes 720896 | tf_op jit(solution)/shard_map/all_to_all | solution.py:512
  76.3 6.6 %collective-permute-start.8 = (bf16[2,2,512,128]{3,2,1,0:T(8,128)(2,1)S(1)}, bf16[2,2,512,128]{3,2,1,0:T(8,128)(2,1)S(1)}, u32[]{:S(2)}, u32[]{:S(2)}) collective-permute-start(bf16[2,2,512,128]{3,2,1,0:T(8,128)(2,1)S(1)} %pad_maximum_fusion.refs_0_), channel_id=1, source_target_pairs={{0,8},{8,0},{16,24},{24,16},{32,40},{40,32},{48,56},{56,48},{64,72... | collective-permute-start | bytes 1572872 | tf_op jit(solution)/shard_map/ppermute | solution.py:510
  76.3 12.6 %collective-permute-start.9 = (bf16[2,2,512,128]{3,2,1,0:T(8,128)(2,1)S(1)}, bf16[2,2,512,128]{3,2,1,0:T(8,128)(2,1)S(1)}, u32[]{:S(2)}, u32[]{:S(2)}) collective-permute-start(bf16[2,2,512,128]{3,2,1,0:T(8,128)(2,1)S(1)} %collective-permute-done.5.refs_1_), channel_id=1, source_target_pairs={{0,8},{8,0},{16,24},{24,16},{32,40},{40,32},{48,56},{56,48},{64,72... | collective-permute-start | bytes 1572872 | tf_op jit(solution)/shard_map/ppermute | solution.py:510
  76.8 12.1 %collective-permute-start.10 = (bf16[2,2,512,128]{3,2,1,0:T(8,128)(2,1)S(1)}, bf16[2,2,512,128]{3,2,1,0:T(8,128)(2,1)}, u32[]{:S(2)}, u32[]{:S(2)}) collective-permute-start(bf16[2,2,512,128]{3,2,1,0:T(8,128)(2,1)S(1)} %collective-permute-done.6.refs_2_), channel_id=1, source_target_pairs={{0,8},{8,0},{16,24},{24,16},{32,40},{40,32},{48,56},{56,48},{64,72... | collective-permute-start | bytes 1572872 | tf_op jit(solution)/shard_map/ppermute | solution.py:510
  76.8 12.1 %collective-permute-start.11 = (bf16[2,2,512,128]{3,2,1,0:T(8,128)(2,1)S(1)}, bf16[2,2,512,128]{3,2,1,0:T(8,128)(2,1)}, u32[]{:S(2)}, u32[]{:S(2)}) collective-permute-start(bf16[2,2,512,128]{3,2,1,0:T(8,128)(2,1)S(1)} %collective-permute-done.7.refs_3_), channel_id=1, source_target_pairs={{0,8},{8,0},{16,24},{24,16},{32,40},{40,32},{48,56},{56,48},{64,72... | collective-permute-start | bytes 1572872 | tf_op jit(solution)/shard_map/ppermute | solution.py:510
  82.8 9.1 %collective-permute-start.13 = (f32[8,128]{1,0:T(8,128)S(1)}, f32[8,128]{1,0:T(8,128)S(1)}, u32[]{:S(2)}, u32[]{:S(2)}) collective-permute-start(f32[8,128]{1,0:T(8,128)S(1)} %get-tuple-element.53), channel_id=1, source_target_pairs={{248,0},{0,8},{8,16},{16,24},{24,32},{32,40},{40,48},{48,56},{56,6... | collective-permute-start | bytes 12296 | tf_op jit(solution)/shard_map/ppermute | solution.py:397
  82.9 9.1 %collective-permute-start.12 = (f32[8,128]{1,0:T(8,128)S(1)}, f32[8,128]{1,0:T(8,128)S(1)}, u32[]{:S(2)}, u32[]{:S(2)}) collective-permute-start(f32[8,128]{1,0:T(8,128)S(1)} %get-tuple-element.52), channel_id=1, source_target_pairs={{8,0},{16,8},{24,16},{32,24},{40,32},{48,40},{56,48},{64,56},{72,6... | collective-permute-start | bytes 12296 | tf_op jit(solution)/shard_map/ppermute | solution.py:397

commit v7 on v6

--- a/solution.py
+++ b/solution.py
@@ -30,7 +30,6 @@
 BF16 = jnp.bfloat16
 WHOLE = pl.BlockSpec()
 SMEM = pl.BlockSpec(memory_space=pltpu.SMEM)
-HBM = pl.BlockSpec(memory_space=pltpu.MemorySpace.HBM)
 HEAVY = pl.CostEstimate(flops=0, transcendentals=0, bytes_accessed=60_000_000)
 LIGHT = pl.CostEstimate(flops=0, transcendentals=0, bytes_accessed=0)
 
@@ -87,20 +86,12 @@
 
 
 def spectral_kernel(
-    slot_ref, before_ref, own_ref, after_ref, near_out, row_out, peak_out,
-    coord_ref, near_ref, row_ref, peak_ref, shift_ref, in_sem, out_sem,
+    slot_ref, before_ref, own_ref, after_ref, near_ref, row_ref, peak_ref, shift_ref
 ):
-    copies = [
-        pltpu.make_async_copy(ref.at[512:536], coord_ref.at[part], in_sem.at[part])
-        for part, ref in enumerate((before_ref, own_ref, after_ref))
-    ]
-    for copy in copies:
-        copy.start()
     fill_shifts(shift_ref)
-    for part in range(3):
-        copies[part].wait()
+    for part, ref in enumerate((before_ref, own_ref, after_ref)):
         for x in range(3):
-            coords = coord_ref[part, 8 * x : 8 * x + 8, 0:32].astype(F32)
+            coords = ref[512 + 8 * x : 520 + 8 * x, 0:32].astype(F32)
             wide = jnp.concatenate([coords] * 4, axis=1)
             for n in range(8):
                 near_ref[8 * part + n, x : x + 1, :] = wide[n : n + 1, :]
@@ -109,12 +100,6 @@
                 for c in range(8):
                     row_ref[c, x] = jnp.broadcast_to(upright[0:32, c : c + 1], (32, 128))
     near_ref[DEAD] = jnp.full((8, 128), FAR, F32)
-    kept = [
-        pltpu.make_async_copy(near_ref, near_out, out_sem.at[0]),
-        pltpu.make_async_copy(row_ref, row_out, out_sem.at[1]),
-    ]
-    for copy in kept:
-        copy.start()
     lane = lanes()
 
     def one_cluster(c, peak):
@@ -138,13 +123,10 @@
             peak = jnp.maximum(peak, jnp.sum(v, axis=1, keepdims=True))
         return peak
 
-    peak = lax.fori_loop(0, 8, one_cluster, jnp.zeros((32, 1), F32))
+    peak = jnp.zeros((32, 1), F32)
+    for c in range(8):
+        peak = one_cluster(c, peak)
     peak_ref[...] = jnp.broadcast_to(jnp.max(peak), peak_ref.shape)
-    copy = pltpu.make_async_copy(peak_ref, peak_out, out_sem.at[2])
-    copy.start()
-    copy.wait()
-    for copy in kept:
-        copy.wait()
 
 
 def gather_operand(slot_ref, source_ref, target_ref, c):
@@ -156,15 +138,9 @@
 
 
 def prepare_kernel(
-    slot_ref, before_ref, own_ref, after_ref, probe_ref, turned_ref, table_ref,
-    flat_ref, hot_ref, sem,
+    slot_ref, before_ref, own_ref, after_ref, probe_ref, table_ref,
+    hot_ref,
 ):
-    pieces = [
-        pltpu.make_async_copy(ref.at[0:512], flat_ref.at[part], sem.at[part])
-        for part, ref in enumerate((before_ref, own_ref, after_ref))
-    ]
-    for copy in pieces:
-        copy.start()
     lane = lanes()
     for t in range(4):
         for c in range(8):
@@ -173,33 +149,21 @@
                 hot_ref[row : row + 1, :] = (lane == slot_ref[c, 4 * g + t]).astype(F32)
     table_ref[...] = hot_ref[...].T[0:NEAR, :]
     probe_ref[DEAD] = jnp.zeros((128, 64), BF16)
-    for part in range(3):
-        pieces[part].wait()
+    for part, ref in enumerate((before_ref, own_ref, after_ref)):
         for c in range(8):
-            turned = flat_ref[part, 64 * c : 64 * c + 64].astype(F32).T
-            if part == 1:
-                turned_ref[c] = turned
+            turned = ref[64 * c : 64 * c + 64].astype(F32).T
             probe_ref[8 * part + c] = turned.astype(BF16)
 
 
 def first_kernel(
-    slot_ref, peak_in, near_in, row_in, probe_ref,
-    scaled_ref, operand_ref, one_ref, half_ref, peak_ref, near_ref, row_ref, shift_ref, sem,
+    slot_ref, peak_ref, near_ref, row_ref, probe_ref,
+    scaled_ref, operand_ref, one_ref, half_ref, shift_ref,
 ):
-    copies = [
-        pltpu.make_async_copy(peak_in, peak_ref, sem.at[0]),
-        pltpu.make_async_copy(near_in, near_ref, sem.at[1]),
-        pltpu.make_async_copy(row_in, row_ref, sem.at[2]),
-    ]
-    for copy in copies:
-        copy.start()
     fill_shifts(shift_ref)
     lane = lanes()
-    for copy in copies:
-        copy.wait()
     inverse_peak = 1.0 / jnp.max(peak_ref[...])
 
-    def one_pair(pair, carry):
+    def one_pair(pair):
         for side in range(2):
             c = pair + 4 * side
             rows = [row_ref[c, x] for x in range(3)]
@@ -228,9 +192,9 @@
             one = jnp.dot(scaled_ref[c], operand_ref[c], preferred_element_type=F32)
             one_ref[c] = one
             half_ref[pair, :, 64 * side : 64 * side + 64] = one.astype(BF16)
-        return carry
-
-    lax.fori_loop(0, 4, one_pair, 0)
+
+    for pair in range(4):
+        one_pair(pair)
 
 
 def block_at(scaled_ref, c, g, a, b, value):
@@ -239,16 +203,10 @@
 
 
 def second_kernel(
-    slot_ref, near_in, row_in, scaled_ref, operand_ref, turned_ref, one_ref,
+    slot_ref, near_ref, row_ref, scaled_ref, operand_ref, probe_ref, one_ref,
     before_ref, own_ref, after_ref, table_ref, send_ref,
-    near_ref, row_ref, half_ref, gathered_ref, near_pull_ref, own_pull_ref, shift_ref, sem,
+    half_ref, gathered_ref, near_pull_ref, own_pull_ref, shift_ref,
 ):
-    copies = [
-        pltpu.make_async_copy(near_in, near_ref, sem.at[0]),
-        pltpu.make_async_copy(row_in, row_ref, sem.at[1]),
-    ]
-    for copy in copies:
-        copy.start()
     fill_shifts(shift_ref)
     lane = lanes()
     for part, ref in enumerate((before_ref, own_ref, after_ref)):
@@ -256,25 +214,23 @@
             half_ref[8 * part + pair] = ref[pair, :, 0:64]
             half_ref[8 * part + pair + 4] = ref[pair, :, 64:128]
     half_ref[DEAD] = jnp.zeros((128, 64), BF16)
-    for copy in copies:
-        copy.wait()
     on_row = lax.broadcasted_iota(jnp.int32, (32, 128), 0) == lax.broadcasted_iota(
         jnp.int32, (32, 128), 1
     )
 
-    def one_pair(pair, carry):
+    def one_pair(pair):
         for side in range(2):
             c = pair + 4 * side
             gather_operand(slot_ref, half_ref, gathered_ref.at[side], c)
             two = jnp.dot(scaled_ref[c], gathered_ref[side], preferred_element_type=F32)
-            probe = turned_ref[c]
+            probe = probe_ref[8 + c].astype(F32)
             term_two = 2.0 * two - probe
             mixture = COEFF_ZERO * probe + COEFF_ONE * one_ref[c] + COEFF_TWO * term_two
             mixture = mixture.astype(BF16)
             wide = mixture.astype(F32)
             for q in range(8):
                 send_ref[
-                    q, pl.ds(pl.multiple_of(16 * pair, 16), 16), 64 * side : 64 * side + 64
+                    q, 16 * pair : 16 * pair + 16, 64 * side : 64 * side + 64
                 ] = wide[16 * q : 16 * q + 16, :]
             rows = [row_ref[c, x] for x in range(3)]
             own = [jnp.zeros((32, 128), F32) for _ in range(3)]
@@ -289,17 +245,17 @@
                 pulls = pair_pulls(sample, columns, rows)
                 for x in range(3):
                     own[x] = own[x] + pulls[x]
-                    near_pull_ref[x, pl.ds(4 * c + g, 1), :] = jnp.sum(
+                    near_pull_ref[x, 4 * c + g : 4 * c + g + 1, :] = jnp.sum(
                         pulls[x], axis=0, keepdims=True
                     )
             for x in range(3):
                 whole = jnp.broadcast_to(jnp.sum(own[x], axis=1, keepdims=True), (32, 128))
-                own_pull_ref[x, pl.ds(c, 1), :] = jnp.sum(
+                own_pull_ref[x, c : c + 1, :] = jnp.sum(
                     jnp.where(on_row, whole, 0.0), axis=0, keepdims=True
                 )
-        return carry
-
-    lax.fori_loop(0, 4, one_pair, 0)
+
+    for pair in range(4):
+        one_pair(pair)
 
     stacked = jnp.concatenate(
         [
@@ -410,6 +366,8 @@
     own = jnp.concatenate([probes.reshape(512, 128), coords.reshape(24, 128)])
     before, after = both(own)
     core = space_rank % 2
+    pair = jnp.stack([jnp.where(core == 0, before, after)[:512], own[:512]])
+    across = along_probe(pair, lambda i: i ^ 1)
     present = neighbours >= 0
     slot = (neighbours // 8 - space_rank + 1) % space_count * 8 + neighbours % 8
     slot = jnp.pad(jnp.where(present, slot, DEAD), ((0, 0), (0, 1)), constant_values=DEAD)
@@ -421,43 +379,36 @@
             jax.ShapeDtypeStruct((8, 3, 32, 128), F32),
             jax.ShapeDtypeStruct((space_count, 128), F32),
         ),
-        in_specs=[SMEM] + [HBM] * 3,
-        out_specs=(HBM,) * 3,
-        scratch_shapes=[
-            pltpu.VMEM((3, 24, 128), BF16),
-            pltpu.VMEM((NEAR + 1, 8, 128), F32),
-            pltpu.VMEM((8, 3, 32, 128), F32),
-            pltpu.VMEM((space_count, 128), F32),
-            pltpu.VMEM((4, 8, 128), F32),
-            pltpu.SemaphoreType.DMA((3,)),
-            pltpu.SemaphoreType.DMA((3,)),
-        ],
+        in_specs=[SMEM] + [WHOLE] * 3,
+        out_specs=(WHOLE,) * 3,
+        scratch_shapes=[pltpu.VMEM((4, 8, 128), F32)],
         cost_estimate=HEAVY,
         compiler_params=params(4),
         name="spectral",
     )(slot, before, own, after)
     peak, held = lax.optimization_barrier((peak, (before, own, after)))
     peaks = lax.all_to_all(peak, "space", 0, 0, tiled=True)
-    probe_turned, turned, table = pl.pallas_call(
+    probe_turned, table = pl.pallas_call(
         prepare_kernel,
         out_shape=(
             jax.ShapeDtypeStruct((NEAR + 1, 128, 64), BF16),
-            jax.ShapeDtypeStruct((8, 128, 64), F32),
             jax.ShapeDtypeStruct((NEAR, 128), F32),
         ),
-        in_specs=[SMEM] + [HBM] * 3,
-        out_specs=(WHOLE,) * 3,
-        scratch_shapes=[
-            pltpu.VMEM((3, 512, 128), BF16),
-            pltpu.VMEM((128, 128), F32),
-            pltpu.SemaphoreType.DMA((3,)),
-        ],
+        in_specs=[SMEM] + [WHOLE] * 3,
+        out_specs=(WHOLE,) * 2,
+        scratch_shapes=[pltpu.VMEM((128, 128), F32)],
         compiler_params=params(4),
         name="prepare",
     )(slot, *held)
-    pair = jnp.stack([jnp.where(core == 0, held[0], held[2])[:512], held[1][:512]])
-    peaks, pair, probe_turned = lax.optimization_barrier((peaks, pair, probe_turned))
-    across = along_probe(pair, lambda i: i ^ 1)
+    peaks, pair, across, probe_turned = lax.optimization_barrier(
+        (peaks, pair, across, probe_turned)
+    )
+    quad = jnp.stack([pair, across])
+    pieces = [quad] + [
+        along_probe(quad, lambda i, distance=distance: (i + 2 * distance) % 8)
+        for distance in range(1, 4)
+    ]
+
     scaled, operand, one, half = pl.pallas_call(
         first_kernel,
         out_shape=(
@@ -466,45 +417,31 @@
             jax.ShapeDtypeStruct((8, 128, 64), F32),
             jax.ShapeDtypeStruct((4, 128, 128), BF16),
         ),
-        in_specs=[SMEM] + [HBM] * 3 + [WHOLE],
+        in_specs=[SMEM] + [WHOLE] * 4,
         out_specs=(WHOLE,) * 4,
-        scratch_shapes=[
-            pltpu.VMEM((space_count, 128), F32),
-            pltpu.VMEM((NEAR + 1, 8, 128), F32),
-            pltpu.VMEM((8, 3, 32, 128), F32),
-            pltpu.VMEM((4, 8, 128), F32),
-            pltpu.SemaphoreType.DMA((3,)),
-        ],
+        scratch_shapes=[pltpu.VMEM((4, 8, 128), F32)],
         cost_estimate=LIGHT,
         compiler_params=params(16),
         name="first",
     )(slot, peaks, near, rows, probe_turned)
     half_before, half_after = both(half)
-    half, pair, across = lax.optimization_barrier((half, pair, across))
-    quad = jnp.stack([pair, across])
-    pieces = [quad] + [
-        along_probe(quad, lambda i, distance=distance: (i + 2 * distance) % 8)
-        for distance in range(1, 4)
-    ]
+
     send = pl.pallas_call(
         second_kernel,
         out_shape=jax.ShapeDtypeStruct((8, 88, 128), F32),
-        in_specs=[SMEM, HBM, HBM] + [WHOLE] * 8,
+        in_specs=[SMEM] + [WHOLE] * 10,
         out_specs=WHOLE,
         cost_estimate=LIGHT,
         scratch_shapes=[
-            pltpu.VMEM((NEAR + 1, 8, 128), F32),
-            pltpu.VMEM((8, 3, 32, 128), F32),
             pltpu.VMEM((NEAR + 1, 128, 64), BF16),
             pltpu.VMEM((2, 2048, 64), BF16),
             pltpu.VMEM((3, 32, 128), F32),
             pltpu.VMEM((3, 8, 128), F32),
             pltpu.VMEM((4, 8, 128), F32),
-            pltpu.SemaphoreType.DMA((2,)),
         ],
         compiler_params=params(16),
         name="second",
-    )(slot, near, rows, scaled, operand, turned, one, half_before, half, half_after, table)
+    )(slot, near, rows, scaled, operand, probe_turned, one, half_before, half, half_after, table)
     send, pieces = lax.optimization_barrier((send, pieces))
     swapped = [
         lax.ppermute(piece, "space", [(i, i ^ 1) for i in range(space_count)]) for piece in pieces

time: 93 us -> 87.9 us (0.945)
  waiting for transfers between devices: 28 us -> 23.8 us
  Pallas kernels: 20.3 us -> 16.7 us
  starting transfers between devices: 40.3 us -> 42.1 us
    ppermute x4, waiting for transfers between devices: 8.31 us -> 3.67 us  [along_probe(): return lax.ppermute(block, 'probe', [(i, target(i)) for i in range(8)])]
    ppermute x4, starting transfers between devices: 5.28 us -> 7.07 us  [along_probe(): return lax.ppermute(block, 'probe', [(i, target(i)) for i in range(8)])]
    pallas_call x1, Pallas kernels: 3.91 us -> 2.71 us  [per_device(): pl.pallas_call(spectral_kernel, out_shape=(jax.ShapeDtypeStruct((NEAR + 1...]
    pallas_call x1, Pallas kernels: 4.43 us -> 3.35 us  [per_device(): pl.pallas_call(first_kernel, out_shape=(jax.ShapeDtypeStruct((8, 128, 204...]
  transfers between devices with their start and end apart: 16 -> 16, of which waited for: 8 -> 6; matrix products, arithmetic and copies ran while one was open for 1% -> 1% of each run, Pallas kernels for 18% -> 19%
where the time goes in v7:
time: 87.9 us; the launch traced here: 87.5 us
  starting transfers between devices  42.1 us (48%)
  waiting for transfers between devices  23.8 us (27%)
  Pallas kernels  16.7 us (19%)
  other arithmetic  3.32 us (4%)
    ppermute x6, starting transfers between devices, around(): lax.ppermute(block, 'space', [((i - distance) % size, i) for i in range(s...  20.4 us
    all_to_all x1, starting transfers between devices, per_device(): peaks = lax.all_to_all(peak, 'space', 0, 0, tiled=True)  9.03 us
    all_to_all x1, waiting for transfers between devices, per_device(): peaks = lax.all_to_all(peak, 'space', 0, 0, tiled=True)  8.78 us
    ppermute x4, starting transfers between devices, along_probe(): return lax.ppermute(block, 'probe', [(i, target(i)) for i in range(8)])  7.07 us
    pallas_call x1, Pallas kernels, per_device(): pl.pallas_call(second_kernel, out_shape=jax.ShapeDtypeStruct((8, 88, 128)...  6.4 us
    ppermute x6, waiting for transfers between devices, around(): lax.ppermute(block, 'space', [((i - distance) % size, i) for i in range(s...  5.93 us
    all_to_all x1, waiting for transfers between devices, per_device(): received = lax.all_to_all(send, 'probe', 0, 0, tiled=True)  5.44 us
    all_to_all x1, starting transfers between devices, per_device(): received = lax.all_to_all(send, 'probe', 0, 0, tiled=True)  4.62 us
  transfers between devices with their start and end apart: 16, of which 6 were waited for; matrix products, arithmetic and copies ran while one was open for 1% of the time, Pallas kernels for 19%

profile of v7, /device:TPU:2, one launch (start us, length us, event | category | flops | bytes accessed | tf_op | source)
XLA Modules:
  0.0 87.5 jit_solution(7911488070551050818)
XLA Ops:
  0.6 0.7 pad_bitcast_fusion
  1.3 0.9 %pad_maximum_fusion.2.own_ref = bf16[536,128]{1,0:T(8,128)(2,1)S(1)} fusion(bf16[24,128]{1,0:T(8,128)(2,1)S(1)} %pad_bitcast_fusion, bf16[512,128]{1,0:T(8,128)(2,1)} %bitcast.26), kind=kLoop, calls=%fused_computation.2 | loop fusion | flops 274432 | bytes 274432 | tf_op jit(solution)/shard_map/concatenate | solution.py:366
  2.2 0.1 collective-permute-start
  2.3 8.3 %collective-permute-start.1 = (bf16[536,128]{1,0:T(8,128)(2,1)S(1)}, bf16[536,128]{1,0:T(8,128)(2,1)S(1)}, u32[]{:S(2)}, u32[]{:S(2)}) collective-permute-start(bf16[536,128]{1,0:T(8,128)(2,1)S(1)} %pad_maximum_fusion.2.own_ref), channel_id=1, source_target_pairs={{8,0},{16,8},{24,16},{32,24},{40,32},{48,40},{56,48},{64,56},{72,6... | collective-permute-start | bytes 411656 | tf_op jit(solution)/shard_map/ppermute | solution.py:353
  10.6 2.7 %collective-permute-done.before_ref = bf16[536,128]{1,0:T(8,128)(2,1)S(1)} collective-permute-done((bf16[536,128]{1,0:T(8,128)(2,1)S(1)}, bf16[536,128]{1,0:T(8,128)(2,1)S(1)}, u32[]{:S(2)}, u32[]{:S(2)}) %collective-permute-start) | collective-permute-done | bytes 137248 | tf_op jit(solution)/shard_map/ppermute | solution.py:353
  13.3 0.4 collective-permute-done.1.after_ref
  13.8 0.9 %pad_maximum_fusion.1 = bf16[2,512,128]{2,1,0:T(8,128)(2,1)S(1)} fusion(bf16[1,512,128]{2,1,0:T(8,128)(2,1)} %bitcast.27, bf16[1,512,128]{2,1,0:T(8,128)(2,1)S(1)} %fusion), kind=kLoop, calls=%fused_computation.1 | loop fusion | flops 131072 | bytes 524288 | tf_op jit(solution)/shard_map/stack | solution.py:369
  14.7 2.2 %collective-permute-start.2 = (bf16[2,512,128]{2,1,0:T(8,128)(2,1)S(1)}, bf16[2,512,128]{2,1,0:T(8,128)(2,1)S(1)}, u32[]{:S(2)}, u32[]{:S(2)}) collective-permute-start(bf16[2,512,128]{2,1,0:T(8,128)(2,1)S(1)} %pad_maximum_fusion.1), channel_id=1, source_target_pairs={{0,1},{1,0},{2,3},{3,2},{4,5},{5,4},{6,7},{7,6},{8,9},{9,8},{10,11... | collective-permute-start | bytes 786440 | tf_op jit(solution)/shard_map/ppermute | solution.py:357
  17.0 0.7 fusion.6
  17.7 2.7 %spectral.1 = (f32[25,8,128]{2,1,0:T(8,128)S(1)}, f32[8,3,32,128]{3,2,1,0:T(8,128)S(1)}, f32[32,128]{1,0:T(8,128)}) custom-call(s32[8,16]{1,0:T(8,128)S(1)} %pad.8.slot_ref, bf16[536,128]{1,0:T(8,128)(2,1)S(1)} %collective-permute-done.before_ref, bf16[536,128]{1,0:T(8,128)(2,1)S(1)} %pad_maximum_fusion.2.own_ref, ...), custom_call_target="tpu_custom_call" | custom-call | bytes 60000000 | tf_op jit(solution)/shard_map/spectral/pallas_call | solution.py:375
  20.4 9.0 %all-to-all-start = ((f32[32,1,128]{2,1,0:T(1,128)}), f32[32,1,128]{2,1,0:T(1,128)S(1)}, u32[]{:S(2)}, u32[]{:S(2)}) async-start(f32[32,1,128]{2,1,0:T(1,128)} %bitcast.6), calls=%async_computation | async-start | bytes 32768 | tf_op jit(solution)/shard_map/all_to_all | solution.py:390
  29.4 0.9 %prepare.1 = (bf16[25,128,64]{2,1,0:T(8,128)(2,1)S(1)}, f32[24,128]{1,0:T(8,128)S(1)}) custom-call(s32[8,16]{1,0:T(8,128)S(1)} %pad.8.slot_ref, bf16[536,128]{1,0:T(8,128)(2,1)S(1)} %collective-permute-done.before_ref, bf16[536,128]{1,0:T(8,128)(2,1)S(1)} %pad_maximum_fusion.2.own_ref, bf16[536,128]{1,0:T(8,128)(2,1)S(1)} %collective-permute-done.1.after_ref), custom_call_target="tpu_custom_call" | custom-call | tf_op jit(solution)/shard_map/prepare/pallas_call | solution.py:391
  30.4 8.8 %all-to-all-done = f32[32,1,128]{2,1,0:T(1,128)S(1)} async-done(((f32[32,1,128]{2,1,0:T(1,128)}), f32[32,1,128]{2,1,0:T(1,128)S(1)}, u32[]{:S(2)}, u32[]{:S(2)}) %all-to-all-start) | async-done | bytes 16416 | tf_op jit(solution)/shard_map/all_to_all | solution.py:390
  39.1 0.0 collective-permute-done.2
  39.1 0.1 pad_maximum_fusion.refs_0_
  39.2 1.6 %collective-permute-start.5 = (bf16[2,2,512,128]{3,2,1,0:T(8,128)(2,1)S(1)}, bf16[2,2,512,128]{3,2,1,0:T(8,128)(2,1)S(1)}, u32[]{:S(2)}, u32[]{:S(2)}) collective-permute-start(bf16[2,2,512,128]{3,2,1,0:T(8,128)(2,1)S(1)} %pad_maximum_fusion.refs_0_), channel_id=1, source_target_pairs={{0,2},{1,3},{2,4},{3,5},{4,6},{5,7},{6,0},{7,1},{8,10},{9,11},{10,... | collective-permute-start | bytes 1572872 | tf_op jit(solution)/shard_map/ppermute | solution.py:357
  40.8 1.1 %collective-permute-start.6 = (bf16[2,2,512,128]{3,2,1,0:T(8,128)(2,1)S(1)}, bf16[2,2,512,128]{3,2,1,0:T(8,128)(2,1)S(1)}, u32[]{:S(2)}, u32[]{:S(2)}) collective-permute-start(bf16[2,2,512,128]{3,2,1,0:T(8,128)(2,1)S(1)} %pad_maximum_fusion.refs_0_), channel_id=1, source_target_pairs={{0,4},{1,5},{2,6},{3,7},{4,0},{5,1},{6,2},{7,3},{8,12},{9,13},{10,... | collective-permute-start | bytes 1572872 | tf_op jit(solution)/shard_map/ppermute | solution.py:357
  41.9 2.2 %collective-permute-start.7 = (bf16[2,2,512,128]{3,2,1,0:T(8,128)(2,1)S(1)}, bf16[2,2,512,128]{3,2,1,0:T(8,128)(2,1)S(1)}, u32[]{:S(2)}, u32[]{:S(2)}) collective-permute-start(bf16[2,2,512,128]{3,2,1,0:T(8,128)(2,1)S(1)} %pad_maximum_fusion.refs_0_), channel_id=1, source_target_pairs={{0,6},{1,7},{2,0},{3,1},{4,2},{5,3},{6,4},{7,5},{8,14},{9,15},{10,... | collective-permute-start | bytes 1572872 | tf_op jit(solution)/shard_map/ppermute | solution.py:357
  44.0 3.4 %first.1 = (bf16[8,128,2048]{2,1,0:T(8,128)(2,1)S(1)}, bf16[8,2048,64]{2,1,0:T(8,128)(2,1)S(1)}, f32[8,128,64]{2,1,0:T(8,128)S(1)}, bf16[4,128,128]{2,1,0:T(8,128)(2,1)S(1)}) custom-call(s32[8,16]{1,0:T(8,128)S(1)} %pad.8.slot_ref, f32[32,128]{1,0:T(8,128)S(1)} %bitcast.24, f32[25,8,128]{2,1,0:T(8,128)S(1)} %get-tuple-element.24.near_ref, ...), custom_call_target="tpu_custom_call" | custom-call | tf_op jit(solution)/shard_map/first/pallas_call | solution.py:412
  47.4 0.1 collective-permute-start.3
  47.5 6.0 %collective-permute-start.4 = (bf16[4,128,128]{2,1,0:T(8,128)(2,1)S(1)}, bf16[4,128,128]{2,1,0:T(8,128)(2,1)S(1)}, u32[]{:S(2)}, u32[]{:S(2)}) collective-permute-start(bf16[4,128,128]{2,1,0:T(8,128)(2,1)S(1)} %get-tuple-element.37.own_ref), channel_id=1, source_target_pairs={{8,0},{16,8},{24,16},{32,24},{40,32},{48,40},{56,48},{64,56},{72,6... | collective-permute-start | bytes 393224 | tf_op jit(solution)/shard_map/ppermute | solution.py:353
  53.4 2.7 %collective-permute-done.3.before_ref = bf16[4,128,128]{2,1,0:T(8,128)(2,1)S(1)} collective-permute-done((bf16[4,128,128]{2,1,0:T(8,128)(2,1)S(1)}, bf16[4,128,128]{2,1,0:T(8,128)(2,1)S(1)}, u32[]{:S(2)}, u32[]{:S(2)}) %collective-permute-start.3) | collective-permute-done | bytes 131104 | tf_op jit(solution)/shard_map/ppermute | solution.py:353
  56.2 0.0 collective-permute-done.4.after_ref
  56.2 6.4 %second.1 = f32[8,88,128]{2,1,0:T(8,128)} custom-call(s32[8,16]{1,0:T(8,128)S(1)} %pad.8.slot_ref, f32[25,8,128]{2,1,0:T(8,128)S(1)} %get-tuple-element.24.near_ref, f32[8,3,32,128]{3,2,1,0:T(8,128)S(1)} %get-tuple-element.25.row_ref, bf16[8,128,2048]{2,1,0:T(8,128)(2,1)S(1)} %get-tuple-element.34.scaled_ref, ...), custom_call_target="tpu_custom_call" | custom-call | tf_op jit(solution)/shard_map/second/pallas_call | solution.py:429
  62.6 0.0 collective-permute-done.5.refs_1_
  62.6 0.0 collective-permute-done.6.refs_2_
  62.6 3.7 %collective-permute-done.7.refs_3_ = bf16[2,2,512,128]{3,2,1,0:T(8,128)(2,1)S(1)} collective-permute-done((bf16[2,2,512,128]{3,2,1,0:T(8,128)(2,1)S(1)}, bf16[2,2,512,128]{3,2,1,0:T(8,128)(2,1)S(1)}, u32[]{:S(2)}, u32[]{:S(2)}) %collective-permute-start.7) | collective-permute-done | bytes 524320 | tf_op jit(solution)/shard_map/ppermute | solution.py:357
  66.2 4.6 %all-to-all-start.1 = ((f32[8,88,128]{2,1,0:T(8,128)}), f32[8,88,128]{2,1,0:T(8,128)S(1)}, u32[]{:S(2)}, u32[]{:S(2)}) async-start(f32[8,88,128]{2,1,0:T(8,128)} %second.1), calls=%async_computation.1 | async-start | bytes 720896 | tf_op jit(solution)/shard_map/all_to_all | solution.py:449
  70.9 0.0 collective-permute-start.8
  70.9 0.5 collective-permute-start.9
  71.4 0.0 collective-permute-start.10
  71.4 0.5 collective-permute-start.11
  71.9 5.4 %all-to-all-done.1.received_ref = f32[8,88,128]{2,1,0:T(8,128)S(1)} async-done(((f32[8,88,128]{2,1,0:T(8,128)}), f32[8,88,128]{2,1,0:T(8,128)S(1)}, u32[]{:S(2)}, u32[]{:S(2)}) %all-to-all-start.1) | async-done | bytes 360480 | tf_op jit(solution)/shard_map/all_to_all | solution.py:449
  77.4 0.1 collective-permute-start.13
  77.4 0.0 collective-permute-done.8.refs_4_
  77.5 5.9 %collective-permute-start.12 = (f32[8,128]{1,0:T(8,128)S(1)}, f32[8,128]{1,0:T(8,128)S(1)}, u32[]{:S(2)}, u32[]{:S(2)}) collective-permute-start(f32[8,128]{1,0:T(8,128)S(1)} %get-tuple-element.46), channel_id=1, source_target_pairs={{8,0},{16,8},{24,16},{32,24},{40,32},{48,40},{56,48},{64,56},{72,6... | collective-permute-start | bytes 12296 | tf_op jit(solution)/shard_map/ppermute | solution.py:353
  83.4 0.1 pad_add_fusion.place_ref
  83.5 0.0 collective-permute-done.9.refs_5_
  83.5 0.0 collective-permute-done.10.refs_6_
  83.5 0.0 collective-permute-done.11.refs_7_
  83.5 3.3 %sample.1 = bf16[16,15,8,128]{3,2,1,0:T(8,128)(2,1)} custom-call(s32[8,16]{1,0:T(8,128)S(1)} %pad.8.slot_ref, s32[2]{0:T(128)S(1)} %pad_add_fusion.place_ref, f32[8,88,128]{2,1,0:T(8,128)S(1)} %all-to-all-done.1.received_ref, bf16[2,2,512,128]{3,2,1,0:T(8,128)(2,1)S(1)} %pad_maximum_fusion.refs_0_, ...), custom_call_target="tpu_custom_call" | custom-call | tf_op jit(solution)/shard_map/sample/pallas_call | solution.py:454
  86.8 0.0 collective-permute-done.13
  86.8 0.0 collective-permute-done.12
  86.8 0.1 slice_bitcast_fusion.2
  86.9 0.6 maximum_bitcast_fusion
  (5 shorter events, 0.0 us)
Async XLA Ops:
  2.2 11.1 %collective-permute-start = (bf16[536,128]{1,0:T(8,128)(2,1)S(1)}, bf16[536,128]{1,0:T(8,128)(2,1)S(1)}, u32[]{:S(2)}, u32[]{:S(2)}) collective-permute-start(bf16[536,128]{1,0:T(8,128)(2,1)S(1)} %pad_maximum_fusion.2.own_ref), channel_id=1, source_target_pairs={{248,0},{0,8},{8,16},{16,24},{24,32},{32,40},{40,48},{48,56},{56,6... | collective-permute-start | bytes 411656 | tf_op jit(solution)/shard_map/ppermute | solution.py:353
  2.3 11.4 %collective-permute-start.1 = (bf16[536,128]{1,0:T(8,128)(2,1)S(1)}, bf16[536,128]{1,0:T(8,128)(2,1)S(1)}, u32[]{:S(2)}, u32[]{:S(2)}) collective-permute-start(bf16[536,128]{1,0:T(8,128)(2,1)S(1)} %pad_maximum_fusion.2.own_ref), channel_id=1, source_target_pairs={{8,0},{16,8},{24,16},{32,24},{40,32},{48,40},{56,48},{64,56},{72,6... | collective-permute-start | bytes 411656 | tf_op jit(solution)/shard_map/ppermute | solution.py:353
  14.7 24.4 %collective-permute-start.2 = (bf16[2,512,128]{2,1,0:T(8,128)(2,1)S(1)}, bf16[2,512,128]{2,1,0:T(8,128)(2,1)S(1)}, u32[]{:S(2)}, u32[]{:S(2)}) collective-permute-start(bf16[2,512,128]{2,1,0:T(8,128)(2,1)S(1)} %pad_maximum_fusion.1), channel_id=1, source_target_pairs={{0,1},{1,0},{2,3},{3,2},{4,5},{5,4},{6,7},{7,6},{8,9},{9,8},{10,11... | collective-permute-start | bytes 786440 | tf_op jit(solution)/shard_map/ppermute | solution.py:357
  20.4 18.7 %all-to-all-start = ((f32[32,1,128]{2,1,0:T(1,128)}), f32[32,1,128]{2,1,0:T(1,128)S(1)}, u32[]{:S(2)}, u32[]{:S(2)}) async-start(f32[32,1,128]{2,1,0:T(1,128)} %bitcast.6), calls=%async_computation | async-start | bytes 32768 | tf_op jit(solution)/shard_map/all_to_all | solution.py:390
  39.2 23.4 %collective-permute-start.5 = (bf16[2,2,512,128]{3,2,1,0:T(8,128)(2,1)S(1)}, bf16[2,2,512,128]{3,2,1,0:T(8,128)(2,1)S(1)}, u32[]{:S(2)}, u32[]{:S(2)}) collective-permute-start(bf16[2,2,512,128]{3,2,1,0:T(8,128)(2,1)S(1)} %pad_maximum_fusion.refs_0_), channel_id=1, source_target_pairs={{0,2},{1,3},{2,4},{3,5},{4,6},{5,7},{6,0},{7,1},{8,10},{9,11},{10,... | collective-permute-start | bytes 1572872 | tf_op jit(solution)/shard_map/ppermute | solution.py:357
  40.8 21.8 %collective-permute-start.6 = (bf16[2,2,512,128]{3,2,1,0:T(8,128)(2,1)S(1)}, bf16[2,2,512,128]{3,2,1,0:T(8,128)(2,1)S(1)}, u32[]{:S(2)}, u32[]{:S(2)}) collective-permute-start(bf16[2,2,512,128]{3,2,1,0:T(8,128)(2,1)S(1)} %pad_maximum_fusion.refs_0_), channel_id=1, source_target_pairs={{0,4},{1,5},{2,6},{3,7},{4,0},{5,1},{6,2},{7,3},{8,12},{9,13},{10,... | collective-permute-start | bytes 1572872 | tf_op jit(solution)/shard_map/ppermute | solution.py:357
  41.9 24.4 %collective-permute-start.7 = (bf16[2,2,512,128]{3,2,1,0:T(8,128)(2,1)S(1)}, bf16[2,2,512,128]{3,2,1,0:T(8,128)(2,1)S(1)}, u32[]{:S(2)}, u32[]{:S(2)}) collective-permute-start(bf16[2,2,512,128]{3,2,1,0:T(8,128)(2,1)S(1)} %pad_maximum_fusion.refs_0_), channel_id=1, source_target_pairs={{0,6},{1,7},{2,0},{3,1},{4,2},{5,3},{6,4},{7,5},{8,14},{9,15},{10,... | collective-permute-start | bytes 1572872 | tf_op jit(solution)/shard_map/ppermute | solution.py:357
  47.4 8.8 %collective-permute-start.3 = (bf16[4,128,128]{2,1,0:T(8,128)(2,1)S(1)}, bf16[4,128,128]{2,1,0:T(8,128)(2,1)S(1)}, u32[]{:S(2)}, u32[]{:S(2)}) collective-permute-start(bf16[4,128,128]{2,1,0:T(8,128)(2,1)S(1)} %get-tuple-element.37.own_ref), channel_id=1, source_target_pairs={{248,0},{0,8},{8,16},{16,24},{24,32},{32,40},{40,48},{48,56},{56,6... | collective-permute-start | bytes 393224 | tf_op jit(solution)/shard_map/ppermute | solution.py:353
  47.5 8.7 %collective-permute-start.4 = (bf16[4,128,128]{2,1,0:T(8,128)(2,1)S(1)}, bf16[4,128,128]{2,1,0:T(8,128)(2,1)S(1)}, u32[]{:S(2)}, u32[]{:S(2)}) collective-permute-start(bf16[4,128,128]{2,1,0:T(8,128)(2,1)S(1)} %get-tuple-element.37.own_ref), channel_id=1, source_target_pairs={{8,0},{16,8},{24,16},{32,24},{40,32},{48,40},{56,48},{64,56},{72,6... | collective-permute-start | bytes 393224 | tf_op jit(solution)/shard_map/ppermute | solution.py:353
  66.2 11.1 %all-to-all-start.1 = ((f32[8,88,128]{2,1,0:T(8,128)}), f32[8,88,128]{2,1,0:T(8,128)S(1)}, u32[]{:S(2)}, u32[]{:S(2)}) async-start(f32[8,88,128]{2,1,0:T(8,128)} %second.1), calls=%async_computation.1 | async-start | bytes 720896 | tf_op jit(solution)/shard_map/all_to_all | solution.py:449
  70.9 6.6 %collective-permute-start.8 = (bf16[2,2,512,128]{3,2,1,0:T(8,128)(2,1)S(1)}, bf16[2,2,512,128]{3,2,1,0:T(8,128)(2,1)}, u32[]{:S(2)}, u32[]{:S(2)}) collective-permute-start(bf16[2,2,512,128]{3,2,1,0:T(8,128)(2,1)S(1)} %pad_maximum_fusion.refs_0_), channel_id=1, source_target_pairs={{0,8},{8,0},{16,24},{24,16},{32,40},{40,32},{48,56},{56,48},{64,72... | collective-permute-start | bytes 1572872 | tf_op jit(solution)/shard_map/ppermute | solution.py:447
  70.9 12.6 %collective-permute-start.9 = (bf16[2,2,512,128]{3,2,1,0:T(8,128)(2,1)S(1)}, bf16[2,2,512,128]{3,2,1,0:T(8,128)(2,1)}, u32[]{:S(2)}, u32[]{:S(2)}) collective-permute-start(bf16[2,2,512,128]{3,2,1,0:T(8,128)(2,1)S(1)} %collective-permute-done.5.refs_1_), channel_id=1, source_target_pairs={{0,8},{8,0},{16,24},{24,16},{32,40},{40,32},{48,56},{56,48},{64,72... | collective-permute-start | bytes 1572872 | tf_op jit(solution)/shard_map/ppermute | solution.py:447
  71.4 12.1 %collective-permute-start.10 = (bf16[2,2,512,128]{3,2,1,0:T(8,128)(2,1)S(1)}, bf16[2,2,512,128]{3,2,1,0:T(8,128)(2,1)}, u32[]{:S(2)}, u32[]{:S(2)}) collective-permute-start(bf16[2,2,512,128]{3,2,1,0:T(8,128)(2,1)S(1)} %collective-permute-done.6.refs_2_), channel_id=1, source_target_pairs={{0,8},{8,0},{16,24},{24,16},{32,40},{40,32},{48,56},{56,48},{64,72... | collective-permute-start | bytes 1572872 | tf_op jit(solution)/shard_map/ppermute | solution.py:447
  71.4 12.1 %collective-permute-start.11 = (bf16[2,2,512,128]{3,2,1,0:T(8,128)(2,1)S(1)}, bf16[2,2,512,128]{3,2,1,0:T(8,128)(2,1)}, u32[]{:S(2)}, u32[]{:S(2)}) collective-permute-start(bf16[2,2,512,128]{3,2,1,0:T(8,128)(2,1)S(1)} %collective-permute-done.7.refs_3_), channel_id=1, source_target_pairs={{0,8},{8,0},{16,24},{24,16},{32,40},{40,32},{48,56},{56,48},{64,72... | collective-permute-start | bytes 1572872 | tf_op jit(solution)/shard_map/ppermute | solution.py:447
  77.4 9.5 %collective-permute-start.13 = (f32[8,128]{1,0:T(8,128)S(1)}, f32[8,128]{1,0:T(8,128)S(1)}, u32[]{:S(2)}, u32[]{:S(2)}) collective-permute-start(f32[8,128]{1,0:T(8,128)S(1)} %get-tuple-element.47), channel_id=1, source_target_pairs={{248,0},{0,8},{8,16},{16,24},{24,32},{32,40},{40,48},{48,56},{56,6... | collective-permute-start | bytes 12296 | tf_op jit(solution)/shard_map/ppermute | solution.py:353
  77.5 9.4 %collective-permute-start.12 = (f32[8,128]{1,0:T(8,128)S(1)}, f32[8,128]{1,0:T(8,128)S(1)}, u32[]{:S(2)}, u32[]{:S(2)}) collective-permute-start(f32[8,128]{1,0:T(8,128)S(1)} %get-tuple-element.46), channel_id=1, source_target_pairs={{8,0},{16,8},{24,16},{32,24},{40,32},{48,40},{56,48},{64,56},{72,6... | collective-permute-start | bytes 12296 | tf_op jit(solution)/shard_map/ppermute | solution.py:353

commit v8 on v7

--- a/solution.py
+++ b/solution.py
@@ -30,6 +30,7 @@
 BF16 = jnp.bfloat16
 WHOLE = pl.BlockSpec()
 SMEM = pl.BlockSpec(memory_space=pltpu.SMEM)
+ANY = pl.BlockSpec(memory_space=pl.ANY)
 HEAVY = pl.CostEstimate(flops=0, transcendentals=0, bytes_accessed=60_000_000)
 LIGHT = pl.CostEstimate(flops=0, transcendentals=0, bytes_accessed=0)
 
@@ -86,8 +87,20 @@
 
 
 def spectral_kernel(
-    slot_ref, before_ref, own_ref, after_ref, near_ref, row_ref, peak_ref, shift_ref
+    slot_ref, core_ref, before_ref, own_ref, after_ref, near_ref, row_ref, peak_ref, pair_ref,
+    shift_ref, sem,
 ):
+    kept = pltpu.make_async_copy(own_ref.at[0:512], pair_ref.at[1], sem.at[1])
+    kept.start()
+
+    @pl.when(core_ref[0] == 0)
+    def _():
+        pltpu.make_async_copy(before_ref.at[0:512], pair_ref.at[0], sem.at[0]).start()
+
+    @pl.when(core_ref[0] != 0)
+    def _():
+        pltpu.make_async_copy(after_ref.at[0:512], pair_ref.at[0], sem.at[0]).start()
+
     fill_shifts(shift_ref)
     for part, ref in enumerate((before_ref, own_ref, after_ref)):
         for x in range(3):
@@ -127,6 +140,8 @@
     for c in range(8):
         peak = one_cluster(c, peak)
     peak_ref[...] = jnp.broadcast_to(jnp.max(peak), peak_ref.shape)
+    kept.wait()
+    pltpu.make_async_copy(before_ref.at[0:512], pair_ref.at[0], sem.at[0]).wait()
 
 
 def gather_operand(slot_ref, source_ref, target_ref, c):
@@ -303,11 +318,18 @@
 
 
 def sample_kernel(
-    slot_ref, place_ref, received_ref, *refs
+    slot_ref, rank_ref, core_ref, received_ref, *refs
 ):
-    pieces, swapped = refs[0:4], refs[4:8]
-    density_ref, left_ref, sample_ref, turn_ref = refs[8:]
-    rank, core = place_ref[0], place_ref[1]
+    pieces, others = refs[0:4], refs[4:8]
+    density_ref, left_ref, sample_ref, turn_ref, swapped_ref, sem = refs[8:]
+    copies = [
+        pltpu.make_async_copy(other.at[e, 1], swapped_ref.at[i, e, 1], sem.at[i, e])
+        for i, other in enumerate(others)
+        for e in range(2)
+    ]
+    for copy in copies:
+        copy.start()
+    rank, core = rank_ref[0], core_ref[0]
     for distance in range(4):
         source = (rank - 2 * distance + 8) % 8
         for e in range(2):
@@ -318,8 +340,12 @@
             left_ref[64:128, low : low + 64] = block[:, 64:128]
     left = left_ref[...]
     scale = 1.0 / math.sqrt(512.0)
+    swapped = [swapped_ref.at[i] for i in range(4)]
     sides = ((pieces, 0, 16 * core), (pieces, 1, 8), (swapped, 1, 16 - 16 * core))
-    for source_refs, index, base in sides:
+    for side, (source_refs, index, base) in enumerate(sides):
+        if side == 2:
+            for copy in copies:
+                copy.wait()
         for pair in range(4):
             c = 2 * pair
             right = jnp.concatenate(
@@ -366,26 +392,27 @@
     own = jnp.concatenate([probes.reshape(512, 128), coords.reshape(24, 128)])
     before, after = both(own)
     core = space_rank % 2
-    pair = jnp.stack([jnp.where(core == 0, before, after)[:512], own[:512]])
-    across = along_probe(pair, lambda i: i ^ 1)
     present = neighbours >= 0
     slot = (neighbours // 8 - space_rank + 1) % space_count * 8 + neighbours % 8
     slot = jnp.pad(jnp.where(present, slot, DEAD), ((0, 0), (0, 1)), constant_values=DEAD)
 
-    near, rows, peak = pl.pallas_call(
+    before, after, slot = lax.optimization_barrier((before, after, slot))
+    near, rows, peak, pair = pl.pallas_call(
         spectral_kernel,
         out_shape=(
             jax.ShapeDtypeStruct((NEAR + 1, 8, 128), F32),
             jax.ShapeDtypeStruct((8, 3, 32, 128), F32),
             jax.ShapeDtypeStruct((space_count, 128), F32),
+            jax.ShapeDtypeStruct((2, 512, 128), BF16),
         ),
-        in_specs=[SMEM] + [WHOLE] * 3,
-        out_specs=(WHOLE,) * 3,
-        scratch_shapes=[pltpu.VMEM((4, 8, 128), F32)],
+        in_specs=[SMEM, SMEM] + [WHOLE] * 3,
+        out_specs=(WHOLE,) * 4,
+        scratch_shapes=[pltpu.VMEM((4, 8, 128), F32), pltpu.SemaphoreType.DMA((2,))],
         cost_estimate=HEAVY,
         compiler_params=params(4),
         name="spectral",
-    )(slot, before, own, after)
+    )(slot, core.reshape(1), before, own, after)
+    across = along_probe(pair, lambda i: i ^ 1)
     peak, held = lax.optimization_barrier((peak, (before, own, after)))
     peaks = lax.all_to_all(peak, "space", 0, 0, tiled=True)
     probe_turned, table = pl.pallas_call(
@@ -454,17 +481,19 @@
     density = pl.pallas_call(
         sample_kernel,
         out_shape=jax.ShapeDtypeStruct((16, 15, 8, 128), BF16),
-        in_specs=[SMEM, SMEM] + [WHOLE] * 9,
+        in_specs=[SMEM] * 3 + [WHOLE] * 5 + [ANY] * 4,
         out_specs=WHOLE,
         scratch_shapes=[
             pltpu.VMEM((128, 512), BF16),
             pltpu.VMEM((NEAR + 1, 128, 128), F32),
             pltpu.VMEM((16 * 120, 128), F32),
+            pltpu.VMEM((4, 2, 2, 512, 128), BF16),
+            pltpu.SemaphoreType.DMA((4, 2)),
         ],
         compiler_params=params(16),
         name="sample",
     )(
-        slot, jnp.stack([lax.axis_index("probe"), core]), received, *pieces, *swapped
+        slot, lax.axis_index("probe").reshape(1), core.reshape(1), received, *pieces, *swapped
     )
     forces = force[8:16] + from_after + from_before
     forces = jnp.stack([forces[:, 32 * x : 32 * x + 32] for x in range(3)])

time: 87.9 us -> 86.6 us (0.985)
  starting transfers between devices: 42.1 us -> 37.2 us
  waiting for transfers between devices: 23.8 us -> 27.5 us
  other arithmetic: 3.32 us -> 2.29 us
    ppermute x6, waiting for transfers between devices: 5.93 us -> 10.9 us  [around(): lax.ppermute(block, 'space', [((i - distance) % size, i) for i in range(s...]
    ppermute x6, starting transfers between devices: 20.4 us -> 16.4 us  [around(): lax.ppermute(block, 'space', [((i - distance) % size, i) for i in range(s...]
    ppermute x4, waiting for transfers between devices: 3.67 us -> 2.42 us  [along_probe(): return lax.ppermute(block, 'probe', [(i, target(i)) for i in range(8)])]
    ppermute x4, starting transfers between devices: 7.07 us -> 5.99 us  [along_probe(): return lax.ppermute(block, 'probe', [(i, target(i)) for i in range(8)])]
    another operation x3 -> x0, other arithmetic: 1.02 us -> none  [the longest x2 0.95 us: per_device(): pair = jnp.stack([jnp.where(core == 0, before, after)[:512], own[:512]])]
    all_to_all x1, starting transfers between devices: 4.62 us -> 5.55 us  [per_device(): received = lax.all_to_all(send, 'probe', 0, 0, tiled=True)]
  transfers between devices with their start and end apart: 16 -> 16, of which waited for: 6 -> 7; matrix products, arithmetic and copies ran while one was open for 1% -> 1% of each run, Pallas kernels for 19% -> 17%
where the time goes in v8:
time: 86.6 us; the launch traced here: 86 us
  starting transfers between devices  37.2 us (43%)
  waiting for transfers between devices  27.5 us (32%)
  Pallas kernels  17.5 us (20%)
  other arithmetic  2.29 us (3%)
    ppermute x6, starting transfers between devices, around(): lax.ppermute(block, 'space', [((i - distance) % size, i) for i in range(s...  16.4 us
    ppermute x6, waiting for transfers between devices, around(): lax.ppermute(block, 'space', [((i - distance) % size, i) for i in range(s...  10.9 us
    all_to_all x1, waiting for transfers between devices, per_device(): peaks = lax.all_to_all(peak, 'space', 0, 0, tiled=True)  8.78 us
    all_to_all x1, starting transfers between devices, per_device(): peaks = lax.all_to_all(peak, 'space', 0, 0, tiled=True)  8.18 us
    pallas_call x1, Pallas kernels, per_device(): pl.pallas_call(second_kernel, out_shape=jax.ShapeDtypeStruct((8, 88, 128)...  6.4 us
    ppermute x4, starting transfers between devices, along_probe(): return lax.ppermute(block, 'probe', [(i, target(i)) for i in range(8)])  5.99 us
    all_to_all x1, starting transfers between devices, per_device(): received = lax.all_to_all(send, 'probe', 0, 0, tiled=True)  5.55 us
    all_to_all x1, waiting for transfers between devices, per_device(): received = lax.all_to_all(send, 'probe', 0, 0, tiled=True)  5.44 us
  transfers between devices with their start and end apart: 16, of which 7 were waited for; matrix products, arithmetic and copies ran while one was open for 1% of the time, Pallas kernels for 17%

profile of v8, /device:TPU:2, one launch (start us, length us, event | category | flops | bytes accessed | tf_op | source)
XLA Modules:
  0.0 86.0 jit_solution(3536127727473067740)
XLA Ops:
  0.6 0.7 pad_bitcast_fusion
  1.3 0.9 %pad_maximum_fusion.1.own_ref = bf16[536,128]{1,0:T(8,128)(2,1)S(1)} fusion(bf16[24,128]{1,0:T(8,128)(2,1)S(1)} %pad_bitcast_fusion, bf16[512,128]{1,0:T(8,128)(2,1)} %bitcast.25), kind=kLoop, calls=%fused_computation.1 | loop fusion | flops 274432 | bytes 274432 | tf_op jit(solution)/shard_map/concatenate | solution.py:392
  2.2 0.1 collective-permute-start
  2.3 8.3 %collective-permute-start.1 = (bf16[536,128]{1,0:T(8,128)(2,1)S(1)}, bf16[536,128]{1,0:T(8,128)(2,1)S(1)}, u32[]{:S(2)}, u32[]{:S(2)}) collective-permute-start(bf16[536,128]{1,0:T(8,128)(2,1)S(1)} %pad_maximum_fusion.1.own_ref), channel_id=1, source_target_pairs={{8,0},{16,8},{24,16},{32,24},{40,32},{48,40},{56,48},{64,56},{72,6... | collective-permute-start | bytes 411656 | tf_op jit(solution)/shard_map/ppermute | solution.py:379
  10.6 0.7 fusion.5
  11.3 2.0 %collective-permute-done.before_ref = bf16[536,128]{1,0:T(8,128)(2,1)S(1)} collective-permute-done((bf16[536,128]{1,0:T(8,128)(2,1)S(1)}, bf16[536,128]{1,0:T(8,128)(2,1)S(1)}, u32[]{:S(2)}, u32[]{:S(2)}) %collective-permute-start) | collective-permute-done | bytes 137248 | tf_op jit(solution)/shard_map/ppermute | solution.py:379
  13.3 1.3 %collective-permute-done.1.after_ref = bf16[536,128]{1,0:T(8,128)(2,1)S(1)} collective-permute-done((bf16[536,128]{1,0:T(8,128)(2,1)S(1)}, bf16[536,128]{1,0:T(8,128)(2,1)S(1)}, u32[]{:S(2)}, u32[]{:S(2)}) %collective-permute-start.1) | collective-permute-done | bytes 137248 | tf_op jit(solution)/shard_map/ppermute | solution.py:379
  14.7 3.1 %spectral.1 = (f32[25,8,128]{2,1,0:T(8,128)S(1)}, f32[8,3,32,128]{3,2,1,0:T(8,128)S(1)}, f32[32,128]{1,0:T(8,128)}, bf16[2,512,128]{2,1,0:T(8,128)(2,1)S(1)}) custom-call(s32[8,16]{1,0:T(8,128)S(1)} %pad.9.slot_ref, s32[1]{0:T(128)} %bitcast.4.core_ref, bf16[536,128]{1,0:T(8,128)(2,1)S(1)} %collective-permute-done.before_ref, ...), custom_call_target="tpu_custom_call" | custom-call | bytes 60000000 | tf_op jit(solution)/shard_map/spectral/pallas_call | solution.py:400
  17.7 1.2 %collective-permute-start.2 = (bf16[2,512,128]{2,1,0:T(8,128)(2,1)S(1)}, bf16[2,512,128]{2,1,0:T(8,128)(2,1)S(1)}, u32[]{:S(2)}, u32[]{:S(2)}) collective-permute-start(bf16[2,512,128]{2,1,0:T(8,128)(2,1)S(1)} %get-tuple-element.47), channel_id=1, source_target_pairs={{0,1},{1,0},{2,3},{3,2},{4,5},{5,4},{6,7},{7,6},{8,9},{9,8},{10,11... | collective-permute-start | bytes 786440 | tf_op jit(solution)/shard_map/ppermute | solution.py:383
  18.9 8.2 %all-to-all-start = ((f32[32,1,128]{2,1,0:T(1,128)}), f32[32,1,128]{2,1,0:T(1,128)S(1)}, u32[]{:S(2)}, u32[]{:S(2)}) async-start(f32[32,1,128]{2,1,0:T(1,128)} %bitcast.6), calls=%async_computation | async-start | bytes 32768 | tf_op jit(solution)/shard_map/all_to_all | solution.py:417
  27.1 0.9 %prepare.1 = (bf16[25,128,64]{2,1,0:T(8,128)(2,1)S(1)}, f32[24,128]{1,0:T(8,128)S(1)}) custom-call(s32[8,16]{1,0:T(8,128)S(1)} %pad.9.slot_ref, bf16[536,128]{1,0:T(8,128)(2,1)S(1)} %collective-permute-done.before_ref, bf16[536,128]{1,0:T(8,128)(2,1)S(1)} %pad_maximum_fusion.1.own_ref, bf16[536,128]{1,0:T(8,128)(2,1)S(1)} %collective-permute-done.1.after_ref), custom_call_target="tpu_custom_call" | custom-call | tf_op jit(solution)/shard_map/prepare/pallas_call | solution.py:418
  28.0 8.8 %all-to-all-done = f32[32,1,128]{2,1,0:T(1,128)S(1)} async-done(((f32[32,1,128]{2,1,0:T(1,128)}), f32[32,1,128]{2,1,0:T(1,128)S(1)}, u32[]{:S(2)}, u32[]{:S(2)}) %all-to-all-start) | async-done | bytes 16416 | tf_op jit(solution)/shard_map/all_to_all | solution.py:417
  36.8 0.0 collective-permute-done.2
  36.8 0.1 pad_maximum_fusion.refs_0_
  36.8 1.6 %collective-permute-start.5 = (bf16[2,2,512,128]{3,2,1,0:T(8,128)(2,1)S(1)}, bf16[2,2,512,128]{3,2,1,0:T(8,128)(2,1)S(1)}, u32[]{:S(2)}, u32[]{:S(2)}) collective-permute-start(bf16[2,2,512,128]{3,2,1,0:T(8,128)(2,1)S(1)} %pad_maximum_fusion.refs_0_), channel_id=1, source_target_pairs={{0,2},{1,3},{2,4},{3,5},{4,6},{5,7},{6,0},{7,1},{8,10},{9,11},{10,... | collective-permute-start | bytes 1572872 | tf_op jit(solution)/shard_map/ppermute | solution.py:383
  38.4 1.1 %collective-permute-start.6 = (bf16[2,2,512,128]{3,2,1,0:T(8,128)(2,1)S(1)}, bf16[2,2,512,128]{3,2,1,0:T(8,128)(2,1)S(1)}, u32[]{:S(2)}, u32[]{:S(2)}) collective-permute-start(bf16[2,2,512,128]{3,2,1,0:T(8,128)(2,1)S(1)} %pad_maximum_fusion.refs_0_), channel_id=1, source_target_pairs={{0,4},{1,5},{2,6},{3,7},{4,0},{5,1},{6,2},{7,3},{8,12},{9,13},{10,... | collective-permute-start | bytes 1572872 | tf_op jit(solution)/shard_map/ppermute | solution.py:383
  39.5 2.2 %collective-permute-start.7 = (bf16[2,2,512,128]{3,2,1,0:T(8,128)(2,1)S(1)}, bf16[2,2,512,128]{3,2,1,0:T(8,128)(2,1)S(1)}, u32[]{:S(2)}, u32[]{:S(2)}) collective-permute-start(bf16[2,2,512,128]{3,2,1,0:T(8,128)(2,1)S(1)} %pad_maximum_fusion.refs_0_), channel_id=1, source_target_pairs={{0,6},{1,7},{2,0},{3,1},{4,2},{5,3},{6,4},{7,5},{8,14},{9,15},{10,... | collective-permute-start | bytes 1572872 | tf_op jit(solution)/shard_map/ppermute | solution.py:383
  41.7 3.4 %first.1 = (bf16[8,128,2048]{2,1,0:T(8,128)(2,1)S(1)}, bf16[8,2048,64]{2,1,0:T(8,128)(2,1)S(1)}, f32[8,128,64]{2,1,0:T(8,128)S(1)}, bf16[4,128,128]{2,1,0:T(8,128)(2,1)S(1)}) custom-call(s32[8,16]{1,0:T(8,128)S(1)} %pad.9.slot_ref, f32[32,128]{1,0:T(8,128)S(1)} %bitcast.22, f32[25,8,128]{2,1,0:T(8,128)S(1)} %get-tuple-element.31.near_ref, ...), custom_call_target="tpu_custom_call" | custom-call | tf_op jit(solution)/shard_map/first/pallas_call | solution.py:439
  45.0 0.1 collective-permute-start.3
  45.1 6.0 %collective-permute-start.4 = (bf16[4,128,128]{2,1,0:T(8,128)(2,1)S(1)}, bf16[4,128,128]{2,1,0:T(8,128)(2,1)S(1)}, u32[]{:S(2)}, u32[]{:S(2)}) collective-permute-start(bf16[4,128,128]{2,1,0:T(8,128)(2,1)S(1)} %get-tuple-element.45.own_ref), channel_id=1, source_target_pairs={{8,0},{16,8},{24,16},{32,24},{40,32},{48,40},{56,48},{64,56},{72,6... | collective-permute-start | bytes 393224 | tf_op jit(solution)/shard_map/ppermute | solution.py:379
  51.1 4.0 %collective-permute-done.3.before_ref = bf16[4,128,128]{2,1,0:T(8,128)(2,1)S(1)} collective-permute-done((bf16[4,128,128]{2,1,0:T(8,128)(2,1)S(1)}, bf16[4,128,128]{2,1,0:T(8,128)(2,1)S(1)}, u32[]{:S(2)}, u32[]{:S(2)}) %collective-permute-start.3) | collective-permute-done | bytes 131104 | tf_op jit(solution)/shard_map/ppermute | solution.py:379
  55.1 0.0 collective-permute-done.4.after_ref
  55.1 6.4 %second.1 = f32[8,88,128]{2,1,0:T(8,128)} custom-call(s32[8,16]{1,0:T(8,128)S(1)} %pad.9.slot_ref, f32[25,8,128]{2,1,0:T(8,128)S(1)} %get-tuple-element.31.near_ref, f32[8,3,32,128]{3,2,1,0:T(8,128)S(1)} %get-tuple-element.32.row_ref, bf16[8,128,2048]{2,1,0:T(8,128)(2,1)S(1)} %get-tuple-element.42.scaled_ref, ...), custom_call_target="tpu_custom_call" | custom-call | tf_op jit(solution)/shard_map/second/pallas_call | solution.py:456
  61.5 0.0 collective-permute-done.5.refs_1_
  61.5 0.0 collective-permute-done.6.refs_2_
  61.5 2.4 %collective-permute-done.7.refs_3_ = bf16[2,2,512,128]{3,2,1,0:T(8,128)(2,1)S(1)} collective-permute-done((bf16[2,2,512,128]{3,2,1,0:T(8,128)(2,1)S(1)}, bf16[2,2,512,128]{3,2,1,0:T(8,128)(2,1)S(1)}, u32[]{:S(2)}, u32[]{:S(2)}) %collective-permute-start.7) | collective-permute-done | bytes 524320 | tf_op jit(solution)/shard_map/ppermute | solution.py:383
  63.9 5.6 %all-to-all-start.1 = ((f32[8,88,128]{2,1,0:T(8,128)}), f32[8,88,128]{2,1,0:T(8,128)S(1)}, u32[]{:S(2)}, u32[]{:S(2)}) async-start(f32[8,88,128]{2,1,0:T(8,128)} %second.1), calls=%async_computation.1 | async-start | bytes 720896 | tf_op jit(solution)/shard_map/all_to_all | solution.py:476
  69.5 0.0 collective-permute-start.10
  69.5 0.5 collective-permute-start.11
  70.0 0.0 collective-permute-start.8
  70.0 0.5 collective-permute-start.9
  70.5 5.4 %all-to-all-done.1.received_ref = f32[8,88,128]{2,1,0:T(8,128)S(1)} async-done(((f32[8,88,128]{2,1,0:T(8,128)}), f32[8,88,128]{2,1,0:T(8,128)S(1)}, u32[]{:S(2)}, u32[]{:S(2)}) %all-to-all-start.1) | async-done | bytes 360480 | tf_op jit(solution)/shard_map/all_to_all | solution.py:476
  76.0 2.1 %collective-permute-start.12 = (f32[8,128]{1,0:T(8,128)S(1)}, f32[8,128]{1,0:T(8,128)S(1)}, u32[]{:S(2)}, u32[]{:S(2)}) collective-permute-start(f32[8,128]{1,0:T(8,128)S(1)} %get-tuple-element.54), channel_id=1, source_target_pairs={{8,0},{16,8},{24,16},{32,24},{40,32},{48,40},{56,48},{64,56},{72,6... | collective-permute-start | bytes 12296 | tf_op jit(solution)/shard_map/ppermute | solution.py:379
  78.1 0.0 collective-permute-done.10.refs_6_
  78.1 0.0 collective-permute-start.13
  78.1 0.0 collective-permute-done.11.refs_7_
  78.1 0.0 collective-permute-done.8.refs_4_
  78.1 0.0 collective-permute-done.9.refs_5_
  78.1 3.7 %sample.1 = bf16[16,15,8,128]{3,2,1,0:T(8,128)(2,1)} custom-call(s32[8,16]{1,0:T(8,128)S(1)} %pad.9.slot_ref, s32[1]{0:T(128)} %bitcast.3.rank_ref, s32[1]{0:T(128)} %bitcast.4.core_ref, f32[8,88,128]{2,1,0:T(8,128)S(1)} %all-to-all-done.1.received_ref, bf16[2,2,512,128]{3,2,1,0:T(8,128)(2,1)S(1)} %pad_maximum_fusion.refs_0_, ...), custom_call_target="tpu_custom_call" | custom-call | tf_op jit(solution)/shard_map/sample/pallas_call | solution.py:481
  81.8 0.0 collective-permute-done.12
  81.8 3.5 %collective-permute-done.13 = f32[8,128]{1,0:T(8,128)S(1)} collective-permute-done((f32[8,128]{1,0:T(8,128)S(1)}, f32[8,128]{1,0:T(8,128)S(1)}, u32[]{:S(2)}, u32[]{:S(2)}) %collective-permute-start.13) | collective-permute-done | bytes 4128 | tf_op jit(solution)/shard_map/ppermute | solution.py:379
  85.3 0.1 slice_bitcast_fusion.2
  85.4 0.6 maximum_bitcast_fusion
  (4 shorter events, 0.0 us)
Async XLA Ops:
  2.2 11.1 %collective-permute-start = (bf16[536,128]{1,0:T(8,128)(2,1)S(1)}, bf16[536,128]{1,0:T(8,128)(2,1)S(1)}, u32[]{:S(2)}, u32[]{:S(2)}) collective-permute-start(bf16[536,128]{1,0:T(8,128)(2,1)S(1)} %pad_maximum_fusion.1.own_ref), channel_id=1, source_target_pairs={{248,0},{0,8},{8,16},{16,24},{24,32},{32,40},{40,48},{48,56},{56,6... | collective-permute-start | bytes 411656 | tf_op jit(solution)/shard_map/ppermute | solution.py:379
  2.3 12.3 %collective-permute-start.1 = (bf16[536,128]{1,0:T(8,128)(2,1)S(1)}, bf16[536,128]{1,0:T(8,128)(2,1)S(1)}, u32[]{:S(2)}, u32[]{:S(2)}) collective-permute-start(bf16[536,128]{1,0:T(8,128)(2,1)S(1)} %pad_maximum_fusion.1.own_ref), channel_id=1, source_target_pairs={{8,0},{16,8},{24,16},{32,24},{40,32},{48,40},{56,48},{64,56},{72,6... | collective-permute-start | bytes 411656 | tf_op jit(solution)/shard_map/ppermute | solution.py:379
  17.7 19.0 %collective-permute-start.2 = (bf16[2,512,128]{2,1,0:T(8,128)(2,1)S(1)}, bf16[2,512,128]{2,1,0:T(8,128)(2,1)S(1)}, u32[]{:S(2)}, u32[]{:S(2)}) collective-permute-start(bf16[2,512,128]{2,1,0:T(8,128)(2,1)S(1)} %get-tuple-element.47), channel_id=1, source_target_pairs={{0,1},{1,0},{2,3},{3,2},{4,5},{5,4},{6,7},{7,6},{8,9},{9,8},{10,11... | collective-permute-start | bytes 786440 | tf_op jit(solution)/shard_map/ppermute | solution.py:383
  18.9 17.9 %all-to-all-start = ((f32[32,1,128]{2,1,0:T(1,128)}), f32[32,1,128]{2,1,0:T(1,128)S(1)}, u32[]{:S(2)}, u32[]{:S(2)}) async-start(f32[32,1,128]{2,1,0:T(1,128)} %bitcast.6), calls=%async_computation | async-start | bytes 32768 | tf_op jit(solution)/shard_map/all_to_all | solution.py:417
  36.8 24.7 %collective-permute-start.5 = (bf16[2,2,512,128]{3,2,1,0:T(8,128)(2,1)S(1)}, bf16[2,2,512,128]{3,2,1,0:T(8,128)(2,1)S(1)}, u32[]{:S(2)}, u32[]{:S(2)}) collective-permute-start(bf16[2,2,512,128]{3,2,1,0:T(8,128)(2,1)S(1)} %pad_maximum_fusion.refs_0_), channel_id=1, source_target_pairs={{0,2},{1,3},{2,4},{3,5},{4,6},{5,7},{6,0},{7,1},{8,10},{9,11},{10,... | collective-permute-start | bytes 1572872 | tf_op jit(solution)/shard_map/ppermute | solution.py:383
  38.4 23.1 %collective-permute-start.6 = (bf16[2,2,512,128]{3,2,1,0:T(8,128)(2,1)S(1)}, bf16[2,2,512,128]{3,2,1,0:T(8,128)(2,1)S(1)}, u32[]{:S(2)}, u32[]{:S(2)}) collective-permute-start(bf16[2,2,512,128]{3,2,1,0:T(8,128)(2,1)S(1)} %pad_maximum_fusion.refs_0_), channel_id=1, source_target_pairs={{0,4},{1,5},{2,6},{3,7},{4,0},{5,1},{6,2},{7,3},{8,12},{9,13},{10,... | collective-permute-start | bytes 1572872 | tf_op jit(solution)/shard_map/ppermute | solution.py:383
  39.5 24.4 %collective-permute-start.7 = (bf16[2,2,512,128]{3,2,1,0:T(8,128)(2,1)S(1)}, bf16[2,2,512,128]{3,2,1,0:T(8,128)(2,1)S(1)}, u32[]{:S(2)}, u32[]{:S(2)}) collective-permute-start(bf16[2,2,512,128]{3,2,1,0:T(8,128)(2,1)S(1)} %pad_maximum_fusion.refs_0_), channel_id=1, source_target_pairs={{0,6},{1,7},{2,0},{3,1},{4,2},{5,3},{6,4},{7,5},{8,14},{9,15},{10,... | collective-permute-start | bytes 1572872 | tf_op jit(solution)/shard_map/ppermute | solution.py:383
  45.0 10.1 %collective-permute-start.3 = (bf16[4,128,128]{2,1,0:T(8,128)(2,1)S(1)}, bf16[4,128,128]{2,1,0:T(8,128)(2,1)S(1)}, u32[]{:S(2)}, u32[]{:S(2)}) collective-permute-start(bf16[4,128,128]{2,1,0:T(8,128)(2,1)S(1)} %get-tuple-element.45.own_ref), channel_id=1, source_target_pairs={{248,0},{0,8},{8,16},{16,24},{24,32},{32,40},{40,48},{48,56},{56,6... | collective-permute-start | bytes 393224 | tf_op jit(solution)/shard_map/ppermute | solution.py:379
  45.1 10.0 %collective-permute-start.4 = (bf16[4,128,128]{2,1,0:T(8,128)(2,1)S(1)}, bf16[4,128,128]{2,1,0:T(8,128)(2,1)S(1)}, u32[]{:S(2)}, u32[]{:S(2)}) collective-permute-start(bf16[4,128,128]{2,1,0:T(8,128)(2,1)S(1)} %get-tuple-element.45.own_ref), channel_id=1, source_target_pairs={{8,0},{16,8},{24,16},{32,24},{40,32},{48,40},{56,48},{64,56},{72,6... | collective-permute-start | bytes 393224 | tf_op jit(solution)/shard_map/ppermute | solution.py:379
  63.9 12.0 %all-to-all-start.1 = ((f32[8,88,128]{2,1,0:T(8,128)}), f32[8,88,128]{2,1,0:T(8,128)S(1)}, u32[]{:S(2)}, u32[]{:S(2)}) async-start(f32[8,88,128]{2,1,0:T(8,128)} %second.1), calls=%async_computation.1 | async-start | bytes 720896 | tf_op jit(solution)/shard_map/all_to_all | solution.py:476
  69.5 8.6 %collective-permute-start.10 = (bf16[2,2,512,128]{3,2,1,0:T(8,128)(2,1)S(1)}, bf16[2,2,512,128]{3,2,1,0:T(8,128)(2,1)}, u32[]{:S(2)}, u32[]{:S(2)}) collective-permute-start(bf16[2,2,512,128]{3,2,1,0:T(8,128)(2,1)S(1)} %collective-permute-done.6.refs_2_), channel_id=1, source_target_pairs={{0,8},{8,0},{16,24},{24,16},{32,40},{40,32},{48,56},{56,48},{64,72... | collective-permute-start | bytes 1572872 | tf_op jit(solution)/shard_map/ppermute | solution.py:474
  69.5 8.6 %collective-permute-start.11 = (bf16[2,2,512,128]{3,2,1,0:T(8,128)(2,1)S(1)}, bf16[2,2,512,128]{3,2,1,0:T(8,128)(2,1)}, u32[]{:S(2)}, u32[]{:S(2)}) collective-permute-start(bf16[2,2,512,128]{3,2,1,0:T(8,128)(2,1)S(1)} %collective-permute-done.7.refs_3_), channel_id=1, source_target_pairs={{0,8},{8,0},{16,24},{24,16},{32,40},{40,32},{48,56},{56,48},{64,72... | collective-permute-start | bytes 1572872 | tf_op jit(solution)/shard_map/ppermute | solution.py:474
  70.0 8.1 %collective-permute-start.8 = (bf16[2,2,512,128]{3,2,1,0:T(8,128)(2,1)S(1)}, bf16[2,2,512,128]{3,2,1,0:T(8,128)(2,1)}, u32[]{:S(2)}, u32[]{:S(2)}) collective-permute-start(bf16[2,2,512,128]{3,2,1,0:T(8,128)(2,1)S(1)} %pad_maximum_fusion.refs_0_), channel_id=1, source_target_pairs={{0,8},{8,0},{16,24},{24,16},{32,40},{40,32},{48,56},{56,48},{64,72... | collective-permute-start | bytes 1572872 | tf_op jit(solution)/shard_map/ppermute | solution.py:474
  70.0 8.1 %collective-permute-start.9 = (bf16[2,2,512,128]{3,2,1,0:T(8,128)(2,1)S(1)}, bf16[2,2,512,128]{3,2,1,0:T(8,128)(2,1)}, u32[]{:S(2)}, u32[]{:S(2)}) collective-permute-start(bf16[2,2,512,128]{3,2,1,0:T(8,128)(2,1)S(1)} %collective-permute-done.5.refs_1_), channel_id=1, source_target_pairs={{0,8},{8,0},{16,24},{24,16},{32,40},{40,32},{48,56},{56,48},{64,72... | collective-permute-start | bytes 1572872 | tf_op jit(solution)/shard_map/ppermute | solution.py:474
  76.0 5.8 %collective-permute-start.12 = (f32[8,128]{1,0:T(8,128)S(1)}, f32[8,128]{1,0:T(8,128)S(1)}, u32[]{:S(2)}, u32[]{:S(2)}) collective-permute-start(f32[8,128]{1,0:T(8,128)S(1)} %get-tuple-element.54), channel_id=1, source_target_pairs={{8,0},{16,8},{24,16},{32,24},{40,32},{48,40},{56,48},{64,56},{72,6... | collective-permute-start | bytes 12296 | tf_op jit(solution)/shard_map/ppermute | solution.py:379
  78.1 7.3 %collective-permute-start.13 = (f32[8,128]{1,0:T(8,128)S(1)}, f32[8,128]{1,0:T(8,128)S(1)}, u32[]{:S(2)}, u32[]{:S(2)}) collective-permute-start(f32[8,128]{1,0:T(8,128)S(1)} %get-tuple-element.55), channel_id=1, source_target_pairs={{248,0},{0,8},{8,16},{16,24},{24,32},{32,40},{40,48},{48,56},{56,6... | collective-permute-start | bytes 12296 | tf_op jit(solution)/shard_map/ppermute | solution.py:379

commit v9 on v8

--- a/solution.py
+++ b/solution.py
@@ -30,7 +30,6 @@
 BF16 = jnp.bfloat16
 WHOLE = pl.BlockSpec()
 SMEM = pl.BlockSpec(memory_space=pltpu.SMEM)
-ANY = pl.BlockSpec(memory_space=pl.ANY)
 HEAVY = pl.CostEstimate(flops=0, transcendentals=0, bytes_accessed=60_000_000)
 LIGHT = pl.CostEstimate(flops=0, transcendentals=0, bytes_accessed=0)
 
@@ -320,15 +319,8 @@
 def sample_kernel(
     slot_ref, rank_ref, core_ref, received_ref, *refs
 ):
-    pieces, others = refs[0:4], refs[4:8]
-    density_ref, left_ref, sample_ref, turn_ref, swapped_ref, sem = refs[8:]
-    copies = [
-        pltpu.make_async_copy(other.at[e, 1], swapped_ref.at[i, e, 1], sem.at[i, e])
-        for i, other in enumerate(others)
-        for e in range(2)
-    ]
-    for copy in copies:
-        copy.start()
+    pieces, swapped = refs[0:4], refs[4:8]
+    density_ref, left_ref, sample_ref, turn_ref = refs[8:]
     rank, core = rank_ref[0], core_ref[0]
     for distance in range(4):
         source = (rank - 2 * distance + 8) % 8
@@ -340,12 +332,8 @@
             left_ref[64:128, low : low + 64] = block[:, 64:128]
     left = left_ref[...]
     scale = 1.0 / math.sqrt(512.0)
-    swapped = [swapped_ref.at[i] for i in range(4)]
     sides = ((pieces, 0, 16 * core), (pieces, 1, 8), (swapped, 1, 16 - 16 * core))
-    for side, (source_refs, index, base) in enumerate(sides):
-        if side == 2:
-            for copy in copies:
-                copy.wait()
+    for source_refs, index, base in sides:
         for pair in range(4):
             c = 2 * pair
             right = jnp.concatenate(
@@ -389,7 +377,7 @@
     both = lambda block: (around(block, space_count, 1), around(block, space_count, -1))
 
     coords = jnp.pad(positions.transpose(1, 0, 2), ((0, 0), (0, 0), (0, 96)))
-    own = jnp.concatenate([probes.reshape(512, 128), coords.reshape(24, 128)])
+    own = jnp.concatenate([probes.reshape(64, 8, 128), coords]).reshape(536, 128)
     before, after = both(own)
     core = space_rank % 2
     present = neighbours >= 0
@@ -481,14 +469,12 @@
     density = pl.pallas_call(
         sample_kernel,
         out_shape=jax.ShapeDtypeStruct((16, 15, 8, 128), BF16),
-        in_specs=[SMEM] * 3 + [WHOLE] * 5 + [ANY] * 4,
+        in_specs=[SMEM] * 3 + [WHOLE] * 9,
         out_specs=WHOLE,
         scratch_shapes=[
             pltpu.VMEM((128, 512), BF16),
             pltpu.VMEM((NEAR + 1, 128, 128), F32),
             pltpu.VMEM((16 * 120, 128), F32),
-            pltpu.VMEM((4, 2, 2, 512, 128), BF16),
-            pltpu.SemaphoreType.DMA((4, 2)),
         ],
         compiler_params=params(16),
         name="sample",

time: 86.6 us -> 85.9 us (level)
    reshape x0 -> x1, other arithmetic: none -> 0.94 us  [per_device(): jnp.concatenate([probes.reshape(64, 8, 128), coords]).reshape(536, 128)]
    concatenate x1 -> x0, other arithmetic: 0.91 us -> none  [per_device(): own = jnp.concatenate([probes.reshape(512, 128), coords.reshape(24, 128)])]
  transfers between devices with their start and end apart: 16 -> 16, of which waited for: 7 -> 7; matrix products, arithmetic and copies ran while one was open for 1% -> 1% of each run, Pallas kernels for 17% -> 16%
where the time goes in v9:
time: 85.9 us; the launch traced here: 85.3 us
  starting transfers between devices  37.2 us (43%)
  waiting for transfers between devices  27.9 us (32%)
  Pallas kernels  17.1 us (20%)
  other arithmetic  2.31 us (3%)
    ppermute x6, starting transfers between devices, around(): lax.ppermute(block, 'space', [((i - distance) % size, i) for i in range(s...  16.4 us
    ppermute x6, waiting for transfers between devices, around(): lax.ppermute(block, 'space', [((i - distance) % size, i) for i in range(s...  11.3 us
    all_to_all x1, waiting for transfers between devices, per_device(): peaks = lax.all_to_all(peak, 'space', 0, 0, tiled=True)  8.78 us
    all_to_all x1, starting transfers between devices, per_device(): peaks = lax.all_to_all(peak, 'space', 0, 0, tiled=True)  8.18 us
    pallas_call x1, Pallas kernels, per_device(): pl.pallas_call(second_kernel, out_shape=jax.ShapeDtypeStruct((8, 88, 128)...  6.39 us
    ppermute x4, starting transfers between devices, along_probe(): return lax.ppermute(block, 'probe', [(i, target(i)) for i in range(8)])  5.99 us
    all_to_all x1, starting transfers between devices, per_device(): received = lax.all_to_all(send, 'probe', 0, 0, tiled=True)  5.55 us
    all_to_all x1, waiting for transfers between devices, per_device(): received = lax.all_to_all(send, 'probe', 0, 0, tiled=True)  5.44 us
  transfers between devices with their start and end apart: 16, of which 7 were waited for; matrix products, arithmetic and copies ran while one was open for 1% of the time, Pallas kernels for 16%

profile of v9, /device:TPU:2, one launch (start us, length us, event | category | flops | bytes accessed | tf_op | source)
XLA Modules:
  0.0 85.3 jit_solution(1187242435283108028)
XLA Ops:
  0.6 0.9 %fusion.2.own_ref = bf16[536,128]{1,0:T(8,128)(2,1)S(1)} fusion(bf16[3,8,32]{2,1,0:T(8,128)(2,1)} %bitcast.26, bf16[64,8,128]{2,1,0:T(8,128)(2,1)} %bitcast.25), kind=kLoop, calls=%fused_computation.4 | loop fusion | flops 411648 | bytes 269824 | tf_op jit(solution)/shard_map/reshape | solution.py:380
  1.6 0.1 collective-permute-start
  1.7 8.3 %collective-permute-start.1 = (bf16[536,128]{1,0:T(8,128)(2,1)S(1)}, bf16[536,128]{1,0:T(8,128)(2,1)S(1)}, u32[]{:S(2)}, u32[]{:S(2)}) collective-permute-start(bf16[536,128]{1,0:T(8,128)(2,1)S(1)} %fusion.2.own_ref), channel_id=1, source_target_pairs={{8,0},{16,8},{24,16},{32,24},{40,32},{48,40},{56,48},{64,56},{72,6... | collective-permute-start | bytes 411656 | tf_op jit(solution)/shard_map/ppermute | solution.py:367
  9.9 0.7 fusion.8
  10.6 2.0 %collective-permute-done.before_ref = bf16[536,128]{1,0:T(8,128)(2,1)S(1)} collective-permute-done((bf16[536,128]{1,0:T(8,128)(2,1)S(1)}, bf16[536,128]{1,0:T(8,128)(2,1)S(1)}, u32[]{:S(2)}, u32[]{:S(2)}) %collective-permute-start) | collective-permute-done | bytes 137248 | tf_op jit(solution)/shard_map/ppermute | solution.py:367
  12.7 1.3 %collective-permute-done.1.after_ref = bf16[536,128]{1,0:T(8,128)(2,1)S(1)} collective-permute-done((bf16[536,128]{1,0:T(8,128)(2,1)S(1)}, bf16[536,128]{1,0:T(8,128)(2,1)S(1)}, u32[]{:S(2)}, u32[]{:S(2)}) %collective-permute-start.1) | collective-permute-done | bytes 137248 | tf_op jit(solution)/shard_map/ppermute | solution.py:367
  14.0 3.1 %spectral.1 = (f32[25,8,128]{2,1,0:T(8,128)S(1)}, f32[8,3,32,128]{3,2,1,0:T(8,128)S(1)}, f32[32,128]{1,0:T(8,128)}, bf16[2,512,128]{2,1,0:T(8,128)(2,1)S(1)}) custom-call(s32[8,16]{1,0:T(8,128)S(1)} %pad.9.slot_ref, s32[1]{0:T(128)} %bitcast.4.core_ref, bf16[536,128]{1,0:T(8,128)(2,1)S(1)} %collective-permute-done.before_ref, ...), custom_call_target="tpu_custom_call" | custom-call | bytes 60000000 | tf_op jit(solution)/shard_map/spectral/pallas_call | solution.py:388
  17.1 1.2 %collective-permute-start.2 = (bf16[2,512,128]{2,1,0:T(8,128)(2,1)S(1)}, bf16[2,512,128]{2,1,0:T(8,128)(2,1)S(1)}, u32[]{:S(2)}, u32[]{:S(2)}) collective-permute-start(bf16[2,512,128]{2,1,0:T(8,128)(2,1)S(1)} %get-tuple-element.47), channel_id=1, source_target_pairs={{0,1},{1,0},{2,3},{3,2},{4,5},{5,4},{6,7},{7,6},{8,9},{9,8},{10,11... | collective-permute-start | bytes 786440 | tf_op jit(solution)/shard_map/ppermute | solution.py:371
  18.2 8.2 %all-to-all-start = ((f32[32,1,128]{2,1,0:T(1,128)}), f32[32,1,128]{2,1,0:T(1,128)S(1)}, u32[]{:S(2)}, u32[]{:S(2)}) async-start(f32[32,1,128]{2,1,0:T(1,128)} %bitcast.6), calls=%async_computation | async-start | bytes 32768 | tf_op jit(solution)/shard_map/all_to_all | solution.py:405
  26.4 0.9 %prepare.1 = (bf16[25,128,64]{2,1,0:T(8,128)(2,1)S(1)}, f32[24,128]{1,0:T(8,128)S(1)}) custom-call(s32[8,16]{1,0:T(8,128)S(1)} %pad.9.slot_ref, bf16[536,128]{1,0:T(8,128)(2,1)S(1)} %collective-permute-done.before_ref, bf16[536,128]{1,0:T(8,128)(2,1)S(1)} %fusion.2.own_ref, bf16[536,128]{1,0:T(8,128)(2,1)S(1)} %collective-permute-done.1.after_ref), custom_call_target="tpu_custom_call" | custom-call | tf_op jit(solution)/shard_map/prepare/pallas_call | solution.py:406
  27.3 8.8 %all-to-all-done = f32[32,1,128]{2,1,0:T(1,128)S(1)} async-done(((f32[32,1,128]{2,1,0:T(1,128)}), f32[32,1,128]{2,1,0:T(1,128)S(1)}, u32[]{:S(2)}, u32[]{:S(2)}) %all-to-all-start) | async-done | bytes 16416 | tf_op jit(solution)/shard_map/all_to_all | solution.py:405
  36.1 0.0 collective-permute-done.2
  36.1 0.1 pad_maximum_fusion.refs_0_
  36.2 1.6 %collective-permute-start.5 = (bf16[2,2,512,128]{3,2,1,0:T(8,128)(2,1)S(1)}, bf16[2,2,512,128]{3,2,1,0:T(8,128)(2,1)S(1)}, u32[]{:S(2)}, u32[]{:S(2)}) collective-permute-start(bf16[2,2,512,128]{3,2,1,0:T(8,128)(2,1)S(1)} %pad_maximum_fusion.refs_0_), channel_id=1, source_target_pairs={{0,2},{1,3},{2,4},{3,5},{4,6},{5,7},{6,0},{7,1},{8,10},{9,11},{10,... | collective-permute-start | bytes 1572872 | tf_op jit(solution)/shard_map/ppermute | solution.py:371
  37.7 1.1 %collective-permute-start.6 = (bf16[2,2,512,128]{3,2,1,0:T(8,128)(2,1)S(1)}, bf16[2,2,512,128]{3,2,1,0:T(8,128)(2,1)S(1)}, u32[]{:S(2)}, u32[]{:S(2)}) collective-permute-start(bf16[2,2,512,128]{3,2,1,0:T(8,128)(2,1)S(1)} %pad_maximum_fusion.refs_0_), channel_id=1, source_target_pairs={{0,4},{1,5},{2,6},{3,7},{4,0},{5,1},{6,2},{7,3},{8,12},{9,13},{10,... | collective-permute-start | bytes 1572872 | tf_op jit(solution)/shard_map/ppermute | solution.py:371
  38.9 2.2 %collective-permute-start.7 = (bf16[2,2,512,128]{3,2,1,0:T(8,128)(2,1)S(1)}, bf16[2,2,512,128]{3,2,1,0:T(8,128)(2,1)S(1)}, u32[]{:S(2)}, u32[]{:S(2)}) collective-permute-start(bf16[2,2,512,128]{3,2,1,0:T(8,128)(2,1)S(1)} %pad_maximum_fusion.refs_0_), channel_id=1, source_target_pairs={{0,6},{1,7},{2,0},{3,1},{4,2},{5,3},{6,4},{7,5},{8,14},{9,15},{10,... | collective-permute-start | bytes 1572872 | tf_op jit(solution)/shard_map/ppermute | solution.py:371
  41.0 3.4 %first.1 = (bf16[8,128,2048]{2,1,0:T(8,128)(2,1)S(1)}, bf16[8,2048,64]{2,1,0:T(8,128)(2,1)S(1)}, f32[8,128,64]{2,1,0:T(8,128)S(1)}, bf16[4,128,128]{2,1,0:T(8,128)(2,1)S(1)}) custom-call(s32[8,16]{1,0:T(8,128)S(1)} %pad.9.slot_ref, f32[32,128]{1,0:T(8,128)S(1)} %bitcast.22, f32[25,8,128]{2,1,0:T(8,128)S(1)} %get-tuple-element.31.near_ref, ...), custom_call_target="tpu_custom_call" | custom-call | tf_op jit(solution)/shard_map/first/pallas_call | solution.py:427
  44.4 0.1 collective-permute-start.3
  44.5 6.0 %collective-permute-start.4 = (bf16[4,128,128]{2,1,0:T(8,128)(2,1)S(1)}, bf16[4,128,128]{2,1,0:T(8,128)(2,1)S(1)}, u32[]{:S(2)}, u32[]{:S(2)}) collective-permute-start(bf16[4,128,128]{2,1,0:T(8,128)(2,1)S(1)} %get-tuple-element.45.own_ref), channel_id=1, source_target_pairs={{8,0},{16,8},{24,16},{32,24},{40,32},{48,40},{56,48},{64,56},{72,6... | collective-permute-start | bytes 393224 | tf_op jit(solution)/shard_map/ppermute | solution.py:367
  50.4 4.0 %collective-permute-done.3.before_ref = bf16[4,128,128]{2,1,0:T(8,128)(2,1)S(1)} collective-permute-done((bf16[4,128,128]{2,1,0:T(8,128)(2,1)S(1)}, bf16[4,128,128]{2,1,0:T(8,128)(2,1)S(1)}, u32[]{:S(2)}, u32[]{:S(2)}) %collective-permute-start.3) | collective-permute-done | bytes 131104 | tf_op jit(solution)/shard_map/ppermute | solution.py:367
  54.5 0.0 collective-permute-done.4.after_ref
  54.5 6.4 %second.1 = f32[8,88,128]{2,1,0:T(8,128)} custom-call(s32[8,16]{1,0:T(8,128)S(1)} %pad.9.slot_ref, f32[25,8,128]{2,1,0:T(8,128)S(1)} %get-tuple-element.31.near_ref, f32[8,3,32,128]{3,2,1,0:T(8,128)S(1)} %get-tuple-element.32.row_ref, bf16[8,128,2048]{2,1,0:T(8,128)(2,1)S(1)} %get-tuple-element.42.scaled_ref, ...), custom_call_target="tpu_custom_call" | custom-call | tf_op jit(solution)/shard_map/second/pallas_call | solution.py:444
  60.9 0.0 collective-permute-done.5.refs_1_
  60.9 0.0 collective-permute-done.6.refs_2_
  60.9 2.4 %collective-permute-done.7.refs_3_ = bf16[2,2,512,128]{3,2,1,0:T(8,128)(2,1)S(1)} collective-permute-done((bf16[2,2,512,128]{3,2,1,0:T(8,128)(2,1)S(1)}, bf16[2,2,512,128]{3,2,1,0:T(8,128)(2,1)S(1)}, u32[]{:S(2)}, u32[]{:S(2)}) %collective-permute-start.7) | collective-permute-done | bytes 524320 | tf_op jit(solution)/shard_map/ppermute | solution.py:371
  63.3 5.6 %all-to-all-start.1 = ((f32[8,88,128]{2,1,0:T(8,128)}), f32[8,88,128]{2,1,0:T(8,128)S(1)}, u32[]{:S(2)}, u32[]{:S(2)}) async-start(f32[8,88,128]{2,1,0:T(8,128)} %second.1), calls=%async_computation.1 | async-start | bytes 720896 | tf_op jit(solution)/shard_map/all_to_all | solution.py:464
  68.8 0.0 collective-permute-start.10
  68.8 0.5 collective-permute-start.11
  69.3 0.0 collective-permute-start.8
  69.3 0.5 collective-permute-start.9
  69.9 5.4 %all-to-all-done.1.received_ref = f32[8,88,128]{2,1,0:T(8,128)S(1)} async-done(((f32[8,88,128]{2,1,0:T(8,128)}), f32[8,88,128]{2,1,0:T(8,128)S(1)}, u32[]{:S(2)}, u32[]{:S(2)}) %all-to-all-start.1) | async-done | bytes 360480 | tf_op jit(solution)/shard_map/all_to_all | solution.py:464
  75.3 2.1 %collective-permute-start.12 = (f32[8,128]{1,0:T(8,128)S(1)}, f32[8,128]{1,0:T(8,128)S(1)}, u32[]{:S(2)}, u32[]{:S(2)}) collective-permute-start(f32[8,128]{1,0:T(8,128)S(1)} %get-tuple-element.54), channel_id=1, source_target_pairs={{8,0},{16,8},{24,16},{32,24},{40,32},{48,40},{56,48},{64,56},{72,6... | collective-permute-start | bytes 12296 | tf_op jit(solution)/shard_map/ppermute | solution.py:367
  77.4 0.0 collective-permute-done.10.refs_6_
  77.4 0.0 collective-permute-start.13
  77.4 0.0 collective-permute-done.11.refs_7_
  77.4 0.0 collective-permute-done.8.refs_4_
  77.4 0.0 collective-permute-done.9.refs_5_
  77.4 3.3 %sample.1 = bf16[16,15,8,128]{3,2,1,0:T(8,128)(2,1)} custom-call(s32[8,16]{1,0:T(8,128)S(1)} %pad.9.slot_ref, s32[1]{0:T(128)} %bitcast.3.rank_ref, s32[1]{0:T(128)} %bitcast.4.core_ref, f32[8,88,128]{2,1,0:T(8,128)S(1)} %all-to-all-done.1.received_ref, bf16[2,2,512,128]{3,2,1,0:T(8,128)(2,1)S(1)} %pad_maximum_fusion.refs_0_, ...), custom_call_target="tpu_custom_call" | custom-call | tf_op jit(solution)/shard_map/sample/pallas_call | solution.py:469
  80.7 0.0 collective-permute-done.12
  80.7 3.9 %collective-permute-done.13 = f32[8,128]{1,0:T(8,128)S(1)} collective-permute-done((f32[8,128]{1,0:T(8,128)S(1)}, f32[8,128]{1,0:T(8,128)S(1)}, u32[]{:S(2)}, u32[]{:S(2)}) %collective-permute-start.13) | collective-permute-done | bytes 4128 | tf_op jit(solution)/shard_map/ppermute | solution.py:367
  84.6 0.1 slice_bitcast_fusion.2
  84.7 0.6 maximum_bitcast_fusion
  (4 shorter events, 0.0 us)
Async XLA Ops:
  1.6 11.1 %collective-permute-start = (bf16[536,128]{1,0:T(8,128)(2,1)S(1)}, bf16[536,128]{1,0:T(8,128)(2,1)S(1)}, u32[]{:S(2)}, u32[]{:S(2)}) collective-permute-start(bf16[536,128]{1,0:T(8,128)(2,1)S(1)} %fusion.2.own_ref), channel_id=1, source_target_pairs={{248,0},{0,8},{8,16},{16,24},{24,32},{32,40},{40,48},{48,56},{56,6... | collective-permute-start | bytes 411656 | tf_op jit(solution)/shard_map/ppermute | solution.py:367
  1.7 12.3 %collective-permute-start.1 = (bf16[536,128]{1,0:T(8,128)(2,1)S(1)}, bf16[536,128]{1,0:T(8,128)(2,1)S(1)}, u32[]{:S(2)}, u32[]{:S(2)}) collective-permute-start(bf16[536,128]{1,0:T(8,128)(2,1)S(1)} %fusion.2.own_ref), channel_id=1, source_target_pairs={{8,0},{16,8},{24,16},{32,24},{40,32},{48,40},{56,48},{64,56},{72,6... | collective-permute-start | bytes 411656 | tf_op jit(solution)/shard_map/ppermute | solution.py:367
  17.1 19.1 %collective-permute-start.2 = (bf16[2,512,128]{2,1,0:T(8,128)(2,1)S(1)}, bf16[2,512,128]{2,1,0:T(8,128)(2,1)S(1)}, u32[]{:S(2)}, u32[]{:S(2)}) collective-permute-start(bf16[2,512,128]{2,1,0:T(8,128)(2,1)S(1)} %get-tuple-element.47), channel_id=1, source_target_pairs={{0,1},{1,0},{2,3},{3,2},{4,5},{5,4},{6,7},{7,6},{8,9},{9,8},{10,11... | collective-permute-start | bytes 786440 | tf_op jit(solution)/shard_map/ppermute | solution.py:371
  18.2 17.9 %all-to-all-start = ((f32[32,1,128]{2,1,0:T(1,128)}), f32[32,1,128]{2,1,0:T(1,128)S(1)}, u32[]{:S(2)}, u32[]{:S(2)}) async-start(f32[32,1,128]{2,1,0:T(1,128)} %bitcast.6), calls=%async_computation | async-start | bytes 32768 | tf_op jit(solution)/shard_map/all_to_all | solution.py:405
  36.2 24.7 %collective-permute-start.5 = (bf16[2,2,512,128]{3,2,1,0:T(8,128)(2,1)S(1)}, bf16[2,2,512,128]{3,2,1,0:T(8,128)(2,1)S(1)}, u32[]{:S(2)}, u32[]{:S(2)}) collective-permute-start(bf16[2,2,512,128]{3,2,1,0:T(8,128)(2,1)S(1)} %pad_maximum_fusion.refs_0_), channel_id=1, source_target_pairs={{0,2},{1,3},{2,4},{3,5},{4,6},{5,7},{6,0},{7,1},{8,10},{9,11},{10,... | collective-permute-start | bytes 1572872 | tf_op jit(solution)/shard_map/ppermute | solution.py:371
  37.7 23.1 %collective-permute-start.6 = (bf16[2,2,512,128]{3,2,1,0:T(8,128)(2,1)S(1)}, bf16[2,2,512,128]{3,2,1,0:T(8,128)(2,1)S(1)}, u32[]{:S(2)}, u32[]{:S(2)}) collective-permute-start(bf16[2,2,512,128]{3,2,1,0:T(8,128)(2,1)S(1)} %pad_maximum_fusion.refs_0_), channel_id=1, source_target_pairs={{0,4},{1,5},{2,6},{3,7},{4,0},{5,1},{6,2},{7,3},{8,12},{9,13},{10,... | collective-permute-start | bytes 1572872 | tf_op jit(solution)/shard_map/ppermute | solution.py:371
  38.9 24.4 %collective-permute-start.7 = (bf16[2,2,512,128]{3,2,1,0:T(8,128)(2,1)S(1)}, bf16[2,2,512,128]{3,2,1,0:T(8,128)(2,1)S(1)}, u32[]{:S(2)}, u32[]{:S(2)}) collective-permute-start(bf16[2,2,512,128]{3,2,1,0:T(8,128)(2,1)S(1)} %pad_maximum_fusion.refs_0_), channel_id=1, source_target_pairs={{0,6},{1,7},{2,0},{3,1},{4,2},{5,3},{6,4},{7,5},{8,14},{9,15},{10,... | collective-permute-start | bytes 1572872 | tf_op jit(solution)/shard_map/ppermute | solution.py:371
  44.4 10.1 %collective-permute-start.3 = (bf16[4,128,128]{2,1,0:T(8,128)(2,1)S(1)}, bf16[4,128,128]{2,1,0:T(8,128)(2,1)S(1)}, u32[]{:S(2)}, u32[]{:S(2)}) collective-permute-start(bf16[4,128,128]{2,1,0:T(8,128)(2,1)S(1)} %get-tuple-element.45.own_ref), channel_id=1, source_target_pairs={{248,0},{0,8},{8,16},{16,24},{24,32},{32,40},{40,48},{48,56},{56,6... | collective-permute-start | bytes 393224 | tf_op jit(solution)/shard_map/ppermute | solution.py:367
  44.5 10.0 %collective-permute-start.4 = (bf16[4,128,128]{2,1,0:T(8,128)(2,1)S(1)}, bf16[4,128,128]{2,1,0:T(8,128)(2,1)S(1)}, u32[]{:S(2)}, u32[]{:S(2)}) collective-permute-start(bf16[4,128,128]{2,1,0:T(8,128)(2,1)S(1)} %get-tuple-element.45.own_ref), channel_id=1, source_target_pairs={{8,0},{16,8},{24,16},{32,24},{40,32},{48,40},{56,48},{64,56},{72,6... | collective-permute-start | bytes 393224 | tf_op jit(solution)/shard_map/ppermute | solution.py:367
  63.3 12.0 %all-to-all-start.1 = ((f32[8,88,128]{2,1,0:T(8,128)}), f32[8,88,128]{2,1,0:T(8,128)S(1)}, u32[]{:S(2)}, u32[]{:S(2)}) async-start(f32[8,88,128]{2,1,0:T(8,128)} %second.1), calls=%async_computation.1 | async-start | bytes 720896 | tf_op jit(solution)/shard_map/all_to_all | solution.py:464
  68.8 8.5 %collective-permute-start.10 = (bf16[2,2,512,128]{3,2,1,0:T(8,128)(2,1)S(1)}, bf16[2,2,512,128]{3,2,1,0:T(8,128)(2,1)}, u32[]{:S(2)}, u32[]{:S(2)}) collective-permute-start(bf16[2,2,512,128]{3,2,1,0:T(8,128)(2,1)S(1)} %collective-permute-done.6.refs_2_), channel_id=1, source_target_pairs={{0,8},{8,0},{16,24},{24,16},{32,40},{40,32},{48,56},{56,48},{64,72... | collective-permute-start | bytes 1572872 | tf_op jit(solution)/shard_map/ppermute | solution.py:462
  68.8 8.5 %collective-permute-start.11 = (bf16[2,2,512,128]{3,2,1,0:T(8,128)(2,1)S(1)}, bf16[2,2,512,128]{3,2,1,0:T(8,128)(2,1)}, u32[]{:S(2)}, u32[]{:S(2)}) collective-permute-start(bf16[2,2,512,128]{3,2,1,0:T(8,128)(2,1)S(1)} %collective-permute-done.7.refs_3_), channel_id=1, source_target_pairs={{0,8},{8,0},{16,24},{24,16},{32,40},{40,32},{48,56},{56,48},{64,72... | collective-permute-start | bytes 1572872 | tf_op jit(solution)/shard_map/ppermute | solution.py:462
  69.3 8.0 %collective-permute-start.8 = (bf16[2,2,512,128]{3,2,1,0:T(8,128)(2,1)S(1)}, bf16[2,2,512,128]{3,2,1,0:T(8,128)(2,1)}, u32[]{:S(2)}, u32[]{:S(2)}) collective-permute-start(bf16[2,2,512,128]{3,2,1,0:T(8,128)(2,1)S(1)} %pad_maximum_fusion.refs_0_), channel_id=1, source_target_pairs={{0,8},{8,0},{16,24},{24,16},{32,40},{40,32},{48,56},{56,48},{64,72... | collective-permute-start | bytes 1572872 | tf_op jit(solution)/shard_map/ppermute | solution.py:462
  69.3 8.1 %collective-permute-start.9 = (bf16[2,2,512,128]{3,2,1,0:T(8,128)(2,1)S(1)}, bf16[2,2,512,128]{3,2,1,0:T(8,128)(2,1)}, u32[]{:S(2)}, u32[]{:S(2)}) collective-permute-start(bf16[2,2,512,128]{3,2,1,0:T(8,128)(2,1)S(1)} %collective-permute-done.5.refs_1_), channel_id=1, source_target_pairs={{0,8},{8,0},{16,24},{24,16},{32,40},{40,32},{48,56},{56,48},{64,72... | collective-permute-start | bytes 1572872 | tf_op jit(solution)/shard_map/ppermute | solution.py:462
  75.3 5.4 %collective-permute-start.12 = (f32[8,128]{1,0:T(8,128)S(1)}, f32[8,128]{1,0:T(8,128)S(1)}, u32[]{:S(2)}, u32[]{:S(2)}) collective-permute-start(f32[8,128]{1,0:T(8,128)S(1)} %get-tuple-element.54), channel_id=1, source_target_pairs={{8,0},{16,8},{24,16},{32,24},{40,32},{48,40},{56,48},{64,56},{72,6... | collective-permute-start | bytes 12296 | tf_op jit(solution)/shard_map/ppermute | solution.py:367
  77.4 7.3 %collective-permute-start.13 = (f32[8,128]{1,0:T(8,128)S(1)}, f32[8,128]{1,0:T(8,128)S(1)}, u32[]{:S(2)}, u32[]{:S(2)}) collective-permute-start(f32[8,128]{1,0:T(8,128)S(1)} %get-tuple-element.55), channel_id=1, source_target_pairs={{248,0},{0,8},{8,16},{16,24},{24,32},{32,40},{40,48},{48,56},{56,6... | collective-permute-start | bytes 12296 | tf_op jit(solution)/shard_map/ppermute | solution.py:367

commit v10 on v9

--- a/solution.py
+++ b/solution.py
@@ -415,10 +415,9 @@
         compiler_params=params(4),
         name="prepare",
     )(slot, *held)
-    peaks, pair, across, probe_turned = lax.optimization_barrier(
-        (peaks, pair, across, probe_turned)
-    )
-    quad = jnp.stack([pair, across])
+    peaks, quad, probe_turned = lax.optimization_barrier(
+        (peaks, jnp.stack([pair, across]), probe_turned)
+    )
     pieces = [quad] + [
         along_probe(quad, lambda i, distance=distance: (i + 2 * distance) % 8)
         for distance in range(1, 4)

time: 85.9 us -> 85.8 us (level)
  no operation moved by 1% of the time
where the time goes in v10:
time: 85.8 us; the launch traced here: 85.2 us
  starting transfers between devices  37.1 us (43%)
  waiting for transfers between devices  27.8 us (32%)
  Pallas kernels  17.1 us (20%)
  other arithmetic  2.32 us (3%)
    ppermute x6, starting transfers between devices, around(): lax.ppermute(block, 'space', [((i - distance) % size, i) for i in range(s...  16.4 us
    ppermute x6, waiting for transfers between devices, around(): lax.ppermute(block, 'space', [((i - distance) % size, i) for i in range(s...  11.3 us
    all_to_all x1, waiting for transfers between devices, per_device(): peaks = lax.all_to_all(peak, 'space', 0, 0, tiled=True)  8.71 us
    all_to_all x1, starting transfers between devices, per_device(): peaks = lax.all_to_all(peak, 'space', 0, 0, tiled=True)  8.18 us
    pallas_call x1, Pallas kernels, per_device(): pl.pallas_call(second_kernel, out_shape=jax.ShapeDtypeStruct((8, 88, 128)...  6.41 us
    ppermute x4, starting transfers between devices, along_probe(): return lax.ppermute(block, 'probe', [(i, target(i)) for i in range(8)])  5.91 us
    all_to_all x1, starting transfers between devices, per_device(): received = lax.all_to_all(send, 'probe', 0, 0, tiled=True)  5.55 us
    all_to_all x1, waiting for transfers between devices, per_device(): received = lax.all_to_all(send, 'probe', 0, 0, tiled=True)  5.44 us
  transfers between devices with their start and end apart: 16, of which 7 were waited for; matrix products, arithmetic and copies ran while one was open for 1% of the time, Pallas kernels for 16%

profile of v10, /device:TPU:2, one launch (start us, length us, event | category | flops | bytes accessed | tf_op | source)
XLA Modules:
  0.0 85.2 jit_solution(13904958960369829650)
XLA Ops:
  0.6 0.9 %fusion.2.own_ref = bf16[536,128]{1,0:T(8,128)(2,1)S(1)} fusion(bf16[3,8,32]{2,1,0:T(8,128)(2,1)} %bitcast.26, bf16[64,8,128]{2,1,0:T(8,128)(2,1)} %bitcast.25), kind=kLoop, calls=%fused_computation.4 | loop fusion | flops 411648 | bytes 269824 | tf_op jit(solution)/shard_map/reshape | solution.py:380
  1.6 0.1 collective-permute-start
  1.7 8.3 %collective-permute-start.1 = (bf16[536,128]{1,0:T(8,128)(2,1)S(1)}, bf16[536,128]{1,0:T(8,128)(2,1)S(1)}, u32[]{:S(2)}, u32[]{:S(2)}) collective-permute-start(bf16[536,128]{1,0:T(8,128)(2,1)S(1)} %fusion.2.own_ref), channel_id=1, source_target_pairs={{8,0},{16,8},{24,16},{32,24},{40,32},{48,40},{56,48},{64,56},{72,6... | collective-permute-start | bytes 411656 | tf_op jit(solution)/shard_map/ppermute | solution.py:367
  9.9 0.7 fusion.8
  10.6 2.0 %collective-permute-done.before_ref = bf16[536,128]{1,0:T(8,128)(2,1)S(1)} collective-permute-done((bf16[536,128]{1,0:T(8,128)(2,1)S(1)}, bf16[536,128]{1,0:T(8,128)(2,1)S(1)}, u32[]{:S(2)}, u32[]{:S(2)}) %collective-permute-start) | collective-permute-done | bytes 137248 | tf_op jit(solution)/shard_map/ppermute | solution.py:367
  12.7 1.3 %collective-permute-done.1.after_ref = bf16[536,128]{1,0:T(8,128)(2,1)S(1)} collective-permute-done((bf16[536,128]{1,0:T(8,128)(2,1)S(1)}, bf16[536,128]{1,0:T(8,128)(2,1)S(1)}, u32[]{:S(2)}, u32[]{:S(2)}) %collective-permute-start.1) | collective-permute-done | bytes 137248 | tf_op jit(solution)/shard_map/ppermute | solution.py:367
  14.0 3.1 %spectral.1 = (f32[25,8,128]{2,1,0:T(8,128)S(1)}, f32[8,3,32,128]{3,2,1,0:T(8,128)S(1)}, f32[32,128]{1,0:T(8,128)}, bf16[2,512,128]{2,1,0:T(8,128)(2,1)S(1)}) custom-call(s32[8,16]{1,0:T(8,128)S(1)} %pad.9.slot_ref, s32[1]{0:T(128)} %bitcast.4.core_ref, bf16[536,128]{1,0:T(8,128)(2,1)S(1)} %collective-permute-done.before_ref, ...), custom_call_target="tpu_custom_call" | custom-call | bytes 60000000 | tf_op jit(solution)/shard_map/spectral/pallas_call | solution.py:388
  17.1 1.2 %collective-permute-start.2 = (bf16[2,512,128]{2,1,0:T(8,128)(2,1)S(1)}, bf16[2,512,128]{2,1,0:T(8,128)(2,1)S(1)}, u32[]{:S(2)}, u32[]{:S(2)}) collective-permute-start(bf16[2,512,128]{2,1,0:T(8,128)(2,1)S(1)} %get-tuple-element.34), channel_id=1, source_target_pairs={{0,1},{1,0},{2,3},{3,2},{4,5},{5,4},{6,7},{7,6},{8,9},{9,8},{10,11... | collective-permute-start | bytes 786440 | tf_op jit(solution)/shard_map/ppermute | solution.py:371
  18.2 8.2 %all-to-all-start = ((f32[32,1,128]{2,1,0:T(1,128)}), f32[32,1,128]{2,1,0:T(1,128)S(1)}, u32[]{:S(2)}, u32[]{:S(2)}) async-start(f32[32,1,128]{2,1,0:T(1,128)} %bitcast.6), calls=%async_computation | async-start | bytes 32768 | tf_op jit(solution)/shard_map/all_to_all | solution.py:405
  26.4 0.9 %prepare.1 = (bf16[25,128,64]{2,1,0:T(8,128)(2,1)S(1)}, f32[24,128]{1,0:T(8,128)S(1)}) custom-call(s32[8,16]{1,0:T(8,128)S(1)} %pad.9.slot_ref, bf16[536,128]{1,0:T(8,128)(2,1)S(1)} %collective-permute-done.before_ref, bf16[536,128]{1,0:T(8,128)(2,1)S(1)} %fusion.2.own_ref, bf16[536,128]{1,0:T(8,128)(2,1)S(1)} %collective-permute-done.1.after_ref), custom_call_target="tpu_custom_call" | custom-call | tf_op jit(solution)/shard_map/prepare/pallas_call | solution.py:406
  27.3 0.0 collective-permute-done.2
  27.4 0.1 pad_maximum_fusion.refs_0_
  27.4 8.7 %all-to-all-done = f32[32,1,128]{2,1,0:T(1,128)S(1)} async-done(((f32[32,1,128]{2,1,0:T(1,128)}), f32[32,1,128]{2,1,0:T(1,128)S(1)}, u32[]{:S(2)}, u32[]{:S(2)}) %all-to-all-start) | async-done | bytes 16416 | tf_op jit(solution)/shard_map/all_to_all | solution.py:405
  36.1 1.5 %collective-permute-start.5 = (bf16[2,2,512,128]{3,2,1,0:T(8,128)(2,1)S(1)}, bf16[2,2,512,128]{3,2,1,0:T(8,128)(2,1)S(1)}, u32[]{:S(2)}, u32[]{:S(2)}) collective-permute-start(bf16[2,2,512,128]{3,2,1,0:T(8,128)(2,1)S(1)} %pad_maximum_fusion.refs_0_), channel_id=1, source_target_pairs={{0,2},{1,3},{2,4},{3,5},{4,6},{5,7},{6,0},{7,1},{8,10},{9,11},{10,... | collective-permute-start | bytes 1572872 | tf_op jit(solution)/shard_map/ppermute | solution.py:371
  37.6 1.1 %collective-permute-start.6 = (bf16[2,2,512,128]{3,2,1,0:T(8,128)(2,1)S(1)}, bf16[2,2,512,128]{3,2,1,0:T(8,128)(2,1)S(1)}, u32[]{:S(2)}, u32[]{:S(2)}) collective-permute-start(bf16[2,2,512,128]{3,2,1,0:T(8,128)(2,1)S(1)} %pad_maximum_fusion.refs_0_), channel_id=1, source_target_pairs={{0,4},{1,5},{2,6},{3,7},{4,0},{5,1},{6,2},{7,3},{8,12},{9,13},{10,... | collective-permute-start | bytes 1572872 | tf_op jit(solution)/shard_map/ppermute | solution.py:371
  38.7 2.2 %collective-permute-start.7 = (bf16[2,2,512,128]{3,2,1,0:T(8,128)(2,1)S(1)}, bf16[2,2,512,128]{3,2,1,0:T(8,128)(2,1)S(1)}, u32[]{:S(2)}, u32[]{:S(2)}) collective-permute-start(bf16[2,2,512,128]{3,2,1,0:T(8,128)(2,1)S(1)} %pad_maximum_fusion.refs_0_), channel_id=1, source_target_pairs={{0,6},{1,7},{2,0},{3,1},{4,2},{5,3},{6,4},{7,5},{8,14},{9,15},{10,... | collective-permute-start | bytes 1572872 | tf_op jit(solution)/shard_map/ppermute | solution.py:371
  40.9 3.4 %first.1 = (bf16[8,128,2048]{2,1,0:T(8,128)(2,1)S(1)}, bf16[8,2048,64]{2,1,0:T(8,128)(2,1)S(1)}, f32[8,128,64]{2,1,0:T(8,128)S(1)}, bf16[4,128,128]{2,1,0:T(8,128)(2,1)S(1)}) custom-call(s32[8,16]{1,0:T(8,128)S(1)} %pad.9.slot_ref, f32[32,128]{1,0:T(8,128)S(1)} %bitcast.22, f32[25,8,128]{2,1,0:T(8,128)S(1)} %get-tuple-element.30.near_ref, ...), custom_call_target="tpu_custom_call" | custom-call | tf_op jit(solution)/shard_map/first/pallas_call | solution.py:426
  44.2 0.1 collective-permute-start.3
  44.3 6.0 %collective-permute-start.4 = (bf16[4,128,128]{2,1,0:T(8,128)(2,1)S(1)}, bf16[4,128,128]{2,1,0:T(8,128)(2,1)S(1)}, u32[]{:S(2)}, u32[]{:S(2)}) collective-permute-start(bf16[4,128,128]{2,1,0:T(8,128)(2,1)S(1)} %get-tuple-element.44.own_ref), channel_id=1, source_target_pairs={{8,0},{16,8},{24,16},{32,24},{40,32},{48,40},{56,48},{64,56},{72,6... | collective-permute-start | bytes 393224 | tf_op jit(solution)/shard_map/ppermute | solution.py:367
  50.3 4.0 %collective-permute-done.3.before_ref = bf16[4,128,128]{2,1,0:T(8,128)(2,1)S(1)} collective-permute-done((bf16[4,128,128]{2,1,0:T(8,128)(2,1)S(1)}, bf16[4,128,128]{2,1,0:T(8,128)(2,1)S(1)}, u32[]{:S(2)}, u32[]{:S(2)}) %collective-permute-start.3) | collective-permute-done | bytes 131104 | tf_op jit(solution)/shard_map/ppermute | solution.py:367
  54.3 0.0 collective-permute-done.4.after_ref
  54.3 6.4 %second.1 = f32[8,88,128]{2,1,0:T(8,128)} custom-call(s32[8,16]{1,0:T(8,128)S(1)} %pad.9.slot_ref, f32[25,8,128]{2,1,0:T(8,128)S(1)} %get-tuple-element.30.near_ref, f32[8,3,32,128]{3,2,1,0:T(8,128)S(1)} %get-tuple-element.31.row_ref, bf16[8,128,2048]{2,1,0:T(8,128)(2,1)S(1)} %get-tuple-element.41.scaled_ref, ...), custom_call_target="tpu_custom_call" | custom-call | tf_op jit(solution)/shard_map/second/pallas_call | solution.py:443
  60.7 0.0 collective-permute-done.5.refs_1_
  60.7 0.0 collective-permute-done.6.refs_2_
  60.7 2.4 %collective-permute-done.7.refs_3_ = bf16[2,2,512,128]{3,2,1,0:T(8,128)(2,1)S(1)} collective-permute-done((bf16[2,2,512,128]{3,2,1,0:T(8,128)(2,1)S(1)}, bf16[2,2,512,128]{3,2,1,0:T(8,128)(2,1)S(1)}, u32[]{:S(2)}, u32[]{:S(2)}) %collective-permute-start.7) | collective-permute-done | bytes 524320 | tf_op jit(solution)/shard_map/ppermute | solution.py:371
  63.1 5.6 %all-to-all-start.1 = ((f32[8,88,128]{2,1,0:T(8,128)}), f32[8,88,128]{2,1,0:T(8,128)S(1)}, u32[]{:S(2)}, u32[]{:S(2)}) async-start(f32[8,88,128]{2,1,0:T(8,128)} %second.1), calls=%async_computation.1 | async-start | bytes 720896 | tf_op jit(solution)/shard_map/all_to_all | solution.py:463
  68.7 0.0 collective-permute-start.10
  68.7 0.5 collective-permute-start.11
  69.2 0.0 collective-permute-start.8
  69.2 0.5 collective-permute-start.9
  69.7 5.4 %all-to-all-done.1.received_ref = f32[8,88,128]{2,1,0:T(8,128)S(1)} async-done(((f32[8,88,128]{2,1,0:T(8,128)}), f32[8,88,128]{2,1,0:T(8,128)S(1)}, u32[]{:S(2)}, u32[]{:S(2)}) %all-to-all-start.1) | async-done | bytes 360480 | tf_op jit(solution)/shard_map/all_to_all | solution.py:463
  75.2 2.1 %collective-permute-start.12 = (f32[8,128]{1,0:T(8,128)S(1)}, f32[8,128]{1,0:T(8,128)S(1)}, u32[]{:S(2)}, u32[]{:S(2)}) collective-permute-start(f32[8,128]{1,0:T(8,128)S(1)} %get-tuple-element.52), channel_id=1, source_target_pairs={{8,0},{16,8},{24,16},{32,24},{40,32},{48,40},{56,48},{64,56},{72,6... | collective-permute-start | bytes 12296 | tf_op jit(solution)/shard_map/ppermute | solution.py:367
  77.2 0.0 collective-permute-done.10.refs_6_
  77.2 0.0 collective-permute-start.13
  77.2 0.0 collective-permute-done.11.refs_7_
  77.2 0.0 collective-permute-done.8.refs_4_
  77.3 0.0 collective-permute-done.9.refs_5_
  77.3 3.3 %sample.1 = bf16[16,15,8,128]{3,2,1,0:T(8,128)(2,1)} custom-call(s32[8,16]{1,0:T(8,128)S(1)} %pad.9.slot_ref, s32[1]{0:T(128)} %bitcast.3.rank_ref, s32[1]{0:T(128)} %bitcast.4.core_ref, f32[8,88,128]{2,1,0:T(8,128)S(1)} %all-to-all-done.1.received_ref, bf16[2,2,512,128]{3,2,1,0:T(8,128)(2,1)S(1)} %pad_maximum_fusion.refs_0_, ...), custom_call_target="tpu_custom_call" | custom-call | tf_op jit(solution)/shard_map/sample/pallas_call | solution.py:468
  80.6 0.0 collective-permute-done.12
  80.6 3.9 %collective-permute-done.13 = f32[8,128]{1,0:T(8,128)S(1)} collective-permute-done((f32[8,128]{1,0:T(8,128)S(1)}, f32[8,128]{1,0:T(8,128)S(1)}, u32[]{:S(2)}, u32[]{:S(2)}) %collective-permute-start.13) | collective-permute-done | bytes 4128 | tf_op jit(solution)/shard_map/ppermute | solution.py:367
  84.5 0.1 slice_bitcast_fusion.2
  84.6 0.6 maximum_bitcast_fusion
  (4 shorter events, 0.0 us)
Async XLA Ops:
  1.6 11.1 %collective-permute-start = (bf16[536,128]{1,0:T(8,128)(2,1)S(1)}, bf16[536,128]{1,0:T(8,128)(2,1)S(1)}, u32[]{:S(2)}, u32[]{:S(2)}) collective-permute-start(bf16[536,128]{1,0:T(8,128)(2,1)S(1)} %fusion.2.own_ref), channel_id=1, source_target_pairs={{248,0},{0,8},{8,16},{16,24},{24,32},{32,40},{40,48},{48,56},{56,6... | collective-permute-start | bytes 411656 | tf_op jit(solution)/shard_map/ppermute | solution.py:367
  1.7 12.3 %collective-permute-start.1 = (bf16[536,128]{1,0:T(8,128)(2,1)S(1)}, bf16[536,128]{1,0:T(8,128)(2,1)S(1)}, u32[]{:S(2)}, u32[]{:S(2)}) collective-permute-start(bf16[536,128]{1,0:T(8,128)(2,1)S(1)} %fusion.2.own_ref), channel_id=1, source_target_pairs={{8,0},{16,8},{24,16},{32,24},{40,32},{48,40},{56,48},{64,56},{72,6... | collective-permute-start | bytes 411656 | tf_op jit(solution)/shard_map/ppermute | solution.py:367
  17.1 10.3 %collective-permute-start.2 = (bf16[2,512,128]{2,1,0:T(8,128)(2,1)S(1)}, bf16[2,512,128]{2,1,0:T(8,128)(2,1)S(1)}, u32[]{:S(2)}, u32[]{:S(2)}) collective-permute-start(bf16[2,512,128]{2,1,0:T(8,128)(2,1)S(1)} %get-tuple-element.34), channel_id=1, source_target_pairs={{0,1},{1,0},{2,3},{3,2},{4,5},{5,4},{6,7},{7,6},{8,9},{9,8},{10,11... | collective-permute-start | bytes 786440 | tf_op jit(solution)/shard_map/ppermute | solution.py:371
  18.2 17.9 %all-to-all-start = ((f32[32,1,128]{2,1,0:T(1,128)}), f32[32,1,128]{2,1,0:T(1,128)S(1)}, u32[]{:S(2)}, u32[]{:S(2)}) async-start(f32[32,1,128]{2,1,0:T(1,128)} %bitcast.6), calls=%async_computation | async-start | bytes 32768 | tf_op jit(solution)/shard_map/all_to_all | solution.py:405
  36.1 24.6 %collective-permute-start.5 = (bf16[2,2,512,128]{3,2,1,0:T(8,128)(2,1)S(1)}, bf16[2,2,512,128]{3,2,1,0:T(8,128)(2,1)S(1)}, u32[]{:S(2)}, u32[]{:S(2)}) collective-permute-start(bf16[2,2,512,128]{3,2,1,0:T(8,128)(2,1)S(1)} %pad_maximum_fusion.refs_0_), channel_id=1, source_target_pairs={{0,2},{1,3},{2,4},{3,5},{4,6},{5,7},{6,0},{7,1},{8,10},{9,11},{10,... | collective-permute-start | bytes 1572872 | tf_op jit(solution)/shard_map/ppermute | solution.py:371
  37.6 23.1 %collective-permute-start.6 = (bf16[2,2,512,128]{3,2,1,0:T(8,128)(2,1)S(1)}, bf16[2,2,512,128]{3,2,1,0:T(8,128)(2,1)S(1)}, u32[]{:S(2)}, u32[]{:S(2)}) collective-permute-start(bf16[2,2,512,128]{3,2,1,0:T(8,128)(2,1)S(1)} %pad_maximum_fusion.refs_0_), channel_id=1, source_target_pairs={{0,4},{1,5},{2,6},{3,7},{4,0},{5,1},{6,2},{7,3},{8,12},{9,13},{10,... | collective-permute-start | bytes 1572872 | tf_op jit(solution)/shard_map/ppermute | solution.py:371
  38.7 24.4 %collective-permute-start.7 = (bf16[2,2,512,128]{3,2,1,0:T(8,128)(2,1)S(1)}, bf16[2,2,512,128]{3,2,1,0:T(8,128)(2,1)S(1)}, u32[]{:S(2)}, u32[]{:S(2)}) collective-permute-start(bf16[2,2,512,128]{3,2,1,0:T(8,128)(2,1)S(1)} %pad_maximum_fusion.refs_0_), channel_id=1, source_target_pairs={{0,6},{1,7},{2,0},{3,1},{4,2},{5,3},{6,4},{7,5},{8,14},{9,15},{10,... | collective-permute-start | bytes 1572872 | tf_op jit(solution)/shard_map/ppermute | solution.py:371
  44.2 10.1 %collective-permute-start.3 = (bf16[4,128,128]{2,1,0:T(8,128)(2,1)S(1)}, bf16[4,128,128]{2,1,0:T(8,128)(2,1)S(1)}, u32[]{:S(2)}, u32[]{:S(2)}) collective-permute-start(bf16[4,128,128]{2,1,0:T(8,128)(2,1)S(1)} %get-tuple-element.44.own_ref), channel_id=1, source_target_pairs={{248,0},{0,8},{8,16},{16,24},{24,32},{32,40},{40,48},{48,56},{56,6... | collective-permute-start | bytes 393224 | tf_op jit(solution)/shard_map/ppermute | solution.py:367
  44.3 10.0 %collective-permute-start.4 = (bf16[4,128,128]{2,1,0:T(8,128)(2,1)S(1)}, bf16[4,128,128]{2,1,0:T(8,128)(2,1)S(1)}, u32[]{:S(2)}, u32[]{:S(2)}) collective-permute-start(bf16[4,128,128]{2,1,0:T(8,128)(2,1)S(1)} %get-tuple-element.44.own_ref), channel_id=1, source_target_pairs={{8,0},{16,8},{24,16},{32,24},{40,32},{48,40},{56,48},{64,56},{72,6... | collective-permute-start | bytes 393224 | tf_op jit(solution)/shard_map/ppermute | solution.py:367
  63.1 12.0 %all-to-all-start.1 = ((f32[8,88,128]{2,1,0:T(8,128)}), f32[8,88,128]{2,1,0:T(8,128)S(1)}, u32[]{:S(2)}, u32[]{:S(2)}) async-start(f32[8,88,128]{2,1,0:T(8,128)} %second.1), calls=%async_computation.1 | async-start | bytes 720896 | tf_op jit(solution)/shard_map/all_to_all | solution.py:463
  68.7 8.5 %collective-permute-start.10 = (bf16[2,2,512,128]{3,2,1,0:T(8,128)(2,1)S(1)}, bf16[2,2,512,128]{3,2,1,0:T(8,128)(2,1)}, u32[]{:S(2)}, u32[]{:S(2)}) collective-permute-start(bf16[2,2,512,128]{3,2,1,0:T(8,128)(2,1)S(1)} %collective-permute-done.6.refs_2_), channel_id=1, source_target_pairs={{0,8},{8,0},{16,24},{24,16},{32,40},{40,32},{48,56},{56,48},{64,72... | collective-permute-start | bytes 1572872 | tf_op jit(solution)/shard_map/ppermute | solution.py:461
  68.7 8.5 %collective-permute-start.11 = (bf16[2,2,512,128]{3,2,1,0:T(8,128)(2,1)S(1)}, bf16[2,2,512,128]{3,2,1,0:T(8,128)(2,1)}, u32[]{:S(2)}, u32[]{:S(2)}) collective-permute-start(bf16[2,2,512,128]{3,2,1,0:T(8,128)(2,1)S(1)} %collective-permute-done.7.refs_3_), channel_id=1, source_target_pairs={{0,8},{8,0},{16,24},{24,16},{32,40},{40,32},{48,56},{56,48},{64,72... | collective-permute-start | bytes 1572872 | tf_op jit(solution)/shard_map/ppermute | solution.py:461
  69.2 8.0 %collective-permute-start.8 = (bf16[2,2,512,128]{3,2,1,0:T(8,128)(2,1)S(1)}, bf16[2,2,512,128]{3,2,1,0:T(8,128)(2,1)}, u32[]{:S(2)}, u32[]{:S(2)}) collective-permute-start(bf16[2,2,512,128]{3,2,1,0:T(8,128)(2,1)S(1)} %pad_maximum_fusion.refs_0_), channel_id=1, source_target_pairs={{0,8},{8,0},{16,24},{24,16},{32,40},{40,32},{48,56},{56,48},{64,72... | collective-permute-start | bytes 1572872 | tf_op jit(solution)/shard_map/ppermute | solution.py:461
  69.2 8.1 %collective-permute-start.9 = (bf16[2,2,512,128]{3,2,1,0:T(8,128)(2,1)S(1)}, bf16[2,2,512,128]{3,2,1,0:T(8,128)(2,1)}, u32[]{:S(2)}, u32[]{:S(2)}) collective-permute-start(bf16[2,2,512,128]{3,2,1,0:T(8,128)(2,1)S(1)} %collective-permute-done.5.refs_1_), channel_id=1, source_target_pairs={{0,8},{8,0},{16,24},{24,16},{32,40},{40,32},{48,56},{56,48},{64,72... | collective-permute-start | bytes 1572872 | tf_op jit(solution)/shard_map/ppermute | solution.py:461
  75.2 5.4 %collective-permute-start.12 = (f32[8,128]{1,0:T(8,128)S(1)}, f32[8,128]{1,0:T(8,128)S(1)}, u32[]{:S(2)}, u32[]{:S(2)}) collective-permute-start(f32[8,128]{1,0:T(8,128)S(1)} %get-tuple-element.52), channel_id=1, source_target_pairs={{8,0},{16,8},{24,16},{32,24},{40,32},{48,40},{56,48},{64,56},{72,6... | collective-permute-start | bytes 12296 | tf_op jit(solution)/shard_map/ppermute | solution.py:367
  77.2 7.3 %collective-permute-start.13 = (f32[8,128]{1,0:T(8,128)S(1)}, f32[8,128]{1,0:T(8,128)S(1)}, u32[]{:S(2)}, u32[]{:S(2)}) collective-permute-start(f32[8,128]{1,0:T(8,128)S(1)} %get-tuple-element.53), channel_id=1, source_target_pairs={{248,0},{0,8},{8,16},{16,24},{24,32},{32,40},{40,48},{48,56},{56,6... | collective-permute-start | bytes 12296 | tf_op jit(solution)/shard_map/ppermute | solution.py:367

commit v11 on v10

--- a/solution.py
+++ b/solution.py
@@ -316,11 +316,16 @@
     return [across * (mixed[x] + bent[x]) + inward * d[x] for x in range(3)]
 
 
+def both_halves(refs):
+    own, first, second, third, last = refs
+    return [own.at[0], own.at[1], first.at[0], first.at[1], second, third, last.at[0], last.at[1]]
+
+
 def sample_kernel(
     slot_ref, rank_ref, core_ref, received_ref, *refs
 ):
-    pieces, swapped = refs[0:4], refs[4:8]
-    density_ref, left_ref, sample_ref, turn_ref = refs[8:]
+    pieces, swapped = both_halves(refs[0:5]), both_halves(refs[5:10])
+    density_ref, left_ref, sample_ref, turn_ref = refs[10:]
     rank, core = rank_ref[0], core_ref[0]
     for distance in range(4):
         source = (rank - 2 * distance + 8) % 8
@@ -340,9 +345,7 @@
                 [
                     jnp.concatenate(
                         [
-                            ref[e, index, 64 * n : 64 * n + 64, :]
-                            for ref in source_refs
-                            for e in range(2)
+                            ref[index, 64 * n : 64 * n + 64, :] for ref in source_refs
                         ],
                         axis=0,
                     )
@@ -418,10 +421,8 @@
     peaks, quad, probe_turned = lax.optimization_barrier(
         (peaks, jnp.stack([pair, across]), probe_turned)
     )
-    pieces = [quad] + [
-        along_probe(quad, lambda i, distance=distance: (i + 2 * distance) % 8)
-        for distance in range(1, 4)
-    ]
+    ahead, behind = lambda i: (i + 2) % 8, lambda i: (i + 6) % 8
+    one_back, one_on = along_probe(quad, ahead), along_probe(quad, behind)
 
     scaled, operand, one, half = pl.pallas_call(
         first_kernel,
@@ -439,6 +440,16 @@
         name="first",
     )(slot, peaks, near, rows, probe_turned)
     half_before, half_after = both(half)
+    half_before, half_after, one_back, one_on = lax.optimization_barrier(
+        (half_before, half_after, one_back, one_on)
+    )
+    pieces = [
+        quad,
+        one_back,
+        along_probe(one_back[0], ahead),
+        along_probe(one_on[1], behind),
+        one_on,
+    ]
 
     send = pl.pallas_call(
         second_kernel,
@@ -468,7 +479,7 @@
     density = pl.pallas_call(
         sample_kernel,
         out_shape=jax.ShapeDtypeStruct((16, 15, 8, 128), BF16),
-        in_specs=[SMEM] * 3 + [WHOLE] * 9,
+        in_specs=[SMEM] * 3 + [WHOLE] * 11,
         out_specs=WHOLE,
         scratch_shapes=[
             pltpu.VMEM((128, 512), BF16),

time: 85.8 us -> 84.5 us (0.985)
  starting transfers between devices: 37.1 us -> 27.3 us
  waiting for transfers between devices: 27.8 us -> 35.9 us
    ppermute x6, waiting for transfers between devices: 11.3 us -> 21.3 us  [around(): lax.ppermute(block, 'space', [((i - distance) % size, i) for i in range(s...]
    ppermute x6, starting transfers between devices: 16.4 us -> 9.44 us  [around(): lax.ppermute(block, 'space', [((i - distance) % size, i) for i in range(s...]
    all_to_all x1, starting transfers between devices: 8.18 us -> 3.83 us  [per_device(): peaks = lax.all_to_all(peak, 'space', 0, 0, tiled=True)]
    ppermute x4 -> x5, waiting for transfers between devices: 2.4 us -> 0.86 us  [along_probe(): return lax.ppermute(block, 'probe', [(i, target(i)) for i in range(8)])]
    ppermute x4 -> x5, starting transfers between devices: 5.91 us -> 6.71 us  [along_probe(): return lax.ppermute(block, 'probe', [(i, target(i)) for i in range(8)])]
  transfers between devices with their start and end apart: 16 -> 18, of which waited for: 7 -> 9; matrix products, arithmetic and copies ran while one was open for 1% -> 1% of each run, Pallas kernels for 16% -> 17%
where the time goes in v11:
time: 84.5 us; the launch traced here: 83.2 us
  waiting for transfers between devices  35.9 us (42%)
  starting transfers between devices  27.3 us (32%)
  Pallas kernels  16.9 us (20%)
  other arithmetic  2.31 us (3%)
    ppermute x6, waiting for transfers between devices, around(): lax.ppermute(block, 'space', [((i - distance) % size, i) for i in range(s...  21.3 us
    ppermute x6, starting transfers between devices, around(): lax.ppermute(block, 'space', [((i - distance) % size, i) for i in range(s...  9.44 us
    all_to_all x1, waiting for transfers between devices, per_device(): peaks = lax.all_to_all(peak, 'space', 0, 0, tiled=True)  8.69 us
    ppermute x5, starting transfers between devices, along_probe(): return lax.ppermute(block, 'probe', [(i, target(i)) for i in range(8)])  6.71 us
    pallas_call x1, Pallas kernels, per_device(): pl.pallas_call(second_kernel, out_shape=jax.ShapeDtypeStruct((8, 88, 128)...  6.39 us
    all_to_all x1, starting transfers between devices, per_device(): received = lax.all_to_all(send, 'probe', 0, 0, tiled=True)  6.24 us
    all_to_all x1, waiting for transfers between devices, per_device(): received = lax.all_to_all(send, 'probe', 0, 0, tiled=True)  5.01 us
    all_to_all x1, starting transfers between devices, per_device(): peaks = lax.all_to_all(peak, 'space', 0, 0, tiled=True)  3.83 us
  transfers between devices with their start and end apart: 18, of which 9 were waited for; matrix products, arithmetic and copies ran while one was open for 1% of the time, Pallas kernels for 17%

profile of v11, /device:TPU:2, one launch (start us, length us, event | category | flops | bytes accessed | tf_op | source)
XLA Modules:
  0.0 83.2 jit_solution(5443286856471657605)
XLA Ops:
  0.6 0.9 %fusion.2.own_ref = bf16[536,128]{1,0:T(8,128)(2,1)S(1)} fusion(bf16[3,8,32]{2,1,0:T(8,128)(2,1)} %bitcast.30, bf16[64,8,128]{2,1,0:T(8,128)(2,1)} %bitcast.29), kind=kLoop, calls=%fused_computation.6 | loop fusion | flops 411648 | bytes 269824 | tf_op jit(solution)/shard_map/reshape | solution.py:383
  1.6 8.3 %collective-permute-start.1 = (bf16[536,128]{1,0:T(8,128)(2,1)S(1)}, bf16[536,128]{1,0:T(8,128)(2,1)S(1)}, u32[]{:S(2)}, u32[]{:S(2)}) collective-permute-start(bf16[536,128]{1,0:T(8,128)(2,1)S(1)} %fusion.2.own_ref), channel_id=1, source_target_pairs={{8,0},{16,8},{24,16},{32,24},{40,32},{48,40},{56,48},{64,56},{72,6... | collective-permute-start | bytes 411656 | tf_op jit(solution)/shard_map/ppermute | solution.py:370
  9.8 0.0 collective-permute-start
  9.8 0.7 fusion.8
  10.6 3.3 %collective-permute-done.1.after_ref = bf16[536,128]{1,0:T(8,128)(2,1)S(1)} collective-permute-done((bf16[536,128]{1,0:T(8,128)(2,1)S(1)}, bf16[536,128]{1,0:T(8,128)(2,1)S(1)}, u32[]{:S(2)}, u32[]{:S(2)}) %collective-permute-start.1) | collective-permute-done | bytes 137248 | tf_op jit(solution)/shard_map/ppermute | solution.py:370
  13.9 5.5 %collective-permute-done.before_ref = bf16[536,128]{1,0:T(8,128)(2,1)S(1)} collective-permute-done((bf16[536,128]{1,0:T(8,128)(2,1)S(1)}, bf16[536,128]{1,0:T(8,128)(2,1)S(1)}, u32[]{:S(2)}, u32[]{:S(2)}) %collective-permute-start) | collective-permute-done | bytes 137248 | tf_op jit(solution)/shard_map/ppermute | solution.py:370
  19.4 3.1 %spectral.1 = (f32[25,8,128]{2,1,0:T(8,128)S(1)}, f32[8,3,32,128]{3,2,1,0:T(8,128)S(1)}, f32[32,128]{1,0:T(8,128)}, bf16[2,512,128]{2,1,0:T(8,128)(2,1)S(1)}) custom-call(s32[8,16]{1,0:T(8,128)S(1)} %pad.9.slot_ref, s32[1]{0:T(128)} %bitcast.4.core_ref, bf16[536,128]{1,0:T(8,128)(2,1)S(1)} %collective-permute-done.before_ref, ...), custom_call_target="tpu_custom_call" | custom-call | bytes 60000000 | tf_op jit(solution)/shard_map/spectral/pallas_call | solution.py:391
  22.5 1.7 %collective-permute-start.2 = (bf16[2,512,128]{2,1,0:T(8,128)(2,1)S(1)}, bf16[2,512,128]{2,1,0:T(8,128)(2,1)S(1)}, u32[]{:S(2)}, u32[]{:S(2)}) collective-permute-start(bf16[2,512,128]{2,1,0:T(8,128)(2,1)S(1)} %get-tuple-element.39), channel_id=1, source_target_pairs={{0,1},{1,0},{2,3},{3,2},{4,5},{5,4},{6,7},{7,6},{8,9},{9,8},{10,11... | collective-permute-start | bytes 786440 | tf_op jit(solution)/shard_map/ppermute | solution.py:374
  24.2 3.8 %all-to-all-start = ((f32[32,1,128]{2,1,0:T(1,128)}), f32[32,1,128]{2,1,0:T(1,128)S(1)}, u32[]{:S(2)}, u32[]{:S(2)}) async-start(f32[32,1,128]{2,1,0:T(1,128)} %bitcast.6), calls=%async_computation | async-start | bytes 32768 | tf_op jit(solution)/shard_map/all_to_all | solution.py:408
  28.0 0.9 %prepare.1 = (bf16[25,128,64]{2,1,0:T(8,128)(2,1)S(1)}, f32[24,128]{1,0:T(8,128)S(1)}) custom-call(s32[8,16]{1,0:T(8,128)S(1)} %pad.9.slot_ref, bf16[536,128]{1,0:T(8,128)(2,1)S(1)} %collective-permute-done.before_ref, bf16[536,128]{1,0:T(8,128)(2,1)S(1)} %fusion.2.own_ref, bf16[536,128]{1,0:T(8,128)(2,1)S(1)} %collective-permute-done.1.after_ref), custom_call_target="tpu_custom_call" | custom-call | tf_op jit(solution)/shard_map/prepare/pallas_call | solution.py:409
  28.9 0.0 collective-permute-done.2
  29.0 0.1 pad_maximum_fusion.refs_0_
  29.0 8.7 %all-to-all-done = f32[32,1,128]{2,1,0:T(1,128)S(1)} async-done(((f32[32,1,128]{2,1,0:T(1,128)}), f32[32,1,128]{2,1,0:T(1,128)S(1)}, u32[]{:S(2)}, u32[]{:S(2)}) %all-to-all-start) | async-done | bytes 16416 | tf_op jit(solution)/shard_map/all_to_all | solution.py:408
  37.7 0.5 collective-permute-start.6
  38.3 1.5 %collective-permute-start.5 = (bf16[2,2,512,128]{3,2,1,0:T(8,128)(2,1)S(1)}, bf16[2,2,512,128]{3,2,1,0:T(8,128)(2,1)S(1)}, u32[]{:S(2)}, u32[]{:S(2)}) collective-permute-start(bf16[2,2,512,128]{3,2,1,0:T(8,128)(2,1)S(1)} %pad_maximum_fusion.refs_0_), channel_id=1, source_target_pairs={{0,2},{1,3},{2,4},{3,5},{4,6},{5,7},{6,0},{7,1},{8,10},{9,11},{10,... | collective-permute-start | bytes 1572872 | tf_op jit(solution)/shard_map/ppermute | solution.py:374
  39.8 3.4 %first.1 = (bf16[8,128,2048]{2,1,0:T(8,128)(2,1)S(1)}, bf16[8,2048,64]{2,1,0:T(8,128)(2,1)S(1)}, f32[8,128,64]{2,1,0:T(8,128)S(1)}, bf16[4,128,128]{2,1,0:T(8,128)(2,1)S(1)}) custom-call(s32[8,16]{1,0:T(8,128)S(1)} %pad.9.slot_ref, f32[32,128]{1,0:T(8,128)S(1)} %bitcast.26, f32[25,8,128]{2,1,0:T(8,128)S(1)} %get-tuple-element.35.near_ref, ...), custom_call_target="tpu_custom_call" | custom-call | tf_op jit(solution)/shard_map/first/pallas_call | solution.py:427
  43.1 0.1 collective-permute-start.4
  43.2 0.5 collective-permute-start.3
  43.7 3.3 %collective-permute-done.4.after_ref = bf16[4,128,128]{2,1,0:T(8,128)(2,1)S(1)} collective-permute-done((bf16[4,128,128]{2,1,0:T(8,128)(2,1)S(1)}, bf16[4,128,128]{2,1,0:T(8,128)(2,1)S(1)}, u32[]{:S(2)}, u32[]{:S(2)}) %collective-permute-start.4) | collective-permute-done | bytes 131104 | tf_op jit(solution)/shard_map/ppermute | solution.py:370
  47.0 5.2 %collective-permute-done.3.before_ref = bf16[4,128,128]{2,1,0:T(8,128)(2,1)S(1)} collective-permute-done((bf16[4,128,128]{2,1,0:T(8,128)(2,1)S(1)}, bf16[4,128,128]{2,1,0:T(8,128)(2,1)S(1)}, u32[]{:S(2)}, u32[]{:S(2)}) %collective-permute-start.3) | collective-permute-done | bytes 131104 | tf_op jit(solution)/shard_map/ppermute | solution.py:370
  52.2 0.0 collective-permute-done.6.refs_4_
  52.2 0.5 collective-permute-done.5.refs_1_
  52.7 3.0 %collective-permute-start.8 = (bf16[2,512,128]{2,1,0:T(8,128)(2,1)S(1)}, bf16[2,512,128]{2,1,0:T(8,128)(2,1)}, u32[]{:S(2)}, u32[]{:S(2)}) collective-permute-start(bf16[2,512,128]{2,1,0:T(8,128)(2,1)S(1)} %slice_bitcast_fusion), channel_id=1, source_target_pairs={{0,6},{1,7},{2,0},{3,1},{4,2},{5,3},{6,4},{7,5},{8,14},{9,15},{10,... | collective-permute-start | bytes 786440 | tf_op jit(solution)/shard_map/ppermute | solution.py:374
  55.8 0.0 collective-permute-start.7
  55.8 6.4 %second.1 = f32[8,88,128]{2,1,0:T(8,128)} custom-call(s32[8,16]{1,0:T(8,128)S(1)} %pad.9.slot_ref, f32[25,8,128]{2,1,0:T(8,128)S(1)} %get-tuple-element.35.near_ref, f32[8,3,32,128]{3,2,1,0:T(8,128)S(1)} %get-tuple-element.36.row_ref, bf16[8,128,2048]{2,1,0:T(8,128)(2,1)S(1)} %get-tuple-element.46.scaled_ref, ...), custom_call_target="tpu_custom_call" | custom-call | tf_op jit(solution)/shard_map/second/pallas_call | solution.py:454
  62.2 0.0 collective-permute-done.8.refs_3_
  62.2 0.3 collective-permute-done.7.refs_2_
  62.5 6.2 %all-to-all-start.1 = ((f32[8,88,128]{2,1,0:T(8,128)}), f32[8,88,128]{2,1,0:T(8,128)S(1)}, u32[]{:S(2)}, u32[]{:S(2)}) async-start(f32[8,88,128]{2,1,0:T(8,128)} %second.1), calls=%async_computation.1 | async-start | bytes 720896 | tf_op jit(solution)/shard_map/all_to_all | solution.py:474
  68.7 0.0 collective-permute-start.9
  68.7 0.5 collective-permute-start.10
  69.2 0.0 collective-permute-start.13
  69.2 0.5 collective-permute-start.11
  69.7 0.0 collective-permute-start.12
  69.7 5.0 %all-to-all-done.1.received_ref = f32[8,88,128]{2,1,0:T(8,128)S(1)} async-done(((f32[8,88,128]{2,1,0:T(8,128)}), f32[8,88,128]{2,1,0:T(8,128)S(1)}, u32[]{:S(2)}, u32[]{:S(2)}) %all-to-all-start.1) | async-done | bytes 360480 | tf_op jit(solution)/shard_map/all_to_all | solution.py:474
  74.8 0.0 collective-permute-done.11.refs_7_
  74.8 0.5 collective-permute-start.14
  75.3 0.0 collective-permute-done.12.refs_8_
  75.3 0.1 collective-permute-start.15
  75.4 0.0 collective-permute-done.9.refs_5_
  75.4 0.0 collective-permute-done.10.refs_6_
  75.4 0.0 collective-permute-done.13.refs_9_
  75.4 3.2 %sample.1 = bf16[16,15,8,128]{3,2,1,0:T(8,128)(2,1)} custom-call(s32[8,16]{1,0:T(8,128)S(1)} %pad.9.slot_ref, s32[1]{0:T(128)} %bitcast.3.rank_ref, s32[1]{0:T(128)} %bitcast.4.core_ref, f32[8,88,128]{2,1,0:T(8,128)S(1)} %all-to-all-done.1.received_ref, bf16[2,2,512,128]{3,2,1,0:T(8,128)(2,1)S(1)} %pad_maximum_fusion.refs_0_, ...), custom_call_target="tpu_custom_call" | custom-call | tf_op jit(solution)/shard_map/sample/pallas_call | solution.py:479
  78.6 0.0 collective-permute-done.14
  78.6 3.9 %collective-permute-done.15 = f32[8,128]{1,0:T(8,128)S(1)} collective-permute-done((f32[8,128]{1,0:T(8,128)S(1)}, f32[8,128]{1,0:T(8,128)S(1)}, u32[]{:S(2)}, u32[]{:S(2)}) %collective-permute-start.15) | collective-permute-done | bytes 4128 | tf_op jit(solution)/shard_map/ppermute | solution.py:370
  82.5 0.1 slice_bitcast_fusion.4
  82.6 0.6 maximum_bitcast_fusion
  (6 shorter events, 0.1 us)
Async XLA Ops:
  1.6 12.3 %collective-permute-start.1 = (bf16[536,128]{1,0:T(8,128)(2,1)S(1)}, bf16[536,128]{1,0:T(8,128)(2,1)S(1)}, u32[]{:S(2)}, u32[]{:S(2)}) collective-permute-start(bf16[536,128]{1,0:T(8,128)(2,1)S(1)} %fusion.2.own_ref), channel_id=1, source_target_pairs={{8,0},{16,8},{24,16},{32,24},{40,32},{48,40},{56,48},{64,56},{72,6... | collective-permute-start | bytes 411656 | tf_op jit(solution)/shard_map/ppermute | solution.py:370
  9.8 9.6 %collective-permute-start = (bf16[536,128]{1,0:T(8,128)(2,1)S(1)}, bf16[536,128]{1,0:T(8,128)(2,1)S(1)}, u32[]{:S(2)}, u32[]{:S(2)}) collective-permute-start(bf16[536,128]{1,0:T(8,128)(2,1)S(1)} %fusion.2.own_ref), channel_id=1, source_target_pairs={{248,0},{0,8},{8,16},{16,24},{24,32},{32,40},{40,48},{48,56},{56,6... | collective-permute-start | bytes 411656 | tf_op jit(solution)/shard_map/ppermute | solution.py:370
  22.5 6.5 %collective-permute-start.2 = (bf16[2,512,128]{2,1,0:T(8,128)(2,1)S(1)}, bf16[2,512,128]{2,1,0:T(8,128)(2,1)S(1)}, u32[]{:S(2)}, u32[]{:S(2)}) collective-permute-start(bf16[2,512,128]{2,1,0:T(8,128)(2,1)S(1)} %get-tuple-element.39), channel_id=1, source_target_pairs={{0,1},{1,0},{2,3},{3,2},{4,5},{5,4},{6,7},{7,6},{8,9},{9,8},{10,11... | collective-permute-start | bytes 786440 | tf_op jit(solution)/shard_map/ppermute | solution.py:374
  24.2 13.6 %all-to-all-start = ((f32[32,1,128]{2,1,0:T(1,128)}), f32[32,1,128]{2,1,0:T(1,128)S(1)}, u32[]{:S(2)}, u32[]{:S(2)}) async-start(f32[32,1,128]{2,1,0:T(1,128)} %bitcast.6), calls=%async_computation | async-start | bytes 32768 | tf_op jit(solution)/shard_map/all_to_all | solution.py:408
  37.7 14.4 %collective-permute-start.6 = (bf16[2,2,512,128]{3,2,1,0:T(8,128)(2,1)S(1)}, bf16[2,2,512,128]{3,2,1,0:T(8,128)(2,1)S(1)}, u32[]{:S(2)}, u32[]{:S(2)}) collective-permute-start(bf16[2,2,512,128]{3,2,1,0:T(8,128)(2,1)S(1)} %pad_maximum_fusion.refs_0_), channel_id=1, source_target_pairs={{0,6},{1,7},{2,0},{3,1},{4,2},{5,3},{6,4},{7,5},{8,14},{9,15},{10,... | collective-permute-start | bytes 1572872 | tf_op jit(solution)/shard_map/ppermute | solution.py:374
  38.3 14.4 %collective-permute-start.5 = (bf16[2,2,512,128]{3,2,1,0:T(8,128)(2,1)S(1)}, bf16[2,2,512,128]{3,2,1,0:T(8,128)(2,1)S(1)}, u32[]{:S(2)}, u32[]{:S(2)}) collective-permute-start(bf16[2,2,512,128]{3,2,1,0:T(8,128)(2,1)S(1)} %pad_maximum_fusion.refs_0_), channel_id=1, source_target_pairs={{0,2},{1,3},{2,4},{3,5},{4,6},{5,7},{6,0},{7,1},{8,10},{9,11},{10,... | collective-permute-start | bytes 1572872 | tf_op jit(solution)/shard_map/ppermute | solution.py:374
  43.1 3.9 %collective-permute-start.4 = (bf16[4,128,128]{2,1,0:T(8,128)(2,1)S(1)}, bf16[4,128,128]{2,1,0:T(8,128)(2,1)S(1)}, u32[]{:S(2)}, u32[]{:S(2)}) collective-permute-start(bf16[4,128,128]{2,1,0:T(8,128)(2,1)S(1)} %get-tuple-element.49.own_ref), channel_id=1, source_target_pairs={{8,0},{16,8},{24,16},{32,24},{40,32},{48,40},{56,48},{64,56},{72,6... | collective-permute-start | bytes 393224 | tf_op jit(solution)/shard_map/ppermute | solution.py:370
  43.2 8.9 %collective-permute-start.3 = (bf16[4,128,128]{2,1,0:T(8,128)(2,1)S(1)}, bf16[4,128,128]{2,1,0:T(8,128)(2,1)S(1)}, u32[]{:S(2)}, u32[]{:S(2)}) collective-permute-start(bf16[4,128,128]{2,1,0:T(8,128)(2,1)S(1)} %get-tuple-element.49.own_ref), channel_id=1, source_target_pairs={{248,0},{0,8},{8,16},{16,24},{24,32},{32,40},{40,48},{48,56},{56,6... | collective-permute-start | bytes 393224 | tf_op jit(solution)/shard_map/ppermute | solution.py:370
  52.7 9.4 %collective-permute-start.8 = (bf16[2,512,128]{2,1,0:T(8,128)(2,1)S(1)}, bf16[2,512,128]{2,1,0:T(8,128)(2,1)}, u32[]{:S(2)}, u32[]{:S(2)}) collective-permute-start(bf16[2,512,128]{2,1,0:T(8,128)(2,1)S(1)} %slice_bitcast_fusion), channel_id=1, source_target_pairs={{0,6},{1,7},{2,0},{3,1},{4,2},{5,3},{6,4},{7,5},{8,14},{9,15},{10,... | collective-permute-start | bytes 786440 | tf_op jit(solution)/shard_map/ppermute | solution.py:374
  55.8 6.7 %collective-permute-start.7 = (bf16[2,512,128]{2,1,0:T(8,128)(2,1)S(1)}, bf16[2,512,128]{2,1,0:T(8,128)(2,1)}, u32[]{:S(2)}, u32[]{:S(2)}) collective-permute-start(bf16[2,512,128]{2,1,0:T(8,128)(2,1)S(1)} %slice_bitcast_fusion.1), channel_id=1, source_target_pairs={{0,2},{1,3},{2,4},{3,5},{4,6},{5,7},{6,0},{7,1},{8,10},{9,11},{10,... | collective-permute-start | bytes 786440 | tf_op jit(solution)/shard_map/ppermute | solution.py:374
  62.5 12.3 %all-to-all-start.1 = ((f32[8,88,128]{2,1,0:T(8,128)}), f32[8,88,128]{2,1,0:T(8,128)S(1)}, u32[]{:S(2)}, u32[]{:S(2)}) async-start(f32[8,88,128]{2,1,0:T(8,128)} %second.1), calls=%async_computation.1 | async-start | bytes 720896 | tf_op jit(solution)/shard_map/all_to_all | solution.py:474
  68.7 6.7 %collective-permute-start.9 = (bf16[2,2,512,128]{3,2,1,0:T(8,128)(2,1)S(1)}, bf16[2,2,512,128]{3,2,1,0:T(8,128)(2,1)S(1)}, u32[]{:S(2)}, u32[]{:S(2)}) collective-permute-start(bf16[2,2,512,128]{3,2,1,0:T(8,128)(2,1)S(1)} %pad_maximum_fusion.refs_0_), channel_id=1, source_target_pairs={{0,8},{8,0},{16,24},{24,16},{32,40},{40,32},{48,56},{56,48},{64,72... | collective-permute-start | bytes 1572872 | tf_op jit(solution)/shard_map/ppermute | solution.py:472
  68.7 6.7 %collective-permute-start.10 = (bf16[2,2,512,128]{3,2,1,0:T(8,128)(2,1)S(1)}, bf16[2,2,512,128]{3,2,1,0:T(8,128)(2,1)}, u32[]{:S(2)}, u32[]{:S(2)}) collective-permute-start(bf16[2,2,512,128]{3,2,1,0:T(8,128)(2,1)S(1)} %collective-permute-done.5.refs_1_), channel_id=1, source_target_pairs={{0,8},{8,0},{16,24},{24,16},{32,40},{40,32},{48,56},{56,48},{64,72... | collective-permute-start | bytes 1572872 | tf_op jit(solution)/shard_map/ppermute | solution.py:472
  69.2 6.2 %collective-permute-start.13 = (bf16[2,2,512,128]{3,2,1,0:T(8,128)(2,1)S(1)}, bf16[2,2,512,128]{3,2,1,0:T(8,128)(2,1)}, u32[]{:S(2)}, u32[]{:S(2)}) collective-permute-start(bf16[2,2,512,128]{3,2,1,0:T(8,128)(2,1)S(1)} %collective-permute-done.6.refs_4_), channel_id=1, source_target_pairs={{0,8},{8,0},{16,24},{24,16},{32,40},{40,32},{48,56},{56,48},{64,72... | collective-permute-start | bytes 1572872 | tf_op jit(solution)/shard_map/ppermute | solution.py:472
  69.2 5.6 %collective-permute-start.11 = (bf16[2,512,128]{2,1,0:T(8,128)(2,1)}, bf16[2,512,128]{2,1,0:T(8,128)(2,1)S(1)}, u32[]{:S(2)}, u32[]{:S(2)}) collective-permute-start(bf16[2,512,128]{2,1,0:T(8,128)(2,1)} %collective-permute-done.7.refs_2_), channel_id=1, source_target_pairs={{0,8},{8,0},{16,24},{24,16},{32,40},{40,32},{48,56},{56,48},{64,72... | collective-permute-start | bytes 786440 | tf_op jit(solution)/shard_map/ppermute | solution.py:472
  69.7 5.5 %collective-permute-start.12 = (bf16[2,512,128]{2,1,0:T(8,128)(2,1)}, bf16[2,512,128]{2,1,0:T(8,128)(2,1)S(1)}, u32[]{:S(2)}, u32[]{:S(2)}) collective-permute-start(bf16[2,512,128]{2,1,0:T(8,128)(2,1)} %collective-permute-done.8.refs_3_), channel_id=1, source_target_pairs={{0,8},{8,0},{16,24},{24,16},{32,40},{40,32},{48,56},{56,48},{64,72... | collective-permute-start | bytes 786440 | tf_op jit(solution)/shard_map/ppermute | solution.py:472
  74.8 3.8 %collective-permute-start.14 = (f32[8,128]{1,0:T(8,128)S(1)}, f32[8,128]{1,0:T(8,128)S(1)}, u32[]{:S(2)}, u32[]{:S(2)}) collective-permute-start(f32[8,128]{1,0:T(8,128)S(1)} %get-tuple-element.62), channel_id=1, source_target_pairs={{8,0},{16,8},{24,16},{32,24},{40,32},{48,40},{56,48},{64,56},{72,6... | collective-permute-start | bytes 12296 | tf_op jit(solution)/shard_map/ppermute | solution.py:370
  75.3 7.3 %collective-permute-start.15 = (f32[8,128]{1,0:T(8,128)S(1)}, f32[8,128]{1,0:T(8,128)S(1)}, u32[]{:S(2)}, u32[]{:S(2)}) collective-permute-start(f32[8,128]{1,0:T(8,128)S(1)} %get-tuple-element.63), channel_id=1, source_target_pairs={{248,0},{0,8},{8,16},{16,24},{24,32},{32,40},{40,48},{48,56},{56,6... | collective-permute-start | bytes 12296 | tf_op jit(solution)/shard_map/ppermute | solution.py:370
